TPU v7x, 32 devices: a whole 2x2x4 slice. The times are simulated.
32 devices in a mesh: dp: 4 (over z), expert: 8 (over y, x, core).
Axes of the slice: x: 2, y: 2, z: 4, core: 2. Of those that a mesh axis runs over, the one named last changes fastest.
Arguments:
- tokens: bfloat16 [4, 1024, 1024], P('dp', 'expert'), may hold values from -6 to 6
- attn_gain: float32 [1024], replicated, may hold values from 0.5 to 1.5
- w_query: bfloat16 [1024, 1024], replicated, may hold values from -0.5 to 0.5
- w_key: bfloat16 [1024, 512], replicated, may hold values from -0.5 to 0.5
- w_value: bfloat16 [1024, 512], replicated, may hold values from -0.1875 to 0.1875
- w_output: bfloat16 [1024, 1024], replicated, may hold values from -6 to 6
- moe_gain: float32 [1024], replicated, may hold values from 0.5 to 1.5
- w_router: bfloat16 [1024, 32], replicated, may hold values from -0.09375 to 0.09375
- w_gate: bfloat16 [32, 1024, 512], P('expert'), may hold values from -0.1875 to 0.1875
- w_up: bfloat16 [32, 1024, 512], P('expert'), may hold values from -0.1875 to 0.1875
- w_down: bfloat16 [32, 512, 1024], P('expert'), may hold values from -6 to 6
- routes: int32 [4, 1024, 8], P('dp', 'expert'), may hold values from 0 to 31, all different within a row; in each aligned block of 128 rows (0 to 127, 128 to 255, ..., all dimensions but the last counted through in order) at most 48 rows name the same one
- segment_ids: int32 [4, 1024], P('dp', 'expert'), may hold values from 0 to 7, never falling along the last dimension, each value on 1 to 512 neighbouring positions
- out_grad: bfloat16 [4, 1024, 1024], P('dp', 'expert'), may hold values from -6 to 6
Outputs:
- mixed: bfloat16 [4, 1024, 1024], P('dp', 'expert')
- grad_tokens: float32 [4, 1024, 1024], P('dp', 'expert')
- grad_attn_gain: float32 [1024], replicated
- grad_query: float32 [1024, 1024], replicated
- grad_key: float32 [1024, 512], replicated
- grad_value: float32 [1024, 512], replicated
- grad_output: float32 [1024, 1024], replicated
- grad_moe_gain: float32 [1024], replicated
- grad_router: float32 [1024, 32], replicated
- grad_gate: float32 [32, 1024, 512], P('expert', 'dp')
- grad_up: float32 [32, 1024, 512], P('expert', 'dp')
- grad_down: float32 [32, 512, 1024], P('expert', 'dp')
Inputs may be any that keep to these rules, and one draw needn't show every extreme that they name: `routes`: each token names 8 different experts. In each aligned block of 128 positions of a packed row no expert is named by more than 48 tokens, and in some block one expert is named by exactly 48. `segment_ids`: along a packed row the document numbers never fall; a document covers one position up to half of 1024, and some document covers exactly half of 1024.
All inputs are finite; a program needn't handle non-finite values.
Results may differ from a plain program's by a relative error of at most 0.018.
Values may be sent and summed in bfloat16 or wider, within the bound.
No kernel may reach another device: no remote copies, remote signals or barrier semaphores. Data moves between devices by JAX's collectives and lax.ppermute only.
A program may use at most 192 MiB of HBM per device.

v0:
```python
import jax
import jax.numpy as jnp
from jax import lax
from jax.experimental import pallas as pl
from jax.experimental.pallas import tpu as pltpu
from jax.sharding import PartitionSpec as P


HEADS = 16
KV_HEADS = 8
HEAD_DIM = 64
EXPERTS = 32
TOP = 8
MOST = 48


ATTN_SCALE = 0.015625
RESIDUAL_SCALE = 0.22
NORM_EPS = 1e-06
ROPE_BASE = 10000.0
NEG_FILL = -1e30
TAIL = 16
SEGMENTS = 8


def rms_forward(values, gain_vec):
    inverse = lax.rsqrt(jnp.mean(values * values, axis=-1, keepdims=True) + NORM_EPS)
    unit_rows = values * inverse
    return (unit_rows * gain_vec, unit_rows, inverse)


def rms_backward(grad_rows, unit_rows, inverse, gain_vec):
    scaled = grad_rows * gain_vec
    grad_gain = jnp.sum(grad_rows * unit_rows, axis=0)
    grad_in = inverse * (scaled - unit_rows * jnp.mean(scaled * unit_rows, axis=-1, keepdims=True))
    return (grad_in, grad_gain)


def rope_tables(positions):
    half = HEAD_DIM // 2
    freqs = ROPE_BASE ** (-(jnp.arange(half, dtype=jnp.float32) * 2.0) / HEAD_DIM)
    angles = positions.astype(jnp.float32)[..., None] * freqs
    cosine = jnp.concatenate([jnp.cos(angles), jnp.cos(angles)], axis=-1)
    sine = jnp.concatenate([jnp.sin(angles), jnp.sin(angles)], axis=-1)
    return (cosine, sine)


def rotate(vectors, cosine, sine):
    half = vectors.shape[-1] // 2
    turned = jnp.concatenate([-vectors[..., half:], vectors[..., :half]], axis=-1)
    return vectors * cosine + turned * sine


def unrotate(grads, cosine, sine):
    half = grads.shape[-1] // 2
    scaled = grads * sine
    turned = jnp.concatenate([scaled[..., half:], -scaled[..., :half]], axis=-1)
    return grads * cosine + turned


def scaled_scores(query_part, key_part, query_seg, key_seg, query_index, key_index):
    raw = (
        jnp.einsum("qrgjd,krgd->rgjqk", query_part, key_part, preferred_element_type=jnp.float32)
        * ATTN_SCALE
    )
    same = jnp.transpose(query_seg)[:, :, None] == jnp.transpose(key_seg)[:, None, :]
    before = key_index[None, :] <= query_index[:, None]
    return (raw, (same & before[None])[:, None, None])


def probs_and_ds(
    query_part,
    key_part,
    value_part,
    dout_part,
    lse_part,
    delta_part,
    query_seg,
    key_seg,
    query_index,
    key_index,
):
    scores, allowed = scaled_scores(
        query_part, key_part, query_seg, key_seg, query_index, key_index
    )
    lse_rows = jnp.transpose(lse_part, (1, 2, 3, 0))[..., None]
    delta_rows = jnp.transpose(delta_part, (1, 2, 3, 0))[..., None]
    probs = jnp.where(allowed, jnp.exp(scores - lse_rows), 0.0)
    dprobs = jnp.einsum(
        "qrgjd,krgd->rgjqk", dout_part, value_part, preferred_element_type=jnp.float32
    )
    dscore = (probs * (dprobs - delta_rows)).astype(jnp.bfloat16)
    return (probs.astype(jnp.bfloat16), dscore)


def per_device_general(
    tokens,
    attn_gain,
    w_query,
    w_key,
    w_value,
    w_output,
    moe_gain,
    w_router,
    w_gate,
    w_up,
    w_down,
    routes,
    segment_ids,
    out_grad,
):
    row_count, group_len, width = tokens.shape
    devices = lax.axis_size("expert")
    my_index = lax.axis_index("expert")
    length = group_len * devices
    repeats = HEADS // KV_HEADS
    tok_count = group_len * row_count
    slot_rows = row_count * MOST
    seg_local = jnp.transpose(segment_ids)
    seg_all = lax.all_gather(seg_local, "expert", axis=0, tiled=True)
    query_index = my_index * group_len + jnp.arange(group_len, dtype=jnp.int32)
    earlier = jnp.sum((seg_all[None, :, :] < seg_local[:, None, :]).astype(jnp.int32), axis=1)
    cosine, sine = rope_tables(query_index[:, None] - earlier)
    cos_heads = cosine[:, :, None, :]
    sin_heads = sine[:, :, None, :]
    residual = jnp.swapaxes(tokens, 0, 1).astype(jnp.float32).reshape(tok_count, width)
    normed, unit_attn, inv_attn = rms_forward(residual, attn_gain)
    normed_rows = normed.astype(jnp.bfloat16)
    query_lin = jnp.dot(normed_rows, w_query, preferred_element_type=jnp.float32).reshape(
        group_len, row_count, HEADS, HEAD_DIM
    )
    queries = (
        rotate(query_lin, cos_heads, sin_heads)
        .astype(jnp.bfloat16)
        .reshape(group_len, row_count, KV_HEADS, repeats, HEAD_DIM)
    )
    key_lin = jnp.dot(normed_rows, w_key, preferred_element_type=jnp.float32).reshape(
        group_len, row_count, KV_HEADS, HEAD_DIM
    )
    keys = rotate(key_lin, cos_heads, sin_heads).astype(jnp.bfloat16)
    values = (
        jnp.dot(normed_rows, w_value, preferred_element_type=jnp.float32)
        .astype(jnp.bfloat16)
        .reshape(group_len, row_count, KV_HEADS, HEAD_DIM)
    )
    keys_all, values_all = (
        lax.all_gather(keys, "expert", axis=0, tiled=True),
        lax.all_gather(values, "expert", axis=0, tiled=True),
    )
    key_block = min(1024, length)
    block_count = length // key_block
    key_blocks = keys_all.reshape(block_count, key_block, row_count, KV_HEADS, HEAD_DIM)
    value_blocks = values_all.reshape(block_count, key_block, row_count, KV_HEADS, HEAD_DIM)
    seg_blocks = seg_all.reshape(block_count, key_block, row_count)
    index_blocks = jnp.arange(length, dtype=jnp.int32).reshape(block_count, key_block)
    key_inputs = (key_blocks, value_blocks, seg_blocks, index_blocks)

    def max_step(carried, current):
        running, totals = carried
        key_part, _, seg_part, index_part = current
        scores, allowed = scaled_scores(
            queries, key_part, seg_local, seg_part, query_index, index_part
        )
        newmax = jnp.maximum(running, jnp.max(jnp.where(allowed, scores, NEG_FILL), axis=-1))
        totals = totals * jnp.exp(running - newmax) + jnp.sum(
            jnp.where(allowed, jnp.exp(scores - newmax[..., None]), 0.0), axis=-1
        )
        return ((newmax, totals), None)

    stat_shape = (row_count, KV_HEADS, repeats, group_len)
    (running, totals), unused = lax.scan(
        max_step,
        (jnp.full(stat_shape, NEG_FILL, jnp.float32), jnp.zeros(stat_shape, jnp.float32)),
        key_inputs,
    )
    logsum = running + jnp.log(totals)
    lse_local = jnp.transpose(logsum, (3, 0, 1, 2))

    def out_step(accum, current):
        key_part, value_part, seg_part, index_part = current
        scores, allowed = scaled_scores(
            queries, key_part, seg_local, seg_part, query_index, index_part
        )
        probs = jnp.where(allowed, jnp.exp(scores - logsum[..., None]), 0.0).astype(jnp.bfloat16)
        return (
            accum
            + jnp.einsum(
                "rgjqk,krgd->qrgjd", probs, value_part, preferred_element_type=jnp.float32
            ),
            None,
        )

    head_shape = (group_len, row_count, KV_HEADS, repeats, HEAD_DIM)
    attended, unused = lax.scan(out_step, jnp.zeros(head_shape, jnp.float32), key_inputs)
    attn_rows = attended.reshape(tok_count, HEADS * HEAD_DIM).astype(jnp.bfloat16)
    branch = jnp.dot(attn_rows, w_output, preferred_element_type=jnp.float32)
    middle = residual + RESIDUAL_SCALE * branch
    normed2, unit_moe, inv_moe = rms_forward(middle, moe_gain)
    moe_rows = normed2.astype(jnp.bfloat16)
    logits = jnp.dot(moe_rows, w_router, preferred_element_type=jnp.float32)
    route_rows = jnp.transpose(routes, (1, 0, 2)).reshape(tok_count, TOP)
    onehot = route_rows[:, :, None] == jnp.arange(EXPERTS, dtype=jnp.int32)[None, None, :]
    picked = jnp.sum(jnp.where(onehot, logits[:, None, :], 0.0), axis=-1)
    gates = jax.nn.softmax(picked, axis=-1)
    by_row = jnp.transpose(
        onehot.reshape(group_len, row_count, TOP, EXPERTS), (1, 0, 2, 3)
    ).reshape(row_count, group_len * TOP, EXPERTS)
    counted = jnp.cumsum(by_row.astype(jnp.int32), axis=1)
    rank = jnp.sum(jnp.where(by_row, counted - 1, 0), axis=-1).reshape(row_count, group_len, TOP)
    rank = jnp.transpose(rank, (1, 0, 2)).reshape(tok_count, TOP)
    row_of = jnp.arange(tok_count, dtype=jnp.int32) % row_count
    target = (route_rows * slot_rows + row_of[:, None] * MOST + rank).reshape(tok_count * TOP)

    def to_slots(route_values):
        placed = (
            jnp.zeros((EXPERTS * slot_rows, width), jnp.bfloat16)
            .at[target]
            .set(route_values.reshape(tok_count * TOP, width))
        )
        return placed.reshape(EXPERTS, slot_rows, width)

    def from_slots(slot_values):
        return (
            slot_values.reshape(EXPERTS * slot_rows, width)[target]
            .reshape(tok_count, TOP, width)
            .astype(jnp.float32)
        )

    sent = to_slots(jnp.broadcast_to(moe_rows[:, None, :], (tok_count, TOP, width)))
    arrived = lax.all_to_all(sent, "expert", split_axis=0, concat_axis=1, tiled=True)
    gate_pre = jnp.einsum("etd,edf->etf", arrived, w_gate, preferred_element_type=jnp.float32)
    up_pre = jnp.einsum("etd,edf->etf", arrived, w_up, preferred_element_type=jnp.float32)
    sigma = jax.nn.sigmoid(gate_pre)
    activated = gate_pre * sigma
    hidden = (activated * up_pre).astype(jnp.bfloat16)
    expert_out = jnp.einsum(
        "etf,efd->etd", hidden, w_down, preferred_element_type=jnp.float32
    ).astype(jnp.bfloat16)
    returned = lax.all_to_all(expert_out, "expert", split_axis=1, concat_axis=0, tiled=True)
    route_out = from_slots(returned)
    moe = jnp.sum(gates[:, :, None] * route_out, axis=1)
    mixed_rows = middle + RESIDUAL_SCALE * moe
    mixed = jnp.swapaxes(mixed_rows.reshape(group_len, row_count, width), 0, 1).astype(jnp.bfloat16)
    upstream = jnp.swapaxes(out_grad, 0, 1).astype(jnp.float32).reshape(tok_count, width)
    dmoe = RESIDUAL_SCALE * upstream
    dgates = jnp.sum(route_out * dmoe[:, None, :], axis=-1)
    dsent = to_slots((gates[:, :, None] * dmoe[:, None, :]).astype(jnp.bfloat16))
    darrived = lax.all_to_all(dsent, "expert", split_axis=0, concat_axis=1, tiled=True)
    dhidden = jnp.einsum("etd,efd->etf", darrived, w_down, preferred_element_type=jnp.float32)
    down_part = jnp.einsum("etf,etd->efd", hidden, darrived, preferred_element_type=jnp.float32)
    dgate_pre = (dhidden * up_pre * sigma * (1.0 + gate_pre * (1.0 - sigma))).astype(jnp.bfloat16)
    dup_pre = (dhidden * activated).astype(jnp.bfloat16)
    gate_part = jnp.einsum("etd,etf->edf", arrived, dgate_pre, preferred_element_type=jnp.float32)
    up_part = jnp.einsum("etd,etf->edf", arrived, dup_pre, preferred_element_type=jnp.float32)
    dinputs = (
        jnp.einsum("etf,edf->etd", dgate_pre, w_gate, preferred_element_type=jnp.float32)
        + jnp.einsum("etf,edf->etd", dup_pre, w_up, preferred_element_type=jnp.float32)
    ).astype(jnp.bfloat16)
    grad_gate, grad_up, grad_down = (
        lax.psum_scatter(
            gate_part.astype(jnp.bfloat16), "dp", scatter_dimension=1, tiled=True
        ).astype(jnp.float32),
        lax.psum_scatter(
            up_part.astype(jnp.bfloat16), "dp", scatter_dimension=1, tiled=True
        ).astype(jnp.float32),
        lax.psum_scatter(
            down_part.astype(jnp.bfloat16), "dp", scatter_dimension=1, tiled=True
        ).astype(jnp.float32),
    )
    dreturned = lax.all_to_all(dinputs, "expert", split_axis=1, concat_axis=0, tiled=True)
    droutes = jnp.sum(from_slots(dreturned), axis=1)
    dpicked = gates * (dgates - jnp.sum(gates * dgates, axis=-1, keepdims=True))
    dlogits = jnp.sum(jnp.where(onehot, dpicked[:, :, None], 0.0), axis=1).astype(jnp.bfloat16)
    router_part = jnp.einsum("nd,ne->de", moe_rows, dlogits, preferred_element_type=jnp.float32)
    dnormed2 = droutes + jnp.einsum(
        "ne,de->nd", dlogits, w_router, preferred_element_type=jnp.float32
    )
    dmiddle_norm, moe_gain_part = rms_backward(dnormed2, unit_moe, inv_moe, moe_gain)
    dmiddle = upstream + dmiddle_norm
    dbranch = (RESIDUAL_SCALE * dmiddle).astype(jnp.bfloat16)
    output_part = jnp.einsum("nh,nd->hd", attn_rows, dbranch, preferred_element_type=jnp.float32)
    dattn = (
        jnp.einsum("nd,hd->nh", dbranch, w_output, preferred_element_type=jnp.float32)
        .astype(jnp.bfloat16)
        .reshape(head_shape)
    )
    delta = jnp.sum(dattn.astype(jnp.float32) * attended, axis=-1)

    def both_step(dq_sum, current):
        key_part, value_part, seg_part, index_part = current
        probs_b, dscore = probs_and_ds(
            queries,
            key_part,
            value_part,
            dattn,
            lse_local,
            delta,
            seg_local,
            seg_part,
            query_index,
            index_part,
        )
        dq_part = (
            jnp.einsum("rgjqk,krgd->qrgjd", dscore, key_part, preferred_element_type=jnp.float32)
            * ATTN_SCALE
        )
        dk_part = (
            jnp.einsum("rgjqk,qrgjd->krgd", dscore, queries, preferred_element_type=jnp.float32)
            * ATTN_SCALE
        )
        dv_part = jnp.einsum(
            "rgjqk,qrgjd->krgd", probs_b, dattn, preferred_element_type=jnp.float32
        )
        return (dq_sum + dq_part, (dk_part, dv_part))

    dq_sum, (dk_stack, dv_stack) = lax.scan(
        both_step, jnp.zeros(head_shape, jnp.float32), key_inputs
    )
    full_shape = (length, row_count, KV_HEADS, HEAD_DIM)
    dkeys, dvalues = (
        lax.psum_scatter(
            dk_stack.reshape(full_shape).astype(jnp.bfloat16),
            "expert",
            scatter_dimension=0,
            tiled=True,
        ).astype(jnp.float32),
        lax.psum_scatter(
            dv_stack.reshape(full_shape).astype(jnp.bfloat16),
            "expert",
            scatter_dimension=0,
            tiled=True,
        ).astype(jnp.float32),
    )
    dquery_lin = (
        unrotate(dq_sum.reshape(group_len, row_count, HEADS, HEAD_DIM), cos_heads, sin_heads)
        .astype(jnp.bfloat16)
        .reshape(tok_count, HEADS * HEAD_DIM)
    )
    dkey_lin = (
        unrotate(dkeys, cos_heads, sin_heads)
        .astype(jnp.bfloat16)
        .reshape(tok_count, KV_HEADS * HEAD_DIM)
    )
    dvalue_rows = dvalues.astype(jnp.bfloat16).reshape(tok_count, KV_HEADS * HEAD_DIM)
    query_part_grad = jnp.einsum(
        "nd,nh->dh", normed_rows, dquery_lin, preferred_element_type=jnp.float32
    )
    key_part_grad = jnp.einsum(
        "nd,nh->dh", normed_rows, dkey_lin, preferred_element_type=jnp.float32
    )
    value_part_grad = jnp.einsum(
        "nd,nh->dh", normed_rows, dvalue_rows, preferred_element_type=jnp.float32
    )
    dnormed = (
        jnp.einsum("nh,dh->nd", dquery_lin, w_query, preferred_element_type=jnp.float32)
        + jnp.einsum("nh,dh->nd", dkey_lin, w_key, preferred_element_type=jnp.float32)
        + jnp.einsum("nh,dh->nd", dvalue_rows, w_value, preferred_element_type=jnp.float32)
    )
    dresid_norm, attn_gain_part = rms_backward(dnormed, unit_attn, inv_attn, attn_gain)
    grad_tokens = jnp.swapaxes((dmiddle + dresid_norm).reshape(group_len, row_count, width), 0, 1)
    query_sum, key_sum, value_sum, output_sum, router_sum, attn_gain_sum, moe_gain_sum = lax.psum(
        (
            query_part_grad,
            key_part_grad,
            value_part_grad,
            output_part,
            router_part,
            attn_gain_part,
            moe_gain_part,
        ),
        ("dp", "expert"),
    )
    return (
        mixed,
        grad_tokens,
        attn_gain_sum,
        query_sum,
        key_sum,
        value_sum,
        output_sum,
        moe_gain_sum,
        router_sum,
        grad_gate,
        grad_up,
        grad_down,
    )


def expert_gather(x_rows, g_rows, mask_rows, slot_rows, router_rows, first, x_scr, g_scr, gate_scr, table_scr, groups):
    held = x_scr.shape[0]
    for g in range(groups):
        rows = x_rows(g)
        logits = lax.dot_general(
            router_rows, rows, (((1,), (1,)), ((), ())), preferred_element_type=jnp.float32
        )
        shown = mask_rows(g) > 0
        raised = jnp.where(
            shown,
            jnp.exp(logits - jnp.max(jnp.where(shown, logits, NEG_FILL), axis=0, keepdims=True)),
            0.0,
        )
        gates = raised / jnp.sum(raised, axis=0, keepdims=True)
        slots = slot_rows(g)
        expert = lax.broadcasted_iota(jnp.int32, gates.shape, 0)
        place = lax.broadcasted_iota(jnp.int32, (MOST, rows.shape[0]), 0)
        tables = []
        for e in range(held):
            gate_row = jnp.sum(jnp.where(expert == first + e, gates, 0.0), axis=0, keepdims=True)
            chosen = place == slots[e : e + 1, :]
            gate_scr[e, g * MOST : (g + 1) * MOST, :] = jnp.sum(
                jnp.where(chosen, gate_row, 0.0), axis=1, keepdims=True
            )
            tables.append(jnp.where(chosen, 1.0, 0.0))
        table = jnp.concatenate(tables, axis=0).astype(jnp.bfloat16)
        if table_scr is not None:
            table_scr[g] = table
        for scr, part in ((x_scr, rows), (g_scr, g_rows(g))):
            picked = jnp.dot(table, part, preferred_element_type=jnp.float32).astype(jnp.bfloat16)
            for e in range(held):
                scr[e, g * MOST : (g + 1) * MOST, :] = picked[e * MOST : (e + 1) * MOST, :]


def nt(left, right):
    return lax.dot_general(
        left, right, (((1,), (1,)), ((), ())), preferred_element_type=jnp.float32
    )


def tn(left, right):
    return lax.dot_general(
        left, right, (((0,), (0,)), ((), ())), preferred_element_type=jnp.float32
    )


def expert_body(x_slots, g_slots, gate_col, gate_w, up_w, down_w):
    gate_pre = jnp.dot(x_slots, gate_w, preferred_element_type=jnp.float32)
    up_pre = jnp.dot(x_slots, up_w, preferred_element_type=jnp.float32)
    sigma = jax.nn.sigmoid(gate_pre)
    activated = gate_pre * sigma
    hidden = (activated * up_pre).astype(jnp.bfloat16)
    dexpert = (gate_col * (RESIDUAL_SCALE * g_slots.astype(jnp.float32))).astype(jnp.bfloat16)
    dhidden = nt(dexpert, down_w)
    dgate_pre = (dhidden * up_pre * sigma * (1.0 + gate_pre * (1.0 - sigma))).astype(jnp.bfloat16)
    dup_pre = (dhidden * activated).astype(jnp.bfloat16)
    return hidden, dexpert, dgate_pre, dup_pre


def near_experts(me, x_near, x_twin, g_near, g_twin, mask_row, slot_row, router_t, w_gate, w_up, w_down):
    chips, group_len, width = x_near.shape
    held, _, inner = w_gate.shape
    groups = 2 * chips
    extra = 16
    lanes = 128

    def kernel(me_ref, xn, xt, gn, gt, mr, sr, rt, wg, wu, wd, near_out, twin_out, y_near, y_twin,
               x_scr, g_scr, gate_scr, table_scr, y_scr, d_scr, dg_scr):
        e = pl.program_id(0)
        my = me_ref[0]

        @pl.when(e == 0)
        def _():
            expert_gather(
                lambda g: (xn if g < chips else xt)[g % chips],
                lambda g: (gn if g < chips else gt)[g % chips],
                lambda g: mr[g],
                lambda g: sr[g],
                rt[...],
                my * held,
                x_scr, g_scr, gate_scr, table_scr, groups,
            )

        g_slots = g_scr[e]
        hidden, _, dgate_pre, dup_pre = expert_body(
            x_scr[e], g_slots, gate_scr[e], wg[0], wu[0], wd[0]
        )
        out = jnp.dot(hidden, wd[0], preferred_element_type=jnp.float32).astype(jnp.bfloat16)
        out_wide = out.astype(jnp.float32)
        dgate = jnp.sum(
            RESIDUAL_SCALE * g_slots.astype(jnp.float32) * out_wide, axis=1, keepdims=True
        )
        weighted = (gate_scr[e] * out_wide).astype(jnp.bfloat16)
        dinputs = (nt(dgate_pre, wg[0]) + nt(dup_pre, wu[0])).astype(jnp.bfloat16)
        spot = pl.ds(pl.multiple_of(e * MOST, 16), MOST)
        for g in range(groups):
            part = slice(g * MOST, (g + 1) * MOST)
            y_scr[g, spot, :] = weighted[part]
            d_scr[g, spot, :] = dinputs[part]
            taken = table_scr[g, spot, :].astype(jnp.float32)
            dg_scr[g, e] = jnp.sum(taken * dgate[part], axis=0, keepdims=True)

        @pl.when(e == held - 1)
        def _():
            block = lax.broadcasted_iota(jnp.int32, (held, width), 1) // lanes
            for g in range(groups):
                d_out, y_out = (near_out, y_near) if g < chips else (twin_out, y_twin)
                table = table_scr[g]
                y_out[g % chips] = tn(table, y_scr[g]).astype(jnp.bfloat16)
                d_out[g % chips, :group_len, :] = tn(table, d_scr[g]).astype(jnp.bfloat16)
                rows = jnp.concatenate([dg_scr[g, i] for i in range(held)], axis=0)
                spread = jnp.where(block == my, jnp.concatenate([rows] * groups, axis=1), 0.0)
                high = spread.astype(jnp.bfloat16).astype(jnp.float32)
                tail = jnp.concatenate(
                    [high, spread - high, jnp.zeros((extra - 2 * held, width), jnp.float32)], axis=0
                )
                d_out[g % chips, group_len:, :] = tail.astype(jnp.bfloat16)

    whole = lambda *shape: pl.BlockSpec(shape, lambda e, m: (0,) * len(shape))
    weight = lambda *shape: pl.BlockSpec((1,) + shape, lambda e, m: (e, 0, 0))
    back = jax.ShapeDtypeStruct((chips, group_len + extra, width), jnp.bfloat16)
    forth = jax.ShapeDtypeStruct((chips, group_len, width), jnp.bfloat16)
    slots = groups * MOST
    return pl.pallas_call(
        kernel,
        grid_spec=pltpu.PrefetchScalarGridSpec(
            num_scalar_prefetch=1,
            grid=(held,),
            in_specs=[
                whole(chips, group_len, width),
                whole(chips, group_len, width),
                whole(chips, group_len, width),
                whole(chips, group_len, width),
                whole(groups, EXPERTS, group_len),
                whole(groups, held, group_len),
                whole(EXPERTS, width),
                weight(width, inner),
                weight(width, inner),
                weight(inner, width),
            ],
            out_specs=[
                whole(chips, group_len + extra, width),
                whole(chips, group_len + extra, width),
                whole(chips, group_len, width),
                whole(chips, group_len, width),
            ],
            scratch_shapes=[
                pltpu.VMEM((held, slots, width), jnp.bfloat16),
                pltpu.VMEM((held, slots, width), jnp.bfloat16),
                pltpu.VMEM((held, slots, 1), jnp.float32),
                pltpu.VMEM((groups, held * MOST, group_len), jnp.bfloat16),
                pltpu.VMEM((groups, held * MOST, width), jnp.bfloat16),
                pltpu.VMEM((groups, held * MOST, width), jnp.bfloat16),
                pltpu.VMEM((groups, held, 1, group_len), jnp.float32),
            ],
        ),
        out_shape=[back, back, forth, forth],
        compiler_params=pltpu.CompilerParams(
            dimension_semantics=("arbitrary",), vmem_limit_bytes=58 * 2**20
        ),
        cost_estimate=pl.CostEstimate(
            flops=2 * 7 * held * slots * width * inner, transcendentals=0, bytes_accessed=2**24
        ),
        name="near_experts",
    )(me.reshape(1), x_near, x_twin, g_near, g_twin, mask_row, slot_row, router_t, w_gate, w_up, w_down)


def expert_weight_grads(ids, sums, x_near, x_twin, g_near, g_twin, mask_all, slot_all, router_t, weights, copies):
    unused, chips, group_len, width = x_near.shape
    held, unused, inner = weights[0].shape
    groups = 2 * chips
    slots = groups * MOST
    wide, narrow = width // copies, inner // copies

    def kernel(ids_ref, xn, xt, gn, gt, mr, sr, rt, wg, wu, wd, *refs):
        gate_out, up_out, down_out, x_scr, g_scr, gate_scr = refs[-6:]
        befores = refs[:-6] if sums is not None else (None, None, None)
        e = pl.program_id(0)
        mine, slab = ids_ref[0], ids_ref[1]

        @pl.when(e == 0)
        def _():
            expert_gather(
                lambda g: (xn if g < chips else xt)[0, g % chips],
                lambda g: (gn if g < chips else gt)[0, g % chips],
                lambda g: mr[g],
                lambda g: sr[g],
                rt[...], mine * held, x_scr, g_scr, gate_scr, None, groups,
            )

        x_slots = x_scr[e]
        hidden, dexpert, dgate_pre, dup_pre = expert_body(
            x_slots, g_scr[e], gate_scr[e], wg[0], wu[0], wd[0]
        )
        x_part, h_part = x_slots[:, :wide], hidden[:, :narrow]
        for k in range(1, copies):
            x_part = jnp.where(slab == k, x_slots[:, k * wide : (k + 1) * wide], x_part)
            h_part = jnp.where(slab == k, hidden[:, k * narrow : (k + 1) * narrow], h_part)
        for out, before, left, right in zip(
            (gate_out, up_out, down_out),
            befores,
            (x_part, x_part, h_part),
            (dgate_pre, dup_pre, dexpert),
        ):
            part = tn(left, right)
            out[0] = part if before is None else before[0] + part

    some = lambda *shape: pl.BlockSpec((groups,) + shape, lambda e, m: (m[2], 0, 0))
    rows = pl.BlockSpec((1, chips, group_len, width), lambda e, m: (m[2], 0, 0, 0))
    weight = lambda *shape: pl.BlockSpec((1,) + shape, lambda e, m: (e, 0, 0))
    whole = lambda *shape: pl.BlockSpec(shape, lambda e, m: (0,) * len(shape))
    outs = [(held, wide, inner), (held, wide, inner), (held, narrow, width)]
    return pl.pallas_call(
        kernel,
        grid_spec=pltpu.PrefetchScalarGridSpec(
            num_scalar_prefetch=1,
            grid=(held,),
            in_specs=[
                rows,
                rows,
                rows,
                rows,
                some(EXPERTS, group_len),
                some(held, group_len),
                whole(EXPERTS, width),
                weight(width, inner),
                weight(width, inner),
                weight(inner, width),
            ]
            + ([weight(*shape[1:]) for shape in outs] if sums is not None else []),
            out_specs=[weight(*shape[1:]) for shape in outs],
            scratch_shapes=[
                pltpu.VMEM((held, slots, width), jnp.bfloat16),
                pltpu.VMEM((held, slots, width), jnp.bfloat16),
                pltpu.VMEM((held, slots, 1), jnp.float32),
            ],
        ),
        out_shape=[jax.ShapeDtypeStruct(shape, jnp.float32) for shape in outs],
        compiler_params=pltpu.CompilerParams(
            dimension_semantics=("arbitrary",), vmem_limit_bytes=58 * 2**20
        ),
        cost_estimate=pl.CostEstimate(
            flops=2 * 4 * held * slots * width * inner, transcendentals=0, bytes_accessed=2**24
        ),
        input_output_aliases={11 + i: i for i in range(3)} if sums is not None else {},
        name="expert_weight_grads",
    )(ids, x_near, x_twin, g_near, g_twin, mask_all, slot_all, router_t, *weights, *(sums or ()))


def assemble_heads(core, near, twin, width, query_cols):
    chips = near.shape[0]
    devices = 2 * chips
    rows = 128
    pair = 2 * HEAD_DIM

    def kernel(core_ref, near_ref, twin_ref, query_ref, key_ref, value_ref):
        blocks = []
        for j in range(devices):
            mine = near_ref[j // 2].astype(jnp.float32)
            other = twin_ref[j // 2].astype(jnp.float32)
            blocks.append(jnp.where(core_ref[0] == j % 2, mine, other))
            query_ref[:, j * query_cols : (j + 1) * query_cols] = blocks[j][:, :query_cols]
        for c in range(chips):
            for ref, start in ((key_ref, query_cols), (value_ref, query_cols + HEAD_DIM)):
                ref[:, c * pair : (c + 1) * pair] = jnp.concatenate(
                    [blocks[2 * c + k][:, start : start + HEAD_DIM] for k in range(2)], axis=1
                )

    block = pl.BlockSpec((chips, rows, query_cols + pair), lambda r, m: (0, r, 0))
    shapes = [(width, devices * query_cols), (width, devices * HEAD_DIM), (width, devices * HEAD_DIM)]
    return pl.pallas_call(
        kernel,
        grid_spec=pltpu.PrefetchScalarGridSpec(
            num_scalar_prefetch=1,
            grid=(width // rows,),
            in_specs=[block, block],
            out_specs=[pl.BlockSpec((rows, s[1]), lambda r, m: (r, 0)) for s in shapes],
        ),
        out_shape=[jax.ShapeDtypeStruct(s, jnp.float32) for s in shapes],
        name="assemble_heads",
    )(core.reshape(1), near, twin)


def assemble_rows(core, near, twin, start, rows, width):
    chips, _, span = near.shape
    pieces = width // span

    def kernel(core_ref, near_ref, twin_ref, output_ref):
        mine = core_ref[0] == pl.program_id(0) % 2
        block = jnp.where(mine, near_ref[0].astype(jnp.float32), twin_ref[0].astype(jnp.float32))
        for z in range(pieces):
            output_ref[:, z * span : (z + 1) * span] = block[z * rows : (z + 1) * rows]

    block = pl.BlockSpec(
        (1, rows * pieces, span), lambda r, m: (r // 2, start // (rows * pieces), 0)
    )
    return pl.pallas_call(
        kernel,
        grid_spec=pltpu.PrefetchScalarGridSpec(
            num_scalar_prefetch=1,
            grid=(2 * chips,),
            in_specs=[block, block],
            out_specs=pl.BlockSpec((rows, width), lambda r, m: (r, 0)),
        ),
        out_shape=jax.ShapeDtypeStruct((2 * chips * rows, width), jnp.float32),
        name="assemble_rows",
    )(core.reshape(1), near, twin)


def turn(values, sign):
    lanes = lax.broadcasted_iota(jnp.int32, values.shape, 1)
    half = HEAD_DIM // 2
    ahead = pltpu.roll(values, values.shape[1] - half, 1)
    behind = pltpu.roll(values, half, 1)
    return jnp.where(lanes % HEAD_DIM < half, -sign * ahead, sign * behind)


def column_of(row):
    size = row.shape[1]
    diagonal = lax.broadcasted_iota(jnp.int32, (size, size), 0) == lax.broadcasted_iota(
        jnp.int32, (size, size), 1
    )
    return jnp.sum(jnp.where(diagonal, row, 0), axis=1, keepdims=True)


def attend_heads(me, near_pay, twin_pay, gain, head_weights, segs, index):
    chips = near_pay.shape[0]
    blocks, group_len = segs.shape
    width, head_cols = head_weights.shape
    length = blocks * group_len
    pair = 2 * HEAD_DIM

    def device(me, g):
        return 2 * (g % chips) + ((me & 1) ^ (g // chips))

    def kernel(me_ref, near_ref, twin_ref, gain_ref, w_ref, freq_ref, seg_ref, seg_rows, index_ref,
               index_rows, normed_out, qkv_out, cos_out, sin_out, attn_out, attended_out, lse_out,
               k_scr, v_scr, pos_scr):
        step = pl.program_id(0)

        @pl.when(step == 0)
        def _():
            numbers = seg_rows[...]
            start = jnp.zeros(numbers.shape, jnp.float32)
            for s in range(SEGMENTS - 1):
                found = jnp.where(numbers == s, 1.0, 0.0)
                count = jnp.sum(jnp.sum(found, axis=1, keepdims=True), axis=0, keepdims=True)
                start = start + jnp.where(numbers > s, count, 0.0)
            pos_scr[...] = index_rows[...].astype(jnp.float32) - start

        def project(pay_ref, half_row):
            rows = pay_ref[:, :group_len, :].reshape(chips * group_len, width).astype(jnp.float32)
            inverse = lax.rsqrt(jnp.mean(rows * rows, axis=1, keepdims=True) + NORM_EPS)
            normed = (rows * inverse * gain_ref[...]).astype(jnp.bfloat16)
            lin_all = jnp.dot(normed, w_ref[...], preferred_element_type=jnp.float32)
            for c in range(chips):
                g = half_row * chips + c
                here = slice(g * group_len, (g + 1) * group_len)
                normed_out[device(me_ref[0], g)] = normed[c * group_len : (c + 1) * group_len]
                lin = lin_all[c * group_len : (c + 1) * group_len]
                angles = freq_ref[...] * pos_scr[g : g + 1, :]
                cosine = jnp.transpose(jnp.concatenate([jnp.cos(angles)] * 4, axis=0))
                sine = jnp.transpose(jnp.concatenate([jnp.sin(angles)] * 4, axis=0))
                cos_out[here, :] = cosine
                sin_out[here, :] = sine
                query, rest = lin[:, :pair], lin[:, pair:]
                query = query * cosine + turn(query, 1.0) * sine
                key = rest * cosine + turn(rest, 1.0) * sine
                lanes = lax.broadcasted_iota(jnp.int32, rest.shape, 1)
                both = jnp.where(lanes < HEAD_DIM, key, rest).astype(jnp.bfloat16)
                qkv_out[here, :pair] = query.astype(jnp.bfloat16)
                qkv_out[here, pair:] = both
                k_scr[here, :] = both[:, :HEAD_DIM]
                v_scr[here, :] = both[:, HEAD_DIM:]

        @pl.when(step == 0)
        def _():
            project(near_ref, 0)

        @pl.when(step == 1)
        def _():
            project(twin_ref, 1)

        @pl.when(step >= 2)
        def _():
            g = step - 2
            here = pl.ds(pl.multiple_of(g * group_len, group_len), group_len)
            place = device(me_ref[0], g) * group_len + lax.broadcasted_iota(
                jnp.int32, (group_len, 1), 0
            )
            allowed = (seg_ref[...] == column_of(seg_rows[pl.ds(g, 1), :])) & (
                index_ref[...] <= place
            )
            outs, stats = [], []
            for h in range(pair // HEAD_DIM):
                query = qkv_out[here, h * HEAD_DIM : (h + 1) * HEAD_DIM] * jnp.bfloat16(ATTN_SCALE)
                scores = jnp.where(allowed, nt(query, k_scr[...]), NEG_FILL)
                top = jnp.max(scores, axis=1, keepdims=True)
                raised = jnp.exp(scores - top)
                total = jnp.sum(raised, axis=1, keepdims=True)
                probs = (raised * (1.0 / total)).astype(jnp.bfloat16)
                outs.append(jnp.dot(probs, v_scr[...], preferred_element_type=jnp.float32))
                stats.append(jnp.broadcast_to(top + jnp.log(total), (group_len, HEAD_DIM)))
            attended = jnp.concatenate(outs, axis=1)
            attended_out[...] = attended
            attn_out[0] = attended.astype(jnp.bfloat16)
            lse_out[...] = jnp.concatenate(stats, axis=1)

    half = HEAD_DIM // 2
    freqs = ROPE_BASE ** (-(jnp.arange(half, dtype=jnp.float32) * 2.0) / HEAD_DIM)
    whole = lambda *shape: pl.BlockSpec(shape, lambda i, m: (0,) * len(shape))
    second = lambda i: jnp.maximum(i - 2, 0)
    f32, bf16 = jnp.float32, jnp.bfloat16
    return pl.pallas_call(
        kernel,
        grid_spec=pltpu.PrefetchScalarGridSpec(
            num_scalar_prefetch=1,
            grid=(2 + blocks,),
            in_specs=[
                whole(*near_pay.shape),
                whole(*twin_pay.shape),
                whole(1, width),
                whole(width, head_cols),
                whole(half, 1),
                whole(1, length),
                whole(blocks, group_len),
                whole(1, length),
                whole(blocks, group_len),
            ],
            out_specs=[
                whole(blocks, group_len, width),
                whole(length, head_cols),
                whole(length, pair),
                whole(length, pair),
                pl.BlockSpec((1, group_len, pair), lambda i, m: (device(m[0], second(i)), 0, 0)),
                pl.BlockSpec((group_len, pair), lambda i, m: (second(i), 0)),
                pl.BlockSpec((group_len, pair), lambda i, m: (second(i), 0)),
            ],
            scratch_shapes=[
                pltpu.VMEM((length, HEAD_DIM), bf16),
                pltpu.VMEM((length, HEAD_DIM), bf16),
                pltpu.VMEM((blocks, group_len), f32),
            ],
        ),
        out_shape=[
            jax.ShapeDtypeStruct((blocks, group_len, width), bf16),
            jax.ShapeDtypeStruct((length, head_cols), bf16),
            jax.ShapeDtypeStruct((length, pair), f32),
            jax.ShapeDtypeStruct((length, pair), f32),
            jax.ShapeDtypeStruct((blocks, group_len, pair), bf16),
            jax.ShapeDtypeStruct((length, pair), f32),
            jax.ShapeDtypeStruct((length, pair), f32),
        ],
        cost_estimate=pl.CostEstimate(
            flops=2 * length * (width * head_cols + 4 * length * HEAD_DIM) * 2,
            transcendentals=2 * length * length,
            bytes_accessed=2**23,
        ),
        name="attend_heads",
    )(
        me.reshape(1), near_pay, twin_pay, gain[None], head_weights, freqs[:, None],
        segs.reshape(1, length), segs, index.reshape(1, length), index,
    )


def attend_back(me, near_db, twin_db, out_heads, qkv, cosine, sine, attended, lse, segs, index, copies):
    chips = near_db.shape[0]
    span = out_heads.shape[1] // copies
    blocks, group_len = segs.shape
    length, head_cols = qkv.shape
    width = out_heads.shape[1]
    pair = 2 * HEAD_DIM

    def device(me, g):
        return 2 * (g % chips) + ((me & 1) ^ (g // chips))

    def kernel(me_ref, near_ref, twin_ref, w_ref, qkv_ref, cos_ref, sin_ref, att_ref, lse_ref,
               seg_ref, seg_rows, index_ref, dlin_out, part_out, k_scr, v_scr, dk_scr, dv_scr, part_scr):
        g = pl.program_id(0)

        @pl.when(g == 0)
        def _():
            k_scr[...] = qkv_ref[:, pair : pair + HEAD_DIM]
            v_scr[...] = qkv_ref[:, pair + HEAD_DIM :]
            dk_scr[...] = jnp.zeros(dk_scr.shape, jnp.float32)
            dv_scr[...] = jnp.zeros(dv_scr.shape, jnp.float32)
            part_scr[...] = jnp.zeros(part_scr.shape, jnp.float32)

        def block(pay_ref):
            here = pl.ds(pl.multiple_of(g * group_len, group_len), group_len)
            mine = device(me_ref[0], g)
            place = mine * group_len + lax.broadcasted_iota(jnp.int32, (group_len, 1), 0)
            allowed = (seg_ref[...] == column_of(seg_rows[pl.ds(g, 1), :])) & (
                index_ref[...] <= place
            )
            rows = pay_ref[g % chips, :group_len, :]
            dattn = nt(rows, w_ref[...]).astype(jnp.bfloat16)
            attended = att_ref[here, :]
            wide = dattn.astype(jnp.float32) * attended
            part_scr[...] += tn(attended.astype(jnp.bfloat16), rows)
            outs = []
            for h in range(pair // HEAD_DIM):
                part = slice(h * HEAD_DIM, (h + 1) * HEAD_DIM)
                query = qkv_ref[here, part]
                scaled = query * jnp.bfloat16(ATTN_SCALE)
                scores = nt(scaled, k_scr[...])
                level = lse_ref[here, h * HEAD_DIM : h * HEAD_DIM + 1]
                probs = jnp.where(allowed, jnp.exp(scores - level), 0.0)
                delta = jnp.sum(wide[:, part], axis=1, keepdims=True)
                dscores = (probs * (nt(dattn[:, part], v_scr[...]) - delta)).astype(jnp.bfloat16)
                outs.append(jnp.dot(dscores, k_scr[...], preferred_element_type=jnp.float32))
                dk_scr[...] += tn(dscores, scaled)
                dv_scr[...] += tn(probs.astype(jnp.bfloat16), dattn[:, part])
            dquery = jnp.concatenate(outs, axis=1) * ATTN_SCALE
            dlin_out[mine, :, :pair] = (
                dquery * cos_ref[here, :] + turn(dquery * sin_ref[here, :], -1.0)
            ).astype(jnp.bfloat16)

        @pl.when(g < chips)
        def _():
            block(near_ref)

        @pl.when(g >= chips)
        def _():
            block(twin_ref)

        @pl.when(g == blocks - 1)
        def _():
            for z in range(copies):
                part_out[z] = part_scr[:, z * span : (z + 1) * span].astype(jnp.bfloat16)
            for b in range(blocks):
                here = slice(b * group_len, (b + 1) * group_len)
                both = jnp.concatenate([dk_scr[here, :], dv_scr[here, :]], axis=1)
                lanes = lax.broadcasted_iota(jnp.int32, both.shape, 1)
                turned = both * cos_ref[here, :] + turn(both * sin_ref[here, :], -1.0)
                dlin_out[device(me_ref[0], b), :, pair:] = jnp.where(
                    lanes < HEAD_DIM, turned, both
                ).astype(jnp.bfloat16)

    whole = lambda *shape: pl.BlockSpec(shape, lambda i, m: (0,) * len(shape))
    return pl.pallas_call(
        kernel,
        grid_spec=pltpu.PrefetchScalarGridSpec(
            num_scalar_prefetch=1,
            grid=(blocks,),
            in_specs=[
                whole(*near_db.shape),
                whole(*twin_db.shape),
                whole(*out_heads.shape),
                whole(length, head_cols),
                whole(length, pair),
                whole(length, pair),
                whole(length, pair),
                whole(length, pair),
                whole(1, length),
                whole(blocks, group_len),
                whole(1, length),
            ],
            out_specs=[whole(blocks, group_len, head_cols), whole(copies, pair, span)],
            scratch_shapes=[
                pltpu.VMEM((length, HEAD_DIM), jnp.bfloat16),
                pltpu.VMEM((length, HEAD_DIM), jnp.bfloat16),
                pltpu.VMEM((length, HEAD_DIM), jnp.float32),
                pltpu.VMEM((length, HEAD_DIM), jnp.float32),
                pltpu.VMEM((pair, width), jnp.float32),
            ],
        ),
        out_shape=[
            jax.ShapeDtypeStruct((blocks, group_len, head_cols), jnp.bfloat16),
            jax.ShapeDtypeStruct((copies, pair, span), jnp.bfloat16),
        ],
        cost_estimate=pl.CostEstimate(
            flops=2 * length * (width * pair + 10 * length * HEAD_DIM),
            transcendentals=2 * length * length,
            bytes_accessed=2**23,
        ),
        name="attend_back",
    )(
        me.reshape(1), near_db, twin_db, out_heads, qkv, cosine, sine, attended, lse,
        segs.reshape(1, length), segs, index.reshape(1, length),
    )


def swap_cores(block, devices):
    return lax.ppermute(block, "expert", [(i, i ^ 1) for i in range(devices)])


def across_chips(blocks, devices):
    groups = [[2 * c + core for c in range(devices // 2)] for core in range(2)]
    return lax.all_to_all(blocks, "expert", 0, 0, axis_index_groups=groups, tiled=True)


def permute(block, shift, axis, count):
    return lax.ppermute(block, axis, [(i, i ^ shift) for i in range(count)])


def spread_row(block, devices):
    near = across_chips(jnp.broadcast_to(block[None], (devices // 2,) + block.shape), devices)
    return near, swap_cores(near, devices)


def merge_cores(near, twin, devices):
    partner = swap_cores(twin, devices)
    return (near.astype(jnp.float32) + partner.astype(jnp.float32)).astype(jnp.bfloat16)


def permute_sum(parts, mine, step, axis, count):
    total = lax.dynamic_index_in_dim(parts, mine, 0, False).astype(jnp.float32)
    for s in range(1, parts.shape[0]):
        part = lax.dynamic_index_in_dim(parts, mine ^ s, 0, False)
        total = total + permute(part, s * step, axis, count).astype(jnp.float32)
    return total


def in_order(near, twin, core):
    even = jnp.where(core == 0, near, twin)
    odd = jnp.where(core == 0, twin, near)
    return jnp.stack([even, odd], axis=1).reshape((2 * near.shape[0],) + near.shape[1:])


def with_tail(rows, tail):
    height, span = tail.shape
    return jnp.concatenate(
        [rows, jnp.pad(tail, ((0, TAIL - height), (0, rows.shape[1] - span)))], axis=0
    )


def pack_gains(gains, span):
    high = gains.astype(jnp.bfloat16)
    lower = (gains - high.astype(jnp.float32)).astype(jnp.bfloat16)
    return jnp.concatenate([high, lower], axis=0).reshape(-1, span)


def unpack_gains(packed, width):
    parts = packed.reshape(packed.shape[0], 2, -1, width).astype(jnp.float32)
    return parts[:, 0] + parts[:, 1]


def exchange(blocks, axis):
    return lax.all_to_all(blocks, axis, 0, 0, tiled=True)


def broadcast(block, count):
    return jnp.broadcast_to(block[None], (count,) + block.shape)


def masked_gates(logits, mask):
    shown = jnp.where(mask, logits, NEG_FILL)
    weight = jnp.where(mask, jnp.exp(shown - jnp.max(shown, axis=-1, keepdims=True)), 0.0)
    return weight / jnp.sum(weight, axis=-1, keepdims=True)


def slot_tables(mask, first, held):
    group_len = mask.shape[2]
    local = lax.dynamic_slice_in_dim(mask, first, held, 1)
    steps = jnp.arange(group_len, dtype=jnp.int32)
    earlier = (steps[:, None] < steps[None, :]).astype(jnp.bfloat16)
    rank = jnp.einsum("gem,mn->gen", local, earlier, preferred_element_type=jnp.float32)
    return mask, jnp.where(local > 0, rank, -1.0).astype(jnp.int32)


def per_device_heads(
    tokens,
    attn_gain,
    w_query,
    w_key,
    w_value,
    w_output,
    moe_gain,
    w_router,
    w_gate,
    w_up,
    w_down,
    routes,
    segment_ids,
    out_grad,
):
    unused, group_len, width = tokens.shape
    devices, copies = lax.axis_size("expert"), lax.axis_size("dp")
    me, me_z = lax.axis_index("expert"), lax.axis_index("dp")
    core = me & 1
    chips = devices // 2
    length = group_len * devices
    repeats = HEADS // KV_HEADS
    query_cols = repeats * HEAD_DIM
    held = EXPERTS // devices
    order = jnp.stack([2 * c + (core ^ k) for k in range(2) for c in range(chips)])
    bf16 = jnp.bfloat16

    own = tokens[0]
    near_pay, twin_pay = spread_row(with_tail(own, segment_ids.astype(bf16)), devices)
    seg_rows = jnp.concatenate(
        [near_pay[:, group_len, :group_len], twin_pay[:, group_len, :group_len]], axis=0
    ).astype(jnp.int32)
    row_index = order[:, None] * group_len + jnp.arange(group_len, dtype=jnp.int32)

    mask_own = jnp.any(
        routes[0][:, :, None] == jnp.arange(EXPERTS, dtype=jnp.int32)[None, None, :], axis=1
    )
    tail_rows = EXPERTS * group_len // width
    mask_tail = jnp.swapaxes(mask_own.astype(bf16), 0, 1).reshape(tail_rows, width)
    grad_pay, near_pay = lax.optimization_barrier((with_tail(out_grad[0], mask_tail), near_pay))
    g_near, g_twin = spread_row(grad_pay, devices)

    def tables(near, twin, axis):
        tails = [side[..., group_len : group_len + tail_rows, :] for side in (near, twin)]
        return slot_tables(
            jnp.concatenate(tails, axis=axis).reshape(-1, EXPERTS, group_len), me * held, held
        )

    mask_row, slot_row = tables(g_near, g_twin, 0)
    g_near_all = lax.all_gather(g_near, "dp", axis=0)
    router_t = jnp.swapaxes(w_router, 0, 1)

    head_weights = jnp.concatenate(
        [
            lax.dynamic_slice_in_dim(w_query, me * query_cols, query_cols, 1),
            lax.dynamic_slice_in_dim(w_key, me * HEAD_DIM, HEAD_DIM, 1),
            lax.dynamic_slice_in_dim(w_value, me * HEAD_DIM, HEAD_DIM, 1),
        ],
        axis=1,
    )
    normed_row, qkv, cosine, sine, attn_heads, attended, lse = attend_heads(
        me, near_pay, twin_pay, attn_gain, head_weights, seg_rows, row_index
    )
    attn_heads, g_near, g_twin = lax.optimization_barrier((attn_heads, g_near, g_twin))
    attn_rows = jnp.swapaxes(exchange(attn_heads, "expert"), 0, 1).reshape(
        group_len, devices * query_cols
    )

    branch = jnp.dot(attn_rows, w_output, preferred_element_type=jnp.float32)
    residual = own.astype(jnp.float32)
    middle = residual + RESIDUAL_SCALE * branch
    normed2, unit_moe, inv_moe = rms_forward(middle, moe_gain)
    moe_rows = normed2.astype(bf16)
    gates_own = masked_gates(
        jnp.dot(moe_rows, w_router, preferred_element_type=jnp.float32), mask_own
    )
    x_near, x_twin = spread_row(moe_rows, devices)
    x_near_all = lax.all_gather(x_near, "dp", axis=0)

    d_near, d_twin, y_near, y_twin = near_experts(
        me, x_near, x_twin, g_near, g_twin, mask_row, slot_row, router_t, w_gate, w_up, w_down
    )
    d_merged = merge_cores(d_near, d_twin, devices)
    weights = (w_gate, w_up, w_down)

    def expert_row(z, sums, x_rows, g_rows, masks, slots):
        ids = jnp.stack([me, me_z, jnp.int32(z)])
        return expert_weight_grads(
            ids, sums, *x_rows, *g_rows, masks, slots, router_t, weights, copies
        )

    crossed = across_chips(d_merged, devices)
    x_mine, g_mine, d_merged = lax.optimization_barrier(
        ((x_near[None], x_twin[None]), (g_near[None], g_twin[None]), d_merged)
    )
    sums = expert_row(0, None, x_mine, g_mine, mask_row, slot_row)
    crossed, sums = lax.optimization_barrier((crossed, sums))
    returned = jnp.sum(crossed.astype(jnp.float32), axis=0)

    parts = returned[group_len : group_len + held] + returned[group_len + held : group_len + 2 * held]
    dgates = jnp.transpose(parts.reshape(held, devices, group_len), (2, 1, 0)).reshape(
        group_len, EXPERTS
    )
    dpicked = gates_own * (dgates - jnp.sum(gates_own * dgates, axis=-1, keepdims=True))
    dlogits = jnp.where(mask_own, dpicked, 0.0).astype(bf16)
    dnormed2 = returned[:group_len] + jnp.einsum(
        "ne,de->nd", dlogits, w_router, preferred_element_type=jnp.float32
    )
    dmiddle_norm, moe_gain_part = rms_backward(dnormed2, unit_moe, inv_moe, moe_gain)
    dmiddle = out_grad[0].astype(jnp.float32) + dmiddle_norm
    dbranch = (RESIDUAL_SCALE * dmiddle).astype(bf16)
    branch_near, branch_twin = spread_row(
        with_tail(dbranch, jnp.swapaxes(dlogits, 0, 1).reshape(tail_rows, width)), devices
    )
    dlogits_row = jnp.concatenate([branch_near[:, group_len:], branch_twin[:, group_len:]], axis=0)
    dlogits_row = dlogits_row[:, :tail_rows].reshape(devices, EXPERTS, group_len)

    out_heads = lax.dynamic_slice_in_dim(w_output, me * query_cols, query_cols, 0)
    dlin, output_part = attend_back(
        me, branch_near, branch_twin, out_heads, qkv, cosine, sine, attended, lse, seg_rows,
        row_index, copies,
    )
    head_cols = query_cols + 2 * HEAD_DIM
    rows_per = width // devices
    router_cols = lax.dynamic_slice_in_dim(
        jnp.concatenate([x_near, x_twin], axis=0), me * rows_per, rows_per, 2
    )
    router_part = jnp.einsum(
        "bnd,ben->de", router_cols, dlogits_row, preferred_element_type=jnp.float32
    ).astype(bf16)
    router_part = router_part.reshape(copies, -1, head_cols)
    router_rows = router_part.shape[1]
    router_part = jnp.pad(router_part, ((0, 0), (0, TAIL - router_rows), (0, 0)))
    head_part = jnp.einsum(
        "nd,nh->dh",
        normed_row.reshape(length, width),
        dlin.reshape(length, head_cols),
        preferred_element_type=jnp.float32,
    ).astype(bf16)
    rows = width // copies
    shared_part = jnp.concatenate(
        [head_part.reshape(copies, rows, head_cols), output_part, router_part], axis=1
    )

    shared_sum = permute_sum(shared_part, me_z, 1, "dp", copies).astype(bf16)
    dlin_back = jnp.swapaxes(exchange(dlin, "expert"), 0, 1)

    def token_grad(start, count, weights):
        rows = dlin_back[:, :, start : start + count].reshape(group_len, devices * count)
        return jnp.einsum("nh,dh->nd", rows, weights, preferred_element_type=jnp.float32)

    dnormed = (
        token_grad(0, query_cols, w_query)
        + token_grad(query_cols, HEAD_DIM, w_key)
        + token_grad(query_cols + HEAD_DIM, HEAD_DIM, w_value)
    )
    unused, unit_attn, inv_attn = rms_forward(residual, attn_gain)
    dresid_norm, attn_gain_part = rms_backward(dnormed, unit_attn, inv_attn, attn_gain)
    grad_tokens = (dmiddle + dresid_norm)[None]
    gain_parts = pack_gains(jnp.stack([attn_gain_part, moe_gain_part]), head_cols)
    column = exchange(broadcast(jnp.concatenate([shared_sum, gain_parts], axis=0), copies), "dp")

    g_near_all, x_near_all, y_near, y_twin, gain_parts = lax.optimization_barrier(
        (g_near_all, x_near_all, y_near, y_twin, gain_parts)
    )
    g_rows = (g_near_all, swap_cores(g_near_all, devices))
    x_rows = (x_near_all, swap_cores(x_near_all, devices))
    masks, slots = tables(*g_rows, 1)
    y_merged = merge_cores(y_near, y_twin, devices)
    y_sum = permute_sum(y_merged, me >> 1, 2, "expert", devices)

    def far_row(step, sums):
        return expert_row((me_z + step) % copies, sums, x_rows, g_rows, masks, slots)

    sums = far_row(1, sums)
    column, sums = lax.optimization_barrier((column, sums))
    router_start = rows + query_cols
    gain_start = router_start + TAIL
    gain_parts = pack_gains(jnp.sum(unpack_gains(column[:, gain_start:], width), axis=0), head_cols)
    column = jnp.concatenate(
        [
            column[:, :rows].reshape(-1, head_cols),
            column[:, rows:router_start].reshape(-1, head_cols),
            column[:, router_start : router_start + router_rows].reshape(-1, head_cols),
            gain_parts,
        ],
        axis=0,
    )
    head_near = across_chips(broadcast(column, chips), devices)
    for step in range(2, copies):
        sums = far_row(step, sums)
    head_near, sums = lax.optimization_barrier((head_near, sums))
    head_twin = swap_cores(head_near, devices)
    mixed = (middle + RESIDUAL_SCALE * y_sum).astype(bf16)[None]
    grad_gate, grad_up, grad_down = sums
    grad_query, grad_key, grad_value = assemble_heads(core, head_near, head_twin, width, query_cols)
    grad_output = assemble_rows(core, head_near, head_twin, width, query_cols, width)
    router_start = width + query_cols * copies
    gain_start = router_start + router_rows * copies
    grad_router = in_order(
        head_near[:, router_start:gain_start], head_twin[:, router_start:gain_start], core
    ).reshape(width, EXPERTS).astype(jnp.float32)
    gain_sums = jnp.sum(unpack_gains(head_near[:, gain_start:], width), axis=0) + jnp.sum(
        unpack_gains(head_twin[:, gain_start:], width), axis=0
    )
    return (
        mixed,
        grad_tokens,
        gain_sums[0],
        grad_query,
        grad_key,
        grad_value,
        grad_output,
        gain_sums[1],
        grad_router,
        grad_gate,
        grad_up,
        grad_down,
    )


def solution(mesh):
    placed = (
        P("dp", "expert", None),
        P(),
        P(),
        P(),
        P(),
        P(),
        P(),
        P(),
        P("expert", None, None),
        P("expert", None, None),
        P("expert", None, None),
        P("dp", "expert", None),
        P("dp", "expert"),
        P("dp", "expert", None),
    )
    by_heads = mesh.shape["expert"] == KV_HEADS
    return jax.shard_map(
        per_device_heads if by_heads else per_device_general,
        mesh=mesh,
        in_specs=placed,
        out_specs=(
            P("dp", "expert", None),
            P("dp", "expert", None),
            P(),
            P(),
            P(),
            P(),
            P(),
            P(),
            P(),
            P("expert", "dp", None),
            P("expert", "dp", None),
            P("expert", "dp", None),
        ),
        check_vma=False,
    )
```

profile of v0, /device:TPU:0, one launch (start us, length us, event | category | flops | bytes accessed | tf_op | source)
XLA Modules:
  0.0 372.9 jit_solution(6662343238452088080)
XLA Ops:
  10.2 5.2 %all-to-all-start = ((bf16[4,144,1024]{2,1,0:T(8,128)(2,1)}), bf16[4,144,1024]{2,1,0:T(8,128)(2,1)}, u32[]{:S(2)}, u32[]{:S(2)}) async-start(bf16[4,144,1024]{2,1,0:T(8,128)(2,1)} %broadcast_in_dim.39), calls=%async_computation | async-start | bytes 2359296 | tf_op jit(solution)/shard_map/all_to_all | solution.py:978
  15.5 15.6 %all-to-all-done.near_ref = bf16[4,144,1024]{2,1,0:T(8,128)(2,1)} async-done(((bf16[4,144,1024]{2,1,0:T(8,128)(2,1)}), bf16[4,144,1024]{2,1,0:T(8,128)(2,1)}, u32[]{:S(2)}, u32[]{:S(2)}) %all-to-all-start) | async-done | bytes 1179680 | tf_op jit(solution)/shard_map/all_to_all | solution.py:978
  32.3 4.3 %all-to-all-start.1 = ((bf16[4,144,1024]{2,1,0:T(8,128)(2,1)}), bf16[4,144,1024]{2,1,0:T(8,128)(2,1)}, u32[]{:S(2)}, u32[]{:S(2)}) async-start(bf16[4,144,1024]{2,1,0:T(8,128)(2,1)} %broadcast_in_dim.41), calls=%async_computation.1 | async-start | bytes 2359296 | tf_op jit(solution)/shard_map/all_to_all | solution.py:978
  36.6 3.2 copy.93
  40.8 1.3 constant_dynamic-slice_fusion.2
  42.0 9.3 %all-to-all-done.1.gn = bf16[4,144,1024]{2,1,0:T(8,128)(2,1)} async-done(((bf16[4,144,1024]{2,1,0:T(8,128)(2,1)}), bf16[4,144,1024]{2,1,0:T(8,128)(2,1)}, u32[]{:S(2)}, u32[]{:S(2)}) %all-to-all-start.1) | async-done | bytes 1179680 | tf_op jit(solution)/shard_map/all_to_all | solution.py:978
  54.4 2.6 copy.96.twin_ref
  58.3 17.1 %attend_heads.1 = (bf16[8,128,1024]{2,1,0:T(8,128)(2,1)}, bf16[1024,256]{1,0:T(8,128)(2,1)}, f32[1024,128]{1,0:T(8,128)}, f32[1024,128]{1,0:T(8,128)}, bf16[8,12...) custom-call(s32[1]{0:T(128)} %bitcast.1.me_ref, bf16[4,144,1024]{2,1,0:T(8,128)(2,1)} %all-to-all-done.near_ref, ...), custom_call_target="tpu_custom_call" | custom-call | flops 2147483648 | bytes 8388608 | tf_op jit(solution)/shard_map/attend_heads/pallas_call | solution.py:802
  75.4 10.2 %all_to_all.45 = bf16[8,128,128]{2,1,0:T(8,128)(2,1)S(1)} all-to-all(bf16[8,128,128]{2,1,0:T(8,128)(2,1)} %get-tuple-element.68), channel_id=1, replica_groups=mesh['dp'=4,'expert'=8] {'expert'}, dimensions={0} | all-to-all | bytes 524288 | tf_op jit(solution)/shard_map/all_to_all | solution.py:1028
  86.7 17.6 %all_to_all.46.xn = bf16[4,128,1024]{2,1,0:T(8,128)(2,1)} all-to-all(bf16[4,128,1024]{2,1,0:T(8,128)(2,1)S(1)} %broadcast_in_dim.42), channel_id=1, replica_groups={{0,2,4,6},{1,3,5,7},{8,10,12,14},{9,11,13,15},{16,18,20,22},{17,19,21,2..., dimensions={0} | all-to-all | bytes 2097152 | tf_op jit(solution)/shard_map/all_to_all | solution.py:978
  107.3 20.4 %near_experts.1 = (bf16[4,144,1024]{2,1,0:T(8,128)(2,1)}, bf16[4,144,1024]{2,1,0:T(8,128)(2,1)}, bf16[4,128,1024]{2,1,0:T(8,128)(2,1)}, bf16[4,128,1024]{2,1,0:T(8,128)(2,1)}) custom-call(s32[1]{0:T(128)} %bitcast.1.me_ref, bf16[4,128,1024]{2,1,0:T(8,128)(2,1)} %all_to_all.46.xn, bf16[4,128,1024]{2,1,0:T(8,128)(2,1)} %collective-permute-done.2.xt, ...), custom_call_target="tpu_custom_call" | custom-call | flops 11274289152 | bytes 16777216 | tf_op jit(solution)/shard_map/near_experts/pallas_call | solution.py:512
  129.1 1.8 collective-permute-done.3
  130.8 3.1 add_convert_fusion
  134.0 4.3 %all-to-all-start.4 = ((bf16[4,144,1024]{2,1,0:T(8,128)(2,1)}), bf16[4,144,1024]{2,1,0:T(8,128)(2,1)}, u32[]{:S(2)}, u32[]{:S(2)}) async-start(bf16[4,144,1024]{2,1,0:T(8,128)(2,1)} %add_convert_fusion), calls=%async_computation.4 | async-start | bytes 2359296 | tf_op jit(solution)/shard_map/all_to_all | solution.py:978
  139.0 16.0 %expert_weight_grads.4 = (f32[4,256,512]{2,1,0:T(8,128)}, f32[4,256,512]{2,1,0:T(8,128)}, f32[4,128,1024]{2,1,0:T(8,128)}) custom-call(s32[3]{0:T(128)} %get-tuple-element.192.ids_ref, bf16[1,4,128,1024]{3,2,1,0:T(8,128)(2,1)} %bitcast.128, bf16[1,4,128,1024]{3,2,1,0:T(8,128)(2,1)} %bitcast.26.xt, bf16[1,4,144,1024]{3,2,1,0:T(8,128)(2,1)} %bitcast.27.gn, ...), custom_call_target="tpu_custom_call" | custom-call | flops 6442450944 | bytes 16777216 | tf_op jit(solution)/shard_map/expert_weight_grads/pallas_call | solution.py:601
  155.0 1.5 convert_reduce_fusion
  157.5 1.4 multiply_reduce_fusion.1
  158.9 1.2 multiply_convert_fusion
  160.3 19.7 %all_to_all.47.near_ref = bf16[4,144,1024]{2,1,0:T(8,128)(2,1)S(1)} all-to-all(bf16[4,144,1024]{2,1,0:T(8,128)(2,1)S(1)} %broadcast_in_dim.50), channel_id=1, replica_groups={{0,2,4,6},{1,3,5,7},{8,10,12,14},{9,11,13,15},{16,18,20,22},{17,19,21,2..., dimensions={0} | all-to-all | bytes 2359296 | tf_op jit(solution)/shard_map/all_to_all | solution.py:978
  181.8 2.1 collective-permute-done.4.twin_ref
  184.9 15.3 %attend_back.1 = (bf16[8,128,256]{2,1,0:T(8,128)(2,1)}, bf16[4,128,256]{2,1,0:T(8,128)(2,1)}) custom-call(s32[1]{0:T(128)} %bitcast.1.me_ref, bf16[4,144,1024]{2,1,0:T(8,128)(2,1)} %copy-done.13, bf16[4,144,1024]{2,1,0:T(8,128)(2,1)} %copy-done.20, bf16[128,1024]{1,0:T(8,128)(2,1)} %constant_dynamic-slice_fusion.1.w_ref, ...), custom_call_target="tpu_custom_call" | custom-call | flops 1610612736 | bytes 8388608 | tf_op jit(solution)/shard_map/attend_back/pallas_call | solution.py:929
  200.2 3.5 all-to-all-start.6
  204.4 9.0 %all-to-all-done.6 = bf16[8,128,256]{2,1,0:T(8,128)(2,1)S(1)} async-done(((bf16[8,128,256]{2,1,0:T(8,128)(2,1)}), bf16[8,128,256]{2,1,0:T(8,128)(2,1)S(1)}, u32[]{:S(2)}, u32[]{:S(2)}) %all-to-all-start.6) | async-done | bytes 524320 | tf_op jit(solution)/shard_map/all_to_all | solution.py:1028
  215.3 2.6 fusion.52
  218.5 1.8 fusion.12
  220.4 2.7 all-gather.7.cloned.1.call-done
  226.9 2.4 fusion.1
  229.5 2.4 collective-permute-start.11
  233.0 4.1 %collective-permute-done.9 = bf16[400,256]{1,0:T(8,128)(2,1)S(1)} collective-permute-done((bf16[400,256]{1,0:T(8,128)(2,1)S(1)}, bf16[400,256]{1,0:T(8,128)(2,1)S(1)}, u32[]{:S(2)}, u32[]{:S(2)}) %collective-permute-start.9) | collective-permute-done | bytes 204832 | tf_op jit(solution)/shard_map/ppermute | solution.py:982
  237.1 5.2 %collective-permute-done.11 = bf16[400,256]{1,0:T(8,128)(2,1)S(1)} collective-permute-done((bf16[400,256]{1,0:T(8,128)(2,1)S(1)}, bf16[400,256]{1,0:T(8,128)(2,1)S(1)}, u32[]{:S(2)}, u32[]{:S(2)}) %collective-permute-start.11) | collective-permute-done | bytes 204832 | tf_op jit(solution)/shard_map/ppermute | solution.py:982
  242.3 8.5 %collective-permute-done.10 = bf16[400,256]{1,0:T(8,128)(2,1)S(1)} collective-permute-done((bf16[400,256]{1,0:T(8,128)(2,1)S(1)}, bf16[400,256]{1,0:T(8,128)(2,1)S(1)}, u32[]{:S(2)}, u32[]{:S(2)}) %collective-permute-start.10) | collective-permute-done | bytes 204832 | tf_op jit(solution)/shard_map/ppermute | solution.py:982
  251.9 3.5 all-to-all-start.7
  258.6 16.3 %expert_weight_grads.5 = (f32[4,256,512]{2,1,0:T(8,128)}, f32[4,256,512]{2,1,0:T(8,128)}, f32[4,128,1024]{2,1,0:T(8,128)}) custom-call(s32[3]{0:T(128)} %get-tuple-element.191.ids_ref, bf16[4,4,128,1024]{3,2,1,0:T(8,128)(2,1)} %bitcast.125, ...), custom_call_target="tpu_custom_call", output_to_operand_aliasing={{0}: (11, {}), {1}: (12, {}), {2}: (13, {})} | custom-call | flops 6442450944 | bytes 16777216 | tf_op jit(solution)/shard_map/expert_weight_grads/pallas_call | solution.py:601
  274.9 1.3 all-to-all-done.7
  276.5 1.9 broadcast_in_dim.104
  278.4 4.9 %all-to-all-start.8 = ((bf16[4,1568,256]{2,1,0:T(8,128)(2,1)}), bf16[4,1568,256]{2,1,0:T(8,128)(2,1)}, u32[]{:S(2)}, u32[]{:S(2)}) async-start(bf16[4,1568,256]{2,1,0:T(8,128)(2,1)} %broadcast_in_dim.104), calls=%async_computation.8 | async-start | bytes 6422528 | tf_op jit(solution)/shard_map/all_to_all | solution.py:978
  283.3 16.3 %expert_weight_grads.6 = (f32[4,256,512]{2,1,0:T(8,128)}, f32[4,256,512]{2,1,0:T(8,128)}, f32[4,128,1024]{2,1,0:T(8,128)}) custom-call(s32[3]{0:T(128)} %get-tuple-element.170.ids_ref, bf16[4,4,128,1024]{3,2,1,0:T(8,128)(2,1)} %bitcast.126, ...), custom_call_target="tpu_custom_call", output_to_operand_aliasing={{0}: (11, {}), {1}: (12, {}), {2}: (13, {})} | custom-call | flops 6442450944 | bytes 16777216 | tf_op jit(solution)/shard_map/expert_weight_grads/pallas_call | solution.py:601
  299.6 16.4 %expert_weight_grads.7 = (f32[4,256,512]{2,1,0:T(8,128)}, f32[4,256,512]{2,1,0:T(8,128)}, f32[4,128,1024]{2,1,0:T(8,128)}) custom-call(s32[3]{0:T(128)} %get-tuple-element.190.ids_ref, bf16[4,4,128,1024]{3,2,1,0:T(8,128)(2,1)} %bitcast.127, ...), custom_call_target="tpu_custom_call", output_to_operand_aliasing={{0}: (11, {}), {1}: (12, {}), {2}: (13, {})} | custom-call | flops 6442450944 | bytes 16777216 | tf_op jit(solution)/shard_map/expert_weight_grads/pallas_call | solution.py:601
  316.0 3.7 all-to-all-done.8.near_ref
  320.2 7.1 %collective-permute-done.5 = bf16[4,128,1024]{2,1,0:T(8,128)(2,1)} collective-permute-done((bf16[4,128,1024]{2,1,0:T(8,128)(2,1)S(1)}, bf16[4,128,1024]{2,1,0:T(8,128)(2,1)}, u32[]{:S(2)}, u32[]{:S(2)}) %collective-permute-start.5) | collective-permute-done | bytes 1048608 | tf_op jit(solution)/shard_map/ppermute | solution.py:973
  327.3 2.0 add_convert_fusion.1
  330.1 1.4 collective-permute-start.6
  331.6 1.5 collective-permute-start.8
  333.6 6.0 %collective-permute-done.6 = bf16[128,1024]{1,0:T(8,128)(2,1)} collective-permute-done((bf16[128,1024]{1,0:T(8,128)(2,1)}, bf16[128,1024]{1,0:T(8,128)(2,1)}, u32[]{:S(2)}, u32[]{:S(2)}) %collective-permute-start.6) | collective-permute-done | bytes 262176 | tf_op jit(solution)/shard_map/ppermute | solution.py:982
  339.6 5.8 %collective-permute-done.8 = bf16[128,1024]{1,0:T(8,128)(2,1)} collective-permute-done((bf16[128,1024]{1,0:T(8,128)(2,1)}, bf16[128,1024]{1,0:T(8,128)(2,1)}, u32[]{:S(2)}, u32[]{:S(2)}) %collective-permute-start.8) | collective-permute-done | bytes 262176 | tf_op jit(solution)/shard_map/ppermute | solution.py:982
  346.6 2.3 fusion.16
  351.6 6.6 %assemble_rows.1 = f32[1024,1024]{1,0:T(8,128)} custom-call(s32[1]{0:T(128)} %bitcast.9.core_ref, bf16[4,1568,256]{2,1,0:T(8,128)(2,1)} %all-to-all-done.8.near_ref, bf16[4,1568,256]{2,1,0:T(8,128)(2,1)} %collective-permute-done.14.twin_ref), custom_call_target="tpu_custom_call" | custom-call | tf_op jit(solution)/shard_map/assemble_rows/pallas_call | solution.py:685
  358.2 7.6 %assemble_heads.1 = (f32[1024,1024]{1,0:T(8,128)}, f32[1024,512]{1,0:T(8,128)}, f32[1024,512]{1,0:T(8,128)}) custom-call(s32[1]{0:T(128)} %bitcast.9.core_ref, bf16[4,1568,256]{2,1,0:T(8,128)(2,1)} %all-to-all-done.8.near_ref, bf16[4,1568,256]{2,1,0:T(8,128)(2,1)} %collective-permute-done.14.twin_ref), custom_call_target="tpu_custom_call" | custom-call | tf_op jit(solution)/shard_map/assemble_heads/pallas_call | solution.py:659
  (177 shorter events, 37.9 us)
Async XLA Ops:
  7.2 78.7 %copy-start = (bf16[1024,1024]{1,0:T(8,128)(2,1)S(1)}, bf16[1024,1024]{1,0:T(8,128)(2,1)}, u32[]{:S(2)}) copy-start(bf16[1024,1024]{1,0:T(8,128)(2,1)} %param.19) | copy-start | bytes 6291460
  8.0 7.4 %copy-start.21 = (s32[1,128,8]{1,2,0:T(8,128)S(1)}, s32[1,128,8]{1,2,0:T(8,128)}, u32[]{:S(2)}) copy-start(s32[1,128,8]{1,2,0:T(8,128)} %param.25) | copy-start | bytes 12292
  8.0 7.4 %copy-start.5 = (bf16[1,128,1024]{2,1,0:T(8,128)(2,1)S(1)}, bf16[1,128,1024]{2,1,0:T(8,128)(2,1)}, u32[]{:S(2)}) copy-start(bf16[1,128,1024]{2,1,0:T(8,128)(2,1)} %param.27) | copy-start | bytes 786436
  10.2 20.9 %all-to-all-start = ((bf16[4,144,1024]{2,1,0:T(8,128)(2,1)}), bf16[4,144,1024]{2,1,0:T(8,128)(2,1)}, u32[]{:S(2)}, u32[]{:S(2)}) async-start(bf16[4,144,1024]{2,1,0:T(8,128)(2,1)} %broadcast_in_dim.39), calls=%async_computation | async-start | bytes 2359296 | tf_op jit(solution)/shard_map/all_to_all | solution.py:978
  32.3 19.1 %all-to-all-start.1 = ((bf16[4,144,1024]{2,1,0:T(8,128)(2,1)}), bf16[4,144,1024]{2,1,0:T(8,128)(2,1)}, u32[]{:S(2)}, u32[]{:S(2)}) async-start(bf16[4,144,1024]{2,1,0:T(8,128)(2,1)} %broadcast_in_dim.41), calls=%async_computation.1 | async-start | bytes 2359296 | tf_op jit(solution)/shard_map/all_to_all | solution.py:978
  36.5 183.9 %all-gather.5.cloned.1.call-start = ((), (), s32[]{:S(2)}) async-start(), calls=%async_computation.9 | async-start | bytes 5898240 | tf_op jit(solution)/shard_map/all_gather | solution.py:1100
  39.8 14.6 %collective-permute-start = (bf16[4,144,1024]{2,0,1:T(4,128)(2,1)}, bf16[4,144,1024]{2,0,1:T(4,128)(2,1)}, u32[]{:S(2)}, u32[]{:S(2)}) collective-permute-start(bf16[4,144,1024]{2,0,1:T(4,128)(2,1)} %copy.93), channel_id=1, source_target_pairs={{0,1},{1,0},{2,3},{3,2},{4,5},{5,4},{6,7},{7,6},{8,9},{9,8},{10,11... | collective-permute-start | bytes 3538952 | tf_op jit(solution)/shard_map/ppermute | solution.py:973
  53.0 22.4 %collective-permute-start.1 = (bf16[4,144,1024]{2,1,0:T(8,128)(2,1)}, bf16[4,144,1024]{2,1,0:T(8,128)(2,1)}, u32[]{:S(2)}, u32[]{:S(2)}) collective-permute-start(bf16[4,144,1024]{2,1,0:T(8,128)(2,1)} %all-to-all-done.1.gn), channel_id=1, source_target_pairs={{0,1},{1,0},{2,3},{3,2},{4,5},{5,4},{6,7},{7,6},{8,9},{9,8},{10,11... | collective-permute-start | bytes 3538952 | tf_op jit(solution)/shard_map/ppermute | solution.py:973
  58.3 27.5 %copy-start.3 = (bf16[1,128,1024]{2,1,0:T(8,128)(2,1)S(1)}, bf16[1,128,1024]{2,1,0:T(8,128)(2,1)}, u32[]{:S(2)}) copy-start(bf16[1,128,1024]{2,1,0:T(8,128)(2,1)} %param.14) | copy-start | bytes 786436
  75.4 11.0 %copy-start.18 = (f32[1024]{0:T(1024)S(1)}, f32[1024]{0:T(1024)}, u32[]{:S(2)}) copy-start(f32[1024]{0:T(1024)} %param.20) | copy-start | bytes 12292
  104.3 3.0 collective-permute-start.2
  106.1 1.2 copy-start.17
  127.6 3.2 collective-permute-start.3
  130.8 7.5 %copy-start.9 = (bf16[1024,32]{0,1:T(8,128)(2,1)S(1)}, bf16[1024,32]{0,1:T(8,128)(2,1)}, u32[]{:S(2)}) copy-start(bf16[1024,32]{0,1:T(8,128)(2,1)} %param.21) | copy-start | bytes 196612
  134.0 21.1 %all-to-all-start.4 = ((bf16[4,144,1024]{2,1,0:T(8,128)(2,1)}), bf16[4,144,1024]{2,1,0:T(8,128)(2,1)}, u32[]{:S(2)}, u32[]{:S(2)}) async-start(bf16[4,144,1024]{2,1,0:T(8,128)(2,1)} %add_convert_fusion), calls=%async_computation.4 | async-start | bytes 2359296 | tf_op jit(solution)/shard_map/all_to_all | solution.py:978
  138.3 84.9 %all-gather.7.cloned.1.call-start = ((), (), s32[]{:S(2)}) async-start(), calls=%async_computation.10 | async-start | bytes 5242880 | tf_op jit(solution)/shard_map/all_gather | solution.py:1128
  139.0 18.5 %copy-start.10 = (bf16[1024,32]{0,1:T(8,128)(2,1)S(1)}, bf16[1024,32]{0,1:T(8,128)(2,1)}, u32[]{:S(2)}) copy-start(bf16[1024,32]{0,1:T(8,128)(2,1)} %param.21) | copy-start | bytes 196612
  158.9 21.1 %copy-start.22 = (f32[128]{0:T(128)}, f32[128]{0:T(128)S(1)}, u32[]{:S(2)}) copy-start(f32[128]{0:T(128)S(1)} %broadcast_multiply_fusion.1) | copy-start | bytes 1540
  180.0 1.0 copy-start.13
  181.0 2.8 collective-permute-start.4
  200.2 13.2 %all-to-all-start.6 = ((bf16[8,128,256]{2,1,0:T(8,128)(2,1)}), bf16[8,128,256]{2,1,0:T(8,128)(2,1)S(1)}, u32[]{:S(2)}, u32[]{:S(2)}) async-start(bf16[8,128,256]{2,1,0:T(8,128)(2,1)} %get-tuple-element.88), calls=%async_computation.6 | async-start | bytes 1048576 | tf_op jit(solution)/shard_map/all_to_all | solution.py:1028
  214.4 3.5 copy-start.11
  215.3 2.6 copy-start.14
  215.3 3.1 copy-start.12
  215.3 3.1 copy-start.19
  215.3 3.1 copy-start.24
  218.5 7.1 %copy-start.2 = (bf16[4,128,1024]{2,1,0:T(8,128)(2,1)S(1)}, bf16[4,128,1024]{2,1,0:T(8,128)(2,1)}, u32[]{:S(2)}) copy-start(bf16[4,128,1024]{2,1,0:T(8,128)(2,1)} %all_to_all.46.xn) | copy-start | bytes 3145732
  220.3 6.6 %copy-start.15 = (bf16[8,128,256]{2,1,0:T(8,128)(2,1)S(1)}, bf16[8,128,256]{2,1,0:T(8,128)(2,1)}, u32[]{:S(2)}) copy-start(bf16[8,128,256]{2,1,0:T(8,128)(2,1)} %get-tuple-element.88) | copy-start | bytes 1572868
  223.1 33.3 %collective-permute-start.13 = (bf16[4,4,144,1024]{3,2,1,0:T(8,128)(2,1)}, bf16[4,4,144,1024]{3,2,1,0:T(8,128)(2,1)}, u32[]{:S(2)}, u32[]{:S(2)}) collective-permute-start(bf16[4,4,144,1024]{3,2,1,0:T(8,128)(2,1)} %bitcast.119), channel_id=1, source_target_pairs={{0,1},{1,0},{2,3},{3,2},{4,5},{5,4},{6,7},{7,6},{8,9},{9,8},{10,11... | collective-permute-start | bytes 14155784 | tf_op jit(solution)/shard_map/ppermute | solution.py:973
  223.2 35.5 %collective-permute-start.12 = (bf16[4,4,128,1024]{3,2,1,0:T(8,128)(2,1)}, bf16[4,4,128,1024]{3,2,1,0:T(8,128)(2,1)}, u32[]{:S(2)}, u32[]{:S(2)}) collective-permute-start(bf16[4,4,128,1024]{3,2,1,0:T(8,128)(2,1)} %bitcast.124), channel_id=1, source_target_pairs={{0,1},{1,0},{2,3},{3,2},{4,5},{5,4},{6,7},{7,6},{8,9},{9,8},{10,11... | collective-permute-start | bytes 12582920 | tf_op jit(solution)/shard_map/ppermute | solution.py:973
  226.9 2.4 copy-start.16
  229.4 7.6 %collective-permute-start.9 = (bf16[400,256]{1,0:T(8,128)(2,1)S(1)}, bf16[400,256]{1,0:T(8,128)(2,1)S(1)}, u32[]{:S(2)}, u32[]{:S(2)}) collective-permute-start(bf16[400,256]{1,0:T(8,128)(2,1)S(1)} %get-tuple-element.181), channel_id=1, source_target_pairs={{0,8},{8,0},{16,24},{24,16},{1,9},{9,1},{17,25},{25,17},{2,10},{10... | collective-permute-start | bytes 614408 | tf_op jit(solution)/shard_map/ppermute | solution.py:982
  229.5 12.8 %collective-permute-start.11 = (bf16[400,256]{1,0:T(8,128)(2,1)S(1)}, bf16[400,256]{1,0:T(8,128)(2,1)S(1)}, u32[]{:S(2)}, u32[]{:S(2)}) collective-permute-start(bf16[400,256]{1,0:T(8,128)(2,1)S(1)} %get-tuple-element.182), channel_id=1, source_target_pairs={{0,24},{8,16},{16,8},{24,0},{1,25},{9,17},{17,9},{25,1},{2,26},{10... | collective-permute-start | bytes 614408 | tf_op jit(solution)/shard_map/ppermute | solution.py:982
  231.9 19.0 %collective-permute-start.10 = (bf16[400,256]{1,0:T(8,128)(2,1)S(1)}, bf16[400,256]{1,0:T(8,128)(2,1)S(1)}, u32[]{:S(2)}, u32[]{:S(2)}) collective-permute-start(bf16[400,256]{1,0:T(8,128)(2,1)S(1)} %get-tuple-element.183), channel_id=1, source_target_pairs={{0,16},{8,24},{16,0},{24,8},{1,17},{9,25},{17,1},{25,9},{2,18},{10... | collective-permute-start | bytes 614408 | tf_op jit(solution)/shard_map/ppermute | solution.py:982
  251.9 24.3 %all-to-all-start.7 = ((bf16[4,416,256]{2,1,0:T(8,128)(2,1)}), bf16[4,416,256]{2,1,0:T(8,128)(2,1)S(1)}, u32[]{:S(2)}, u32[]{:S(2)}) async-start(bf16[4,416,256]{2,1,0:T(8,128)(2,1)} %broadcast_in_dim.53), calls=%async_computation.7 | async-start | bytes 1703936 | tf_op jit(solution)/shard_map/all_to_all | solution.py:1028
  278.4 41.3 %all-to-all-start.8 = ((bf16[4,1568,256]{2,1,0:T(8,128)(2,1)}), bf16[4,1568,256]{2,1,0:T(8,128)(2,1)}, u32[]{:S(2)}, u32[]{:S(2)}) async-start(bf16[4,1568,256]{2,1,0:T(8,128)(2,1)} %broadcast_in_dim.104), calls=%async_computation.8 | async-start | bytes 6422528 | tf_op jit(solution)/shard_map/all_to_all | solution.py:978
  299.6 20.1 %copy-start.27 = (bf16[4,128,1024]{2,1,0:T(8,128)(2,1)S(1)}, bf16[4,128,1024]{2,1,0:T(8,128)(2,1)}, u32[]{:S(2)}) copy-start(bf16[4,128,1024]{2,1,0:T(8,128)(2,1)} %get-tuple-element.90) | copy-start | bytes 3145732
  319.7 29.2 %collective-permute-start.14 = (bf16[4,1568,256]{2,1,0:T(8,128)(2,1)}, bf16[4,1568,256]{2,1,0:T(8,128)(2,1)}, u32[]{:S(2)}, u32[]{:S(2)}) collective-permute-start(bf16[4,1568,256]{2,1,0:T(8,128)(2,1)} %all-to-all-done.8.near_ref), channel_id=1, source_target_pairs={{0,1},{1,0},{2,3},{3,2},{4,5},{5,4},{6,7},{7,6},{8,9},{9,8},{10,11... | collective-permute-start | bytes 9633800 | tf_op jit(solution)/shard_map/ppermute | solution.py:973
  319.7 7.6 %collective-permute-start.5 = (bf16[4,128,1024]{2,1,0:T(8,128)(2,1)S(1)}, bf16[4,128,1024]{2,1,0:T(8,128)(2,1)}, u32[]{:S(2)}, u32[]{:S(2)}) collective-permute-start(bf16[4,128,1024]{2,1,0:T(8,128)(2,1)S(1)} %copy-done.27), channel_id=1, source_target_pairs={{0,1},{1,0},{2,3},{3,2},{4,5},{5,4},{6,7},{7,6},{8,9},{9,8},{10,11... | collective-permute-start | bytes 3145736 | tf_op jit(solution)/shard_map/ppermute | solution.py:973
  320.2 13.4 %copy-start.26 = (f32[128]{0:T(128)S(1)}, f32[128]{0:T(128)}, u32[]{:S(2)}) copy-start(f32[128]{0:T(128)} %get-tuple-element.168) | copy-start | bytes 1540
  320.2 26.3 %copy-start.6 = (bf16[1,128,1024]{2,1,0:T(8,128)(2,1)S(1)}, bf16[1,128,1024]{2,1,0:T(8,128)(2,1)}, u32[]{:S(2)}) copy-start(bf16[1,128,1024]{2,1,0:T(8,128)(2,1)} %param.27) | copy-start | bytes 786436
  320.2 26.3 %copy-start.8 = (f32[128,1024]{1,0:T(8,128)S(1)}, f32[128,1024]{1,0:T(8,128)}, u32[]{:S(2)}) copy-start(f32[128,1024]{1,0:T(8,128)} %get-tuple-element.198) | copy-start | bytes 1572868
  320.2 26.3 %copy-start.23 = (f32[128]{0:T(128)S(1)}, f32[128]{0:T(128)}, u32[]{:S(2)}) copy-start(f32[128]{0:T(128)} %copy-done.22) | copy-start | bytes 1540
  320.2 26.3 %copy-start.25 = (f32[128]{0:T(128)S(1)}, f32[128]{0:T(128)}, u32[]{:S(2)}) copy-start(f32[128]{0:T(128)} %add_rsqrt_fusion) | copy-start | bytes 1540
  330.1 9.5 %collective-permute-start.6 = (bf16[128,1024]{1,0:T(8,128)(2,1)}, bf16[128,1024]{1,0:T(8,128)(2,1)}, u32[]{:S(2)}, u32[]{:S(2)}) collective-permute-start(bf16[128,1024]{1,0:T(8,128)(2,1)} %get-tuple-element.178), channel_id=1, source_target_pairs={{0,2},{1,3},{2,0},{3,1},{4,6},{5,7},{6,4},{7,5},{8,10},{9,11},{10,... | collective-permute-start | bytes 786440 | tf_op jit(solution)/shard_map/ppermute | solution.py:982
  331.6 13.8 %collective-permute-start.8 = (bf16[128,1024]{1,0:T(8,128)(2,1)}, bf16[128,1024]{1,0:T(8,128)(2,1)}, u32[]{:S(2)}, u32[]{:S(2)}) collective-permute-start(bf16[128,1024]{1,0:T(8,128)(2,1)} %get-tuple-element.179), channel_id=1, source_target_pairs={{0,6},{1,7},{2,4},{3,5},{4,2},{5,3},{6,0},{7,1},{8,14},{9,15},{10,... | collective-permute-start | bytes 786440 | tf_op jit(solution)/shard_map/ppermute | solution.py:982
  333.1 13.5 %collective-permute-start.7 = (bf16[128,1024]{1,0:T(8,128)(2,1)S(1)}, bf16[128,1024]{1,0:T(8,128)(2,1)}, u32[]{:S(2)}, u32[]{:S(2)}) collective-permute-start(bf16[128,1024]{1,0:T(8,128)(2,1)S(1)} %get-tuple-element.180), channel_id=1, source_target_pairs={{0,4},{1,5},{2,6},{3,7},{4,0},{5,1},{6,2},{7,3},{8,12},{9,13},{10,... | collective-permute-start | bytes 786440 | tf_op jit(solution)/shard_map/ppermute | solution.py:982
  351.6 14.2 %copy-start.1 = (bf16[1024,1024]{1,0:T(8,128)(2,1)S(1)}, bf16[1024,1024]{1,0:T(8,128)(2,1)}, u32[]{:S(2)}) copy-start(bf16[1024,1024]{1,0:T(8,128)(2,1)} %param.19) | copy-start | bytes 6291460
  (3 other events, 2.7 us)
Sparse Core Ops, SparseCore 0:
  51.5 89.6 all-gather.4
  142.8 80.3 all-gather.6
where the time goes:
time: 380 us; the launch traced here: 373 us
  Pallas kernels  132 us (35%)
  waiting for transfers between devices  84.3 us (22%)
  blocking collectives  47.5 us (12%)
  starting transfers between devices  33.9 us (9%)
  local copies, waits for them, and re-layouts  29.5 us (8%)
  other arithmetic  19.2 us (5%)
  between operations  15 us (4%)
  matrix products  11.5 us (3%)
    pallas_call x4, Pallas kernels, expert_weight_grads(): pl.pallas_call(kernel, grid_spec=pltpu.PrefetchScalarGridSpec(num_scalar_...  65 us
    all_to_all x2, blocking collectives, across_chips(): lax.all_to_all(blocks, 'expert', 0, 0, axis_index_groups=groups, tiled=True)  37.3 us
    ppermute x6, waiting for transfers between devices, permute(): return lax.ppermute(block, axis, [(i, i ^ shift) for i in range(count)])  30.8 us
    all_to_all x4, waiting for transfers between devices, across_chips(): lax.all_to_all(blocks, 'expert', 0, 0, axis_index_groups=groups, tiled=True)  28.6 us
    pallas_call x1, Pallas kernels, near_experts(): pl.pallas_call(kernel, grid_spec=pltpu.PrefetchScalarGridSpec(num_scalar_...  20.4 us
    all_to_all x4, starting transfers between devices, across_chips(): lax.all_to_all(blocks, 'expert', 0, 0, axis_index_groups=groups, tiled=True)  18.6 us
    pallas_call x1, Pallas kernels, attend_heads(): pl.pallas_call(kernel, grid_spec=pltpu.PrefetchScalarGridSpec(num_scalar_...  17.1 us
    pallas_call x1, Pallas kernels, attend_back(): pl.pallas_call(kernel, grid_spec=pltpu.PrefetchScalarGridSpec(num_scalar_...  15.3 us
  transfers between devices with their start and end apart: 23, of which 16 were waited for; matrix products, arithmetic and copies ran while one was open for 13% of the time, Pallas kernels for 32%

commit v1 on v0

--- a/solution.py
+++ b/solution.py
@@ -554,7 +554,7 @@
 
 
 def expert_weight_grads(ids, sums, x_near, x_twin, g_near, g_twin, mask_all, slot_all, router_t, weights, copies):
-    unused, chips, group_len, width = x_near.shape
+    chips, unused, group_len, width = x_near.shape
     held, unused, inner = weights[0].shape
     groups = 2 * chips
     slots = groups * MOST
@@ -569,8 +569,8 @@
         @pl.when(e == 0)
         def _():
             expert_gather(
-                lambda g: (xn if g < chips else xt)[0, g % chips],
-                lambda g: (gn if g < chips else gt)[0, g % chips],
+                lambda g: (xn if g < chips else xt)[g % chips, 0],
+                lambda g: (gn if g < chips else gt)[g % chips, 0],
                 lambda g: mr[g],
                 lambda g: sr[g],
                 rt[...], mine * held, x_scr, g_scr, gate_scr, None, groups,
@@ -594,7 +594,7 @@
             out[0] = part if before is None else before[0] + part
 
     some = lambda *shape: pl.BlockSpec((groups,) + shape, lambda e, m: (m[2], 0, 0))
-    rows = pl.BlockSpec((1, chips, group_len, width), lambda e, m: (m[2], 0, 0, 0))
+    rows = pl.BlockSpec((chips, 1, group_len, width), lambda e, m: (0, m[2], 0, 0))
     weight = lambda *shape: pl.BlockSpec((1,) + shape, lambda e, m: (e, 0, 0))
     whole = lambda *shape: pl.BlockSpec(shape, lambda e, m: (0,) * len(shape))
     outs = [(held, wide, inner), (held, wide, inner), (held, narrow, width)]
@@ -987,6 +987,16 @@
     return near, swap_cores(near, devices)
 
 
+def far_rows_of(block, copies):
+    return jnp.stack([permute(block, s, "dp", copies) for s in range(1, copies)])
+
+
+def spread_far(rows, devices):
+    return jnp.stack(
+        [rows] + [permute(rows, 2 * c, "expert", devices) for c in range(1, devices // 2)]
+    )
+
+
 def merge_cores(near, twin, devices):
     partner = swap_cores(twin, devices)
     return (near.astype(jnp.float32) + partner.astype(jnp.float32)).astype(jnp.bfloat16)
@@ -1087,17 +1097,18 @@
     )
     tail_rows = EXPERTS * group_len // width
     mask_tail = jnp.swapaxes(mask_own.astype(bf16), 0, 1).reshape(tail_rows, width)
-    grad_pay, near_pay = lax.optimization_barrier((with_tail(out_grad[0], mask_tail), near_pay))
+    grad_pay = with_tail(out_grad[0], mask_tail)
+    g_far_own = far_rows_of(grad_pay, copies)
+    grad_pay, near_pay = lax.optimization_barrier((grad_pay, near_pay))
     g_near, g_twin = spread_row(grad_pay, devices)
 
-    def tables(near, twin, axis):
-        tails = [side[..., group_len : group_len + tail_rows, :] for side in (near, twin)]
-        return slot_tables(
-            jnp.concatenate(tails, axis=axis).reshape(-1, EXPERTS, group_len), me * held, held
-        )
-
-    mask_row, slot_row = tables(g_near, g_twin, 0)
-    g_near_all = lax.all_gather(g_near, "dp", axis=0)
+    def tables(tails):
+        return slot_tables(tails.reshape(-1, EXPERTS, group_len), me * held, held)
+
+    tail_span = slice(group_len, group_len + tail_rows)
+    mask_row, slot_row = tables(
+        jnp.concatenate([g_near[:, tail_span], g_twin[:, tail_span]], axis=0)
+    )
     router_t = jnp.swapaxes(w_router, 0, 1)
 
     head_weights = jnp.concatenate(
@@ -1125,7 +1136,9 @@
         jnp.dot(moe_rows, w_router, preferred_element_type=jnp.float32), mask_own
     )
     x_near, x_twin = spread_row(moe_rows, devices)
-    x_near_all = lax.all_gather(x_near, "dp", axis=0)
+    x_far_own = far_rows_of(moe_rows, copies)
+    x_near, g_far_own = lax.optimization_barrier((x_near, g_far_own))
+    g_far = spread_far(g_far_own, devices)
 
     d_near, d_twin, y_near, y_twin = near_experts(
         me, x_near, x_twin, g_near, g_twin, mask_row, slot_row, router_t, w_gate, w_up, w_down
@@ -1141,7 +1154,7 @@
 
     crossed = across_chips(d_merged, devices)
     x_mine, g_mine, d_merged = lax.optimization_barrier(
-        ((x_near[None], x_twin[None]), (g_near[None], g_twin[None]), d_merged)
+        ((x_near[:, None], x_twin[:, None]), (g_near[:, None], g_twin[:, None]), d_merged)
     )
     sums = expert_row(0, None, x_mine, g_mine, mask_row, slot_row)
     crossed, sums = lax.optimization_barrier((crossed, sums))
@@ -1162,6 +1175,8 @@
     branch_near, branch_twin = spread_row(
         with_tail(dbranch, jnp.swapaxes(dlogits, 0, 1).reshape(tail_rows, width)), devices
     )
+    branch_near, x_far_own = lax.optimization_barrier((branch_near, x_far_own))
+    x_far = spread_far(x_far_own, devices)
     dlogits_row = jnp.concatenate([branch_near[:, group_len:], branch_twin[:, group_len:]], axis=0)
     dlogits_row = dlogits_row[:, :tail_rows].reshape(devices, EXPERTS, group_len)
 
@@ -1210,17 +1225,18 @@
     gain_parts = pack_gains(jnp.stack([attn_gain_part, moe_gain_part]), head_cols)
     column = exchange(broadcast(jnp.concatenate([shared_sum, gain_parts], axis=0), copies), "dp")
 
-    g_near_all, x_near_all, y_near, y_twin, gain_parts = lax.optimization_barrier(
-        (g_near_all, x_near_all, y_near, y_twin, gain_parts)
-    )
-    g_rows = (g_near_all, swap_cores(g_near_all, devices))
-    x_rows = (x_near_all, swap_cores(x_near_all, devices))
-    masks, slots = tables(*g_rows, 1)
+    g_far, x_far, y_near, y_twin, gain_parts = lax.optimization_barrier(
+        (g_far, x_far, y_near, y_twin, gain_parts)
+    )
+    g_rows, x_rows = (g_far, swap_cores(g_far, devices)), (x_far, swap_cores(x_far, devices))
+    masks, slots = tables(
+        jnp.transpose(jnp.stack([rows_of[:, :, tail_span] for rows_of in g_rows]), (2, 0, 1, 3, 4))
+    )
     y_merged = merge_cores(y_near, y_twin, devices)
     y_sum = permute_sum(y_merged, me >> 1, 2, "expert", devices)
 
     def far_row(step, sums):
-        return expert_row((me_z + step) % copies, sums, x_rows, g_rows, masks, slots)
+        return expert_row(step - 1, sums, x_rows, g_rows, masks, slots)
 
     sums = far_row(1, sums)
     column, sums = lax.optimization_barrier((column, sums))

time: 380 us -> 465 us (1.22)
  waiting for transfers between devices: 84.3 us -> 142 us
  starting transfers between devices: 33.9 us -> 50.6 us
  between operations: 15 us -> 1.73 us
  other arithmetic: 19.2 us -> 31.8 us
  local copies, waits for them, and re-layouts: 29.5 us -> 41.6 us
    ppermute x6 -> x18, waiting for transfers between devices: 30.8 us -> 103 us  [permute(): return lax.ppermute(block, axis, [(i, i ^ shift) for i in range(count)])]
    ppermute x6 -> x18, starting transfers between devices: 7.03 us -> 22.8 us  [permute(): return lax.ppermute(block, axis, [(i, i ^ shift) for i in range(count)])]
    another operation x0 -> x4, other arithmetic: none -> 8.57 us  [the longest x2 5.43 us: spread_far(): jnp.stack([rows] + [permute(rows, 2 * c, 'expert', devices) for c in rang...]
    slice x5, local copies, waits for them, and re-layouts: 1.96 us -> 8.84 us  [token_grad(): dlin_back[:, :, start:start + count].reshape(group_len, devices * count)]
    all_to_all x2, waiting for transfers between devices: 10.3 us -> 4.05 us  [exchange(): return lax.all_to_all(blocks, axis, 0, 0, tiled=True)]
  transfers between devices with their start and end apart: 23 -> 33, of which waited for: 16 -> 20; matrix products, arithmetic and copies ran while one was open for 13% -> 10% of each run, Pallas kernels for 32% -> 21%
where the time goes in v1:
time: 465 us; the launch traced here: 457 us
  waiting for transfers between devices  142 us (31%)
  Pallas kernels  131 us (28%)
  starting transfers between devices  50.6 us (11%)
  blocking collectives  47.2 us (10%)
  local copies, waits for them, and re-layouts  41.6 us (9%)
  other arithmetic  31.8 us (7%)
  matrix products  10.7 us (2%)
    ppermute x18, waiting for transfers between devices, permute(): return lax.ppermute(block, axis, [(i, i ^ shift) for i in range(count)])  103 us
    pallas_call x4, Pallas kernels, expert_weight_grads(): pl.pallas_call(kernel, grid_spec=pltpu.PrefetchScalarGridSpec(num_scalar_...  64.6 us
    all_to_all x2, blocking collectives, across_chips(): lax.all_to_all(blocks, 'expert', 0, 0, axis_index_groups=groups, tiled=True)  37 us
    all_to_all x4, waiting for transfers between devices, across_chips(): lax.all_to_all(blocks, 'expert', 0, 0, axis_index_groups=groups, tiled=True)  26.1 us
    ppermute x18, starting transfers between devices, permute(): return lax.ppermute(block, axis, [(i, i ^ shift) for i in range(count)])  22.8 us
    pallas_call x1, Pallas kernels, near_experts(): pl.pallas_call(kernel, grid_spec=pltpu.PrefetchScalarGridSpec(num_scalar_...  20.4 us
    all_to_all x4, starting transfers between devices, across_chips(): lax.all_to_all(blocks, 'expert', 0, 0, axis_index_groups=groups, tiled=True)  18.2 us
    pallas_call x1, Pallas kernels, attend_heads(): pl.pallas_call(kernel, grid_spec=pltpu.PrefetchScalarGridSpec(num_scalar_...  16.7 us
  transfers between devices with their start and end apart: 33, of which 20 were waited for; matrix products, arithmetic and copies ran while one was open for 10% of the time, Pallas kernels for 21%

profile of v1, /device:TPU:0, one launch (start us, length us, event | category | flops | bytes accessed | tf_op | source)
XLA Modules:
  0.0 457.2 jit_solution(12750064026434606171)
XLA Ops:
  3.7 5.2 %all-to-all-start = ((bf16[4,144,1024]{2,1,0:T(8,128)(2,1)}), bf16[4,144,1024]{2,1,0:T(8,128)(2,1)S(1)}, u32[]{:S(2)}, u32[]{:S(2)}) async-start(bf16[4,144,1024]{2,1,0:T(8,128)(2,1)} %broadcast_in_dim.41), calls=%async_computation | async-start | bytes 2359296 | tf_op jit(solution)/shard_map/all_to_all | solution.py:978
  9.6 14.2 %all-to-all-done.near_ref = bf16[4,144,1024]{2,1,0:T(8,128)(2,1)S(1)} async-done(((bf16[4,144,1024]{2,1,0:T(8,128)(2,1)}), bf16[4,144,1024]{2,1,0:T(8,128)(2,1)S(1)}, u32[]{:S(2)}, u32[]{:S(2)}) %all-to-all-start) | async-done | bytes 1179680 | tf_op jit(solution)/shard_map/all_to_all | solution.py:978
  23.9 2.3 broadcast_in_dim.43
  26.2 4.3 all-to-all-start.1
  36.3 8.8 %all-to-all-done.1.gn = bf16[4,144,1024]{2,1,0:T(8,128)(2,1)} async-done(((bf16[4,144,1024]{2,1,0:T(8,128)(2,1)}), bf16[4,144,1024]{2,1,0:T(8,128)(2,1)}, u32[]{:S(2)}, u32[]{:S(2)}) %all-to-all-start.1) | async-done | bytes 1179680 | tf_op jit(solution)/shard_map/all_to_all | solution.py:978
  46.4 2.6 copy.108.twin_ref
  50.4 16.7 %attend_heads.1 = (bf16[8,128,1024]{2,1,0:T(8,128)(2,1)}, bf16[1024,256]{1,0:T(8,128)(2,1)}, f32[1024,128]{1,0:T(8,128)}, f32[1024,128]{1,0:T(8,128)}, bf16[8,12...) custom-call(s32[1]{0:T(128)} %bitcast.1.me_ref, bf16[4,144,1024]{2,1,0:T(8,128)(2,1)} %copy-done.8, ...), custom_call_target="tpu_custom_call" | custom-call | flops 2147483648 | bytes 8388608 | tf_op jit(solution)/shard_map/attend_heads/pallas_call | solution.py:802
  67.0 10.2 %all_to_all.45 = bf16[8,128,128]{2,1,0:T(8,128)(2,1)S(1)} all-to-all(bf16[8,128,128]{2,1,0:T(8,128)(2,1)} %get-tuple-element.72), channel_id=1, replica_groups=mesh['dp'=4,'expert'=8] {'expert'}, dimensions={0} | all-to-all | bytes 524288 | tf_op jit(solution)/shard_map/all_to_all | solution.py:1038
  78.4 17.4 %all_to_all.46.xn = bf16[4,128,1024]{2,1,0:T(8,128)(2,1)} all-to-all(bf16[4,128,1024]{2,1,0:T(8,128)(2,1)S(1)} %broadcast_in_dim.44), channel_id=1, replica_groups={{0,2,4,6},{1,3,5,7},{8,10,12,14},{9,11,13,15},{16,18,20,22},{17,19,21,2..., dimensions={0} | all-to-all | bytes 2097152 | tf_op jit(solution)/shard_map/all_to_all | solution.py:978
  95.8 3.7 collective-permute-start.4
  100.2 7.5 %collective-permute-done.4 = bf16[144,1024]{1,0:T(8,128)(2,1)} collective-permute-done((bf16[144,1024]{1,0:T(8,128)(2,1)S(1)}, bf16[144,1024]{1,0:T(8,128)(2,1)}, u32[]{:S(2)}, u32[]{:S(2)}) %collective-permute-start.4) | collective-permute-done | bytes 294944 | tf_op jit(solution)/shard_map/ppermute | solution.py:982
  107.7 17.6 %collective-permute-done.3 = bf16[144,1024]{1,0:T(8,128)(2,1)} collective-permute-done((bf16[144,1024]{1,0:T(8,128)(2,1)S(1)}, bf16[144,1024]{1,0:T(8,128)(2,1)}, u32[]{:S(2)}, u32[]{:S(2)}) %collective-permute-start.3) | collective-permute-done | bytes 294944 | tf_op jit(solution)/shard_map/ppermute | solution.py:982
  125.4 2.1 pad_maximum_fusion.2
  130.1 20.4 %near_experts.1 = (bf16[4,144,1024]{2,1,0:T(8,128)(2,1)}, bf16[4,144,1024]{2,1,0:T(8,128)(2,1)}, bf16[4,128,1024]{2,1,0:T(8,128)(2,1)}, bf16[4,128,1024]{2,1,0:T(8,128)(2,1)}) custom-call(s32[1]{0:T(128)} %bitcast.1.me_ref, bf16[4,128,1024]{2,1,0:T(8,128)(2,1)} %all_to_all.46.xn, bf16[4,128,1024]{2,1,0:T(8,128)(2,1)} %collective-permute-done.8.xt, ...), custom_call_target="tpu_custom_call" | custom-call | flops 11274289152 | bytes 16777216 | tf_op jit(solution)/shard_map/near_experts/pallas_call | solution.py:512
  151.0 2.6 collective-permute-done.9
  153.6 3.1 add_convert_fusion
  156.8 4.8 %all-to-all-start.4 = ((bf16[4,144,1024]{2,1,0:T(8,128)(2,1)}), bf16[4,144,1024]{2,1,0:T(8,128)(2,1)}, u32[]{:S(2)}, u32[]{:S(2)}) async-start(bf16[4,144,1024]{2,1,0:T(8,128)(2,1)} %add_convert_fusion), calls=%async_computation.4 | async-start | bytes 2359296 | tf_op jit(solution)/shard_map/all_to_all | solution.py:978
  161.9 15.7 %expert_weight_grads.4 = (f32[4,256,512]{2,1,0:T(8,128)}, f32[4,256,512]{2,1,0:T(8,128)}, f32[4,128,1024]{2,1,0:T(8,128)}) custom-call(s32[3]{0:T(128)} %pad_add_fusion.ids_ref, bf16[4,1,128,1024]{3,2,1,0:T(8,128)(2,1)} %bitcast.34.xn, bf16[4,1,128,1024]{3,2,1,0:T(8,128)(2,1)} %bitcast.31.xt, bf16[4,1,144,1024]{3,2,1,0:T(8,128)(2,1)} %bitcast.35.gn, ...), custom_call_target="tpu_custom_call" | custom-call | flops 6442450944 | bytes 16777216 | tf_op jit(solution)/shard_map/expert_weight_grads/pallas_call | solution.py:601
  181.2 19.5 %all_to_all.47.near_ref = bf16[4,144,1024]{2,1,0:T(8,128)(2,1)S(1)} all-to-all(bf16[4,144,1024]{2,1,0:T(8,128)(2,1)S(1)} %broadcast_in_dim.53), channel_id=1, replica_groups={{0,2,4,6},{1,3,5,7},{8,10,12,14},{9,11,13,15},{16,18,20,22},{17,19,21,2..., dimensions={0} | all-to-all | bytes 2359296 | tf_op jit(solution)/shard_map/all_to_all | solution.py:978
  201.8 2.5 collective-permute-start.12
  206.2 6.7 %collective-permute-done.12 = bf16[128,1024]{1,0:T(8,128)(2,1)S(1)} collective-permute-done((bf16[128,1024]{1,0:T(8,128)(2,1)S(1)}, bf16[128,1024]{1,0:T(8,128)(2,1)S(1)}, u32[]{:S(2)}, u32[]{:S(2)}) %collective-permute-start.12) | collective-permute-done | bytes 262176 | tf_op jit(solution)/shard_map/ppermute | solution.py:982
  214.4 11.6 %collective-permute-done.11 = bf16[128,1024]{1,0:T(8,128)(2,1)S(1)} collective-permute-done((bf16[128,1024]{1,0:T(8,128)(2,1)S(1)}, bf16[128,1024]{1,0:T(8,128)(2,1)S(1)}, u32[]{:S(2)}, u32[]{:S(2)}) %collective-permute-start.11) | collective-permute-done | bytes 262176 | tf_op jit(solution)/shard_map/ppermute | solution.py:982
  232.9 15.3 %attend_back.1 = (bf16[8,128,256]{2,1,0:T(8,128)(2,1)}, bf16[4,128,256]{2,1,0:T(8,128)(2,1)}) custom-call(s32[1]{0:T(128)} %bitcast.1.me_ref, bf16[4,144,1024]{2,1,0:T(8,128)(2,1)} %copy-done.20, bf16[4,144,1024]{2,1,0:T(8,128)(2,1)} %copy-done.30, bf16[128,1024]{1,0:T(8,128)(2,1)} %constant_dynamic-slice_fusion.1.w_ref, ...), custom_call_target="tpu_custom_call" | custom-call | flops 1610612736 | bytes 8388608 | tf_op jit(solution)/shard_map/attend_back/pallas_call | solution.py:929
  248.2 4.3 all-to-all-start.6
  252.5 2.2 pad_maximum_fusion.gn
  254.7 11.9 %collective-permute-done.15 = bf16[3,128,1024]{2,1,0:T(8,128)(2,1)} collective-permute-done((bf16[3,128,1024]{2,1,0:T(8,128)(2,1)}, bf16[3,128,1024]{2,1,0:T(8,128)(2,1)}, u32[]{:S(2)}, u32[]{:S(2)}) %collective-permute-start.15) | collective-permute-done | bytes 786464 | tf_op jit(solution)/shard_map/ppermute | solution.py:982
  266.6 10.2 %collective-permute-done.14 = bf16[3,128,1024]{2,1,0:T(8,128)(2,1)} collective-permute-done((bf16[3,128,1024]{2,1,0:T(8,128)(2,1)}, bf16[3,128,1024]{2,1,0:T(8,128)(2,1)}, u32[]{:S(2)}, u32[]{:S(2)}) %collective-permute-start.14) | collective-permute-done | bytes 786464 | tf_op jit(solution)/shard_map/ppermute | solution.py:982
  276.8 5.7 %collective-permute-done.13 = bf16[3,128,1024]{2,1,0:T(8,128)(2,1)} collective-permute-done((bf16[3,128,1024]{2,1,0:T(8,128)(2,1)}, bf16[3,128,1024]{2,1,0:T(8,128)(2,1)}, u32[]{:S(2)}, u32[]{:S(2)}) %collective-permute-start.13) | collective-permute-done | bytes 786464 | tf_op jit(solution)/shard_map/ppermute | solution.py:982
  282.6 3.2 pad_maximum_fusion.1.xn
  296.3 2.6 fusion.52
  309.3 2.5 fusion.1
  314.9 2.1 collective-permute-start.22
  317.1 7.8 %collective-permute-done.21 = bf16[400,256]{1,0:T(8,128)(2,1)} collective-permute-done((bf16[400,256]{1,0:T(8,128)(2,1)}, bf16[400,256]{1,0:T(8,128)(2,1)}, u32[]{:S(2)}, u32[]{:S(2)}) %collective-permute-start.21) | collective-permute-done | bytes 204832 | tf_op jit(solution)/shard_map/ppermute | solution.py:982
  325.7 9.6 %collective-permute-done.22 = bf16[400,256]{1,0:T(8,128)(2,1)} collective-permute-done((bf16[400,256]{1,0:T(8,128)(2,1)}, bf16[400,256]{1,0:T(8,128)(2,1)}, u32[]{:S(2)}, u32[]{:S(2)}) %collective-permute-start.22) | collective-permute-done | bytes 204832 | tf_op jit(solution)/shard_map/ppermute | solution.py:982
  338.2 4.2 all-to-all-start.7
  344.6 16.3 %expert_weight_grads.5 = (f32[4,256,512]{2,1,0:T(8,128)}, f32[4,256,512]{2,1,0:T(8,128)}, f32[4,128,1024]{2,1,0:T(8,128)}) custom-call(s32[3]{0:T(128)} %pad_add_fusion.ids_ref, bf16[4,3,128,1024]{3,2,1,0:T(8,128)(2,1)} %pad_maximum_fusion.1.xn, ...), custom_call_target="tpu_custom_call", output_to_operand_aliasing={{0}: (11, {}), {1}: (12, {}), {2}: (13, {})} | custom-call | flops 6442450944 | bytes 16777216 | tf_op jit(solution)/shard_map/expert_weight_grads/pallas_call | solution.py:601
  360.9 2.4 all-to-all-done.7
  369.0 3.9 all-to-all-start.8
  373.5 16.3 %expert_weight_grads.6 = (f32[4,256,512]{2,1,0:T(8,128)}, f32[4,256,512]{2,1,0:T(8,128)}, f32[4,128,1024]{2,1,0:T(8,128)}) custom-call(s32[3]{0:T(128)} %get-tuple-element.203.ids_ref, bf16[4,3,128,1024]{3,2,1,0:T(8,128)(2,1)} %pad_maximum_fusion.1.xn, ...), custom_call_target="tpu_custom_call", output_to_operand_aliasing={{0}: (11, {}), {1}: (12, {}), {2}: (13, {})} | custom-call | flops 6442450944 | bytes 16777216 | tf_op jit(solution)/shard_map/expert_weight_grads/pallas_call | solution.py:601
  389.8 16.3 %expert_weight_grads.7 = (f32[4,256,512]{2,1,0:T(8,128)}, f32[4,256,512]{2,1,0:T(8,128)}, f32[4,128,1024]{2,1,0:T(8,128)}) custom-call(s32[3]{0:T(128)} %get-tuple-element.202.ids_ref, bf16[4,3,128,1024]{3,2,1,0:T(8,128)(2,1)} %pad_maximum_fusion.1.xn, ...), custom_call_target="tpu_custom_call", output_to_operand_aliasing={{0}: (11, {}), {1}: (12, {}), {2}: (13, {})} | custom-call | flops 6442450944 | bytes 16777216 | tf_op jit(solution)/shard_map/expert_weight_grads/pallas_call | solution.py:601
  406.1 3.1 all-to-all-done.8.near_ref
  409.8 6.8 %collective-permute-done.17 = bf16[4,128,1024]{2,1,0:T(8,128)(2,1)} collective-permute-done((bf16[4,128,1024]{2,1,0:T(8,128)(2,1)}, bf16[4,128,1024]{2,1,0:T(8,128)(2,1)}, u32[]{:S(2)}, u32[]{:S(2)}) %collective-permute-start.17) | collective-permute-done | bytes 1048608 | tf_op jit(solution)/shard_map/ppermute | solution.py:973
  416.6 1.9 add_convert_fusion.1
  423.9 6.0 %collective-permute-done.18 = bf16[128,1024]{1,0:T(8,128)(2,1)} collective-permute-done((bf16[128,1024]{1,0:T(8,128)(2,1)}, bf16[128,1024]{1,0:T(8,128)(2,1)}, u32[]{:S(2)}, u32[]{:S(2)}) %collective-permute-start.18) | collective-permute-done | bytes 262176 | tf_op jit(solution)/shard_map/ppermute | solution.py:982
  429.9 5.8 %collective-permute-done.20 = bf16[128,1024]{1,0:T(8,128)(2,1)} collective-permute-done((bf16[128,1024]{1,0:T(8,128)(2,1)}, bf16[128,1024]{1,0:T(8,128)(2,1)}, u32[]{:S(2)}, u32[]{:S(2)}) %collective-permute-start.20) | collective-permute-done | bytes 262176 | tf_op jit(solution)/shard_map/ppermute | solution.py:982
  437.1 3.0 fusion.16
  442.7 6.6 %assemble_rows.1 = f32[1024,1024]{1,0:T(8,128)} custom-call(s32[1]{0:T(128)} %bitcast.9.core_ref, bf16[4,1568,256]{2,1,0:T(8,128)(2,1)} %copy-done.3, bf16[4,1568,256]{2,1,0:T(8,128)(2,1)} %collective-permute-done.26.twin_ref), custom_call_target="tpu_custom_call" | custom-call | tf_op jit(solution)/shard_map/assemble_rows/pallas_call | solution.py:685
  449.4 7.6 %assemble_heads.1 = (f32[1024,1024]{1,0:T(8,128)}, f32[1024,512]{1,0:T(8,128)}, f32[1024,512]{1,0:T(8,128)}) custom-call(s32[1]{0:T(128)} %bitcast.9.core_ref, bf16[4,1568,256]{2,1,0:T(8,128)(2,1)} %copy-done.3, bf16[4,1568,256]{2,1,0:T(8,128)(2,1)} %collective-permute-done.26.twin_ref), custom_call_target="tpu_custom_call" | custom-call | tf_op jit(solution)/shard_map/assemble_heads/pallas_call | solution.py:659
  (222 shorter events, 77.9 us)
Async XLA Ops:
  0.6 76.8 %copy-start = (bf16[1024,1024]{1,0:T(8,128)(2,1)S(1)}, bf16[1024,1024]{1,0:T(8,128)(2,1)}, u32[]{:S(2)}) copy-start(bf16[1024,1024]{1,0:T(8,128)(2,1)} %param.19) | copy-start | bytes 6291460
  3.7 20.2 %all-to-all-start = ((bf16[4,144,1024]{2,1,0:T(8,128)(2,1)}), bf16[4,144,1024]{2,1,0:T(8,128)(2,1)S(1)}, u32[]{:S(2)}, u32[]{:S(2)}) async-start(bf16[4,144,1024]{2,1,0:T(8,128)(2,1)} %broadcast_in_dim.41), calls=%async_computation | async-start | bytes 2359296 | tf_op jit(solution)/shard_map/all_to_all | solution.py:978
  26.2 18.9 %all-to-all-start.1 = ((bf16[4,144,1024]{2,1,0:T(8,128)(2,1)}), bf16[4,144,1024]{2,1,0:T(8,128)(2,1)}, u32[]{:S(2)}, u32[]{:S(2)}) async-start(bf16[4,144,1024]{2,1,0:T(8,128)(2,1)} %broadcast_in_dim.43), calls=%async_computation.1 | async-start | bytes 2359296 | tf_op jit(solution)/shard_map/all_to_all | solution.py:978
  32.4 14.0 %collective-permute-start = (bf16[4,144,1024]{2,0,1:T(4,128)(2,1)}, bf16[4,144,1024]{2,0,1:T(4,128)(2,1)}, u32[]{:S(2)}, u32[]{:S(2)}) collective-permute-start(bf16[4,144,1024]{2,0,1:T(4,128)(2,1)} %copy.105), channel_id=1, source_target_pairs={{0,1},{1,0},{2,3},{3,2},{4,5},{5,4},{6,7},{7,6},{8,9},{9,8},{10,11... | collective-permute-start | bytes 3538952 | tf_op jit(solution)/shard_map/ppermute | solution.py:973
  45.1 21.9 %collective-permute-start.1 = (bf16[4,144,1024]{2,1,0:T(8,128)(2,1)}, bf16[4,144,1024]{2,1,0:T(8,128)(2,1)}, u32[]{:S(2)}, u32[]{:S(2)}) collective-permute-start(bf16[4,144,1024]{2,1,0:T(8,128)(2,1)} %all-to-all-done.1.gn), channel_id=1, source_target_pairs={{0,1},{1,0},{2,3},{3,2},{4,5},{5,4},{6,7},{7,6},{8,9},{9,8},{10,11... | collective-permute-start | bytes 3538952 | tf_op jit(solution)/shard_map/ppermute | solution.py:973
  50.3 27.1 %copy-start.5 = (bf16[1,128,1024]{2,1,0:T(8,128)(2,1)S(1)}, bf16[1,128,1024]{2,1,0:T(8,128)(2,1)}, u32[]{:S(2)}) copy-start(bf16[1,128,1024]{2,1,0:T(8,128)(2,1)} %param.14) | copy-start | bytes 786436
  78.0 101.6 %copy-start.4 = (f32[128,1024]{1,0:T(8,128)}, f32[128,1024]{1,0:T(8,128)S(1)}, u32[]{:S(2)}) copy-start(f32[128,1024]{1,0:T(8,128)S(1)} %get-tuple-element.197) | copy-start | bytes 1572868
  78.1 101.6 %copy-start.31 = (f32[128]{0:T(128)}, f32[128]{0:T(128)S(1)}, u32[]{:S(2)}) copy-start(f32[128]{0:T(128)S(1)} %add_rsqrt_fusion.1) | copy-start | bytes 1540
  78.2 83.4 %copy-start.13 = (bf16[128,1024]{1,0:T(8,128)(2,1)}, bf16[128,1024]{1,0:T(8,128)(2,1)S(1)}, u32[]{:S(2)}) copy-start(bf16[128,1024]{1,0:T(8,128)(2,1)S(1)} %multiply_convert_fusion.1) | copy-start | bytes 786436
  95.8 34.3 %collective-permute-start.8 = (bf16[4,128,1024]{2,1,0:T(8,128)(2,1)}, bf16[4,128,1024]{2,1,0:T(8,128)(2,1)}, u32[]{:S(2)}, u32[]{:S(2)}) collective-permute-start(bf16[4,128,1024]{2,1,0:T(8,128)(2,1)} %all_to_all.46.xn), channel_id=1, source_target_pairs={{0,1},{1,0},{2,3},{3,2},{4,5},{5,4},{6,7},{7,6},{8,9},{9,8},{10,11... | collective-permute-start | bytes 3145736 | tf_op jit(solution)/shard_map/ppermute | solution.py:973
  95.8 11.9 %collective-permute-start.4 = (bf16[144,1024]{1,0:T(8,128)(2,1)S(1)}, bf16[144,1024]{1,0:T(8,128)(2,1)}, u32[]{:S(2)}, u32[]{:S(2)}) collective-permute-start(bf16[144,1024]{1,0:T(8,128)(2,1)S(1)} %copy-done.21), channel_id=1, source_target_pairs={{0,24},{8,16},{16,8},{24,0},{1,25},{9,17},{17,9},{25,1},{2,26},{10... | collective-permute-start | bytes 884744 | tf_op jit(solution)/shard_map/ppermute | solution.py:982
  99.5 25.9 %collective-permute-start.3 = (bf16[144,1024]{1,0:T(8,128)(2,1)S(1)}, bf16[144,1024]{1,0:T(8,128)(2,1)}, u32[]{:S(2)}, u32[]{:S(2)}) collective-permute-start(bf16[144,1024]{1,0:T(8,128)(2,1)S(1)} %copy-done.21), channel_id=1, source_target_pairs={{0,16},{8,24},{16,0},{24,8},{1,17},{9,25},{17,1},{25,9},{2,18},{10... | collective-permute-start | bytes 884744 | tf_op jit(solution)/shard_map/ppermute | solution.py:982
  99.5 25.9 %collective-permute-start.2 = (bf16[144,1024]{1,0:T(8,128)(2,1)S(1)}, bf16[144,1024]{1,0:T(8,128)(2,1)}, u32[]{:S(2)}, u32[]{:S(2)}) collective-permute-start(bf16[144,1024]{1,0:T(8,128)(2,1)S(1)} %copy-done.21), channel_id=1, source_target_pairs={{0,8},{8,0},{16,24},{24,16},{1,9},{9,1},{17,25},{25,17},{2,10},{10... | collective-permute-start | bytes 884744 | tf_op jit(solution)/shard_map/ppermute | solution.py:982
  150.4 3.2 collective-permute-start.9
  156.8 20.8 %all-to-all-start.4 = ((bf16[4,144,1024]{2,1,0:T(8,128)(2,1)}), bf16[4,144,1024]{2,1,0:T(8,128)(2,1)}, u32[]{:S(2)}, u32[]{:S(2)}) async-start(bf16[4,144,1024]{2,1,0:T(8,128)(2,1)} %add_convert_fusion), calls=%async_computation.4 | async-start | bytes 2359296 | tf_op jit(solution)/shard_map/all_to_all | solution.py:978
  179.6 21.1 %copy-start.9 = (f32[128,1024]{1,0:T(8,128)}, f32[128,1024]{1,0:T(8,128)S(1)}, u32[]{:S(2)}) copy-start(f32[128,1024]{1,0:T(8,128)S(1)} %get-tuple-element.200) | copy-start | bytes 1572868
  200.7 26.9 %copy-start.20 = (bf16[4,144,1024]{2,1,0:T(8,128)(2,1)}, bf16[4,144,1024]{2,1,0:T(8,128)(2,1)S(1)}, u32[]{:S(2)}) copy-start(bf16[4,144,1024]{2,1,0:T(8,128)(2,1)S(1)} %all_to_all.47.near_ref) | copy-start | bytes 3538948
  200.7 29.9 %collective-permute-start.16 = (bf16[4,144,1024]{2,1,0:T(8,128)(2,1)S(1)}, bf16[4,144,1024]{2,1,0:T(8,128)(2,1)S(1)}, u32[]{:S(2)}, u32[]{:S(2)}) collective-permute-start(bf16[4,144,1024]{2,1,0:T(8,128)(2,1)S(1)} %all_to_all.47.near_ref), channel_id=1, source_target_pairs={{0,1},{1,0},{2,3},{3,2},{4,5},{5,4},{6,7},{7,6},{8,9},{9,8},{10,11... | collective-permute-start | bytes 3538952 | tf_op jit(solution)/shard_map/ppermute | solution.py:973
  200.8 29.3 %collective-permute-start.7 = (bf16[3,144,1024]{2,1,0:T(8,128)(2,1)}, bf16[3,144,1024]{2,1,0:T(8,128)(2,1)S(1)}, u32[]{:S(2)}, u32[]{:S(2)}) collective-permute-start(bf16[3,144,1024]{2,1,0:T(8,128)(2,1)} %pad_maximum_fusion.2), channel_id=1, source_target_pairs={{0,6},{1,7},{2,4},{3,5},{4,2},{5,3},{6,0},{7,1},{8,14},{9,15},{10,... | collective-permute-start | bytes 2654216 | tf_op jit(solution)/shard_map/ppermute | solution.py:982
  201.8 11.1 %collective-permute-start.12 = (bf16[128,1024]{1,0:T(8,128)(2,1)S(1)}, bf16[128,1024]{1,0:T(8,128)(2,1)S(1)}, u32[]{:S(2)}, u32[]{:S(2)}) collective-permute-start(bf16[128,1024]{1,0:T(8,128)(2,1)S(1)} %copy-done.14), channel_id=1, source_target_pairs={{0,24},{8,16},{16,8},{24,0},{1,25},{9,17},{17,9},{25,1},{2,26},{10... | collective-permute-start | bytes 786440 | tf_op jit(solution)/shard_map/ppermute | solution.py:982
  204.3 21.7 %collective-permute-start.11 = (bf16[128,1024]{1,0:T(8,128)(2,1)S(1)}, bf16[128,1024]{1,0:T(8,128)(2,1)S(1)}, u32[]{:S(2)}, u32[]{:S(2)}) collective-permute-start(bf16[128,1024]{1,0:T(8,128)(2,1)S(1)} %copy-done.14), channel_id=1, source_target_pairs={{0,16},{8,24},{16,0},{24,8},{1,17},{9,25},{17,1},{25,9},{2,18},{10... | collective-permute-start | bytes 786440 | tf_op jit(solution)/shard_map/ppermute | solution.py:982
  204.3 23.3 %collective-permute-start.10 = (bf16[128,1024]{1,0:T(8,128)(2,1)S(1)}, bf16[128,1024]{1,0:T(8,128)(2,1)S(1)}, u32[]{:S(2)}, u32[]{:S(2)}) collective-permute-start(bf16[128,1024]{1,0:T(8,128)(2,1)S(1)} %copy-done.14), channel_id=1, source_target_pairs={{0,8},{8,0},{16,24},{24,16},{1,9},{9,1},{17,25},{25,17},{2,10},{10... | collective-permute-start | bytes 786440 | tf_op jit(solution)/shard_map/ppermute | solution.py:982
  212.9 39.6 %collective-permute-start.6 = (bf16[3,144,1024]{2,1,0:T(8,128)(2,1)}, bf16[3,144,1024]{2,1,0:T(8,128)(2,1)}, u32[]{:S(2)}, u32[]{:S(2)}) collective-permute-start(bf16[3,144,1024]{2,1,0:T(8,128)(2,1)} %pad_maximum_fusion.2), channel_id=1, source_target_pairs={{0,4},{1,5},{2,6},{3,7},{4,0},{5,1},{6,2},{7,3},{8,12},{9,13},{10,... | collective-permute-start | bytes 2654216 | tf_op jit(solution)/shard_map/ppermute | solution.py:982
  226.0 26.5 %collective-permute-start.5 = (bf16[3,144,1024]{2,1,0:T(8,128)(2,1)}, bf16[3,144,1024]{2,1,0:T(8,128)(2,1)}, u32[]{:S(2)}, u32[]{:S(2)}) collective-permute-start(bf16[3,144,1024]{2,1,0:T(8,128)(2,1)} %pad_maximum_fusion.2), channel_id=1, source_target_pairs={{0,2},{1,3},{2,0},{3,1},{4,6},{5,7},{6,4},{7,5},{8,10},{9,11},{10,... | collective-permute-start | bytes 2654216 | tf_op jit(solution)/shard_map/ppermute | solution.py:982
  228.6 38.0 %collective-permute-start.15 = (bf16[3,128,1024]{2,1,0:T(8,128)(2,1)}, bf16[3,128,1024]{2,1,0:T(8,128)(2,1)}, u32[]{:S(2)}, u32[]{:S(2)}) collective-permute-start(bf16[3,128,1024]{2,1,0:T(8,128)(2,1)} %pad_maximum_fusion.4), channel_id=1, source_target_pairs={{0,6},{1,7},{2,4},{3,5},{4,2},{5,3},{6,0},{7,1},{8,14},{9,15},{10,... | collective-permute-start | bytes 2359304 | tf_op jit(solution)/shard_map/ppermute | solution.py:982
  230.1 46.8 %collective-permute-start.14 = (bf16[3,128,1024]{2,1,0:T(8,128)(2,1)}, bf16[3,128,1024]{2,1,0:T(8,128)(2,1)}, u32[]{:S(2)}, u32[]{:S(2)}) collective-permute-start(bf16[3,128,1024]{2,1,0:T(8,128)(2,1)} %pad_maximum_fusion.4), channel_id=1, source_target_pairs={{0,4},{1,5},{2,6},{3,7},{4,0},{5,1},{6,2},{7,3},{8,12},{9,13},{10,... | collective-permute-start | bytes 2359304 | tf_op jit(solution)/shard_map/ppermute | solution.py:982
  231.0 51.6 %collective-permute-start.13 = (bf16[3,128,1024]{2,1,0:T(8,128)(2,1)}, bf16[3,128,1024]{2,1,0:T(8,128)(2,1)}, u32[]{:S(2)}, u32[]{:S(2)}) collective-permute-start(bf16[3,128,1024]{2,1,0:T(8,128)(2,1)} %pad_maximum_fusion.4), channel_id=1, source_target_pairs={{0,2},{1,3},{2,0},{3,1},{4,6},{5,7},{6,4},{7,5},{8,10},{9,11},{10,... | collective-permute-start | bytes 2359304 | tf_op jit(solution)/shard_map/ppermute | solution.py:982
  232.9 66.6 %copy-start.36 = (f32[128]{0:T(128)}, f32[128]{0:T(128)S(1)}, u32[]{:S(2)}) copy-start(f32[128]{0:T(128)S(1)} %add_rsqrt_fusion) | copy-start | bytes 1540
  248.2 39.3 %all-to-all-start.6 = ((bf16[8,128,256]{2,1,0:T(8,128)(2,1)}), bf16[8,128,256]{2,1,0:T(8,128)(2,1)}, u32[]{:S(2)}, u32[]{:S(2)}) async-start(bf16[8,128,256]{2,1,0:T(8,128)(2,1)} %get-tuple-element.96), calls=%async_computation.6 | async-start | bytes 1048576 | tf_op jit(solution)/shard_map/all_to_all | solution.py:1038
  254.7 87.7 %copy-start.2 = (bf16[4,3,144,1024]{3,2,1,0:T(8,128)(2,1)}, bf16[4,3,144,1024]{3,2,1,0:T(8,128)(2,1)S(1)}, u32[]{:S(2)}) copy-start(bf16[4,3,144,1024]{3,2,1,0:T(8,128)(2,1)S(1)} %pad_maximum_fusion.gn) | copy-start | bytes 10616836
  302.0 40.5 %collective-permute-start.25 = (bf16[4,3,144,1024]{3,2,1,0:T(8,128)(2,1)S(1)}, bf16[4,3,144,1024]{3,2,1,0:T(8,128)(2,1)}, u32[]{:S(2)}, u32[]{:S(2)}) collective-permute-start(bf16[4,3,144,1024]{3,2,1,0:T(8,128)(2,1)S(1)} %pad_maximum_fusion.gn), channel_id=1, source_target_pairs={{0,1},{1,0},{2,3},{3,2},{4,5},{5,4},{6,7},{7,6},{8,9},{9,8},{10,11... | collective-permute-start | bytes 10616840 | tf_op jit(solution)/shard_map/ppermute | solution.py:973
  302.0 42.6 %collective-permute-start.24 = (bf16[4,3,128,1024]{3,2,1,0:T(8,128)(2,1)}, bf16[4,3,128,1024]{3,2,1,0:T(8,128)(2,1)}, u32[]{:S(2)}, u32[]{:S(2)}) collective-permute-start(bf16[4,3,128,1024]{3,2,1,0:T(8,128)(2,1)} %pad_maximum_fusion.1.xn), channel_id=1, source_target_pairs={{0,1},{1,0},{2,3},{3,2},{4,5},{5,4},{6,7},{7,6},{8,9},{9,8},{10,11... | collective-permute-start | bytes 9437192 | tf_op jit(solution)/shard_map/ppermute | solution.py:973
  313.6 11.3 %collective-permute-start.21 = (bf16[400,256]{1,0:T(8,128)(2,1)}, bf16[400,256]{1,0:T(8,128)(2,1)}, u32[]{:S(2)}, u32[]{:S(2)}) collective-permute-start(bf16[400,256]{1,0:T(8,128)(2,1)} %get-tuple-element.187), channel_id=1, source_target_pairs={{0,8},{8,0},{16,24},{24,16},{1,9},{9,1},{17,25},{25,17},{2,10},{10... | collective-permute-start | bytes 614408 | tf_op jit(solution)/shard_map/ppermute | solution.py:982
  313.6 12.1 %collective-permute-start.23 = (bf16[400,256]{1,0:T(8,128)(2,1)}, bf16[400,256]{1,0:T(8,128)(2,1)}, u32[]{:S(2)}, u32[]{:S(2)}) collective-permute-start(bf16[400,256]{1,0:T(8,128)(2,1)} %get-tuple-element.188), channel_id=1, source_target_pairs={{0,24},{8,16},{16,8},{24,0},{1,25},{9,17},{17,9},{25,1},{2,26},{10... | collective-permute-start | bytes 614408 | tf_op jit(solution)/shard_map/ppermute | solution.py:982
  314.9 20.3 %collective-permute-start.22 = (bf16[400,256]{1,0:T(8,128)(2,1)}, bf16[400,256]{1,0:T(8,128)(2,1)}, u32[]{:S(2)}, u32[]{:S(2)}) collective-permute-start(bf16[400,256]{1,0:T(8,128)(2,1)} %get-tuple-element.189), channel_id=1, source_target_pairs={{0,16},{8,24},{16,0},{24,8},{1,17},{9,25},{17,1},{25,9},{2,18},{10... | collective-permute-start | bytes 614408 | tf_op jit(solution)/shard_map/ppermute | solution.py:982
  338.2 25.1 %all-to-all-start.7 = ((bf16[4,416,256]{2,1,0:T(8,128)(2,1)}), bf16[4,416,256]{2,1,0:T(8,128)(2,1)}, u32[]{:S(2)}, u32[]{:S(2)}) async-start(bf16[4,416,256]{2,1,0:T(8,128)(2,1)} %broadcast_in_dim.105), calls=%async_computation.7 | async-start | bytes 1703936 | tf_op jit(solution)/shard_map/all_to_all | solution.py:1038
  369.0 40.2 %all-to-all-start.8 = ((bf16[4,1568,256]{2,1,0:T(8,128)(2,1)}), bf16[4,1568,256]{2,1,0:T(8,128)(2,1)S(1)}, u32[]{:S(2)}, u32[]{:S(2)}) async-start(bf16[4,1568,256]{2,1,0:T(8,128)(2,1)} %broadcast_in_dim.107), calls=%async_computation.8 | async-start | bytes 6422528 | tf_op jit(solution)/shard_map/all_to_all | solution.py:978
  409.2 30.9 %copy-start.3 = (bf16[4,1568,256]{2,1,0:T(8,128)(2,1)}, bf16[4,1568,256]{2,1,0:T(8,128)(2,1)S(1)}, u32[]{:S(2)}) copy-start(bf16[4,1568,256]{2,1,0:T(8,128)(2,1)S(1)} %all-to-all-done.8.near_ref) | copy-start | bytes 9633796
  409.2 30.9 %collective-permute-start.26 = (bf16[4,1568,256]{2,1,0:T(8,128)(2,1)S(1)}, bf16[4,1568,256]{2,1,0:T(8,128)(2,1)}, u32[]{:S(2)}, u32[]{:S(2)}) collective-permute-start(bf16[4,1568,256]{2,1,0:T(8,128)(2,1)S(1)} %all-to-all-done.8.near_ref), channel_id=1, source_target_pairs={{0,1},{1,0},{2,3},{3,2},{4,5},{5,4},{6,7},{7,6},{8,9},{9,8},{10,11... | collective-permute-start | bytes 9633800 | tf_op jit(solution)/shard_map/ppermute | solution.py:973
  409.2 7.4 %collective-permute-start.17 = (bf16[4,128,1024]{2,1,0:T(8,128)(2,1)}, bf16[4,128,1024]{2,1,0:T(8,128)(2,1)}, u32[]{:S(2)}, u32[]{:S(2)}) collective-permute-start(bf16[4,128,1024]{2,1,0:T(8,128)(2,1)} %get-tuple-element.98), channel_id=1, source_target_pairs={{0,1},{1,0},{2,3},{3,2},{4,5},{5,4},{6,7},{7,6},{8,9},{9,8},{10,11... | collective-permute-start | bytes 3145736 | tf_op jit(solution)/shard_map/ppermute | solution.py:973
  409.7 27.3 %copy-start.7 = (bf16[1,128,1024]{2,1,0:T(8,128)(2,1)S(1)}, bf16[1,128,1024]{2,1,0:T(8,128)(2,1)}, u32[]{:S(2)}) copy-start(bf16[1,128,1024]{2,1,0:T(8,128)(2,1)} %param.14) | copy-start | bytes 786436
  409.7 27.3 %copy-start.29 = (f32[1024]{0:T(1024)S(1)}, f32[1024]{0:T(1024)}, u32[]{:S(2)}) copy-start(f32[1024]{0:T(1024)} %param.15) | copy-start | bytes 12292
  409.8 27.3 %copy-start.32 = (f32[128]{0:T(128)S(1)}, f32[128]{0:T(128)}, u32[]{:S(2)}) copy-start(f32[128]{0:T(128)} %copy-done.31) | copy-start | bytes 1540
  409.8 27.3 %copy-start.35 = (f32[128]{0:T(128)S(1)}, f32[128]{0:T(128)}, u32[]{:S(2)}) copy-start(f32[128]{0:T(128)} %copy-done.34) | copy-start | bytes 1540
  409.8 27.3 %copy-start.37 = (f32[128]{0:T(128)S(1)}, f32[128]{0:T(128)}, u32[]{:S(2)}) copy-start(f32[128]{0:T(128)} %copy-done.36) | copy-start | bytes 1540
  420.4 9.5 %collective-permute-start.18 = (bf16[128,1024]{1,0:T(8,128)(2,1)}, bf16[128,1024]{1,0:T(8,128)(2,1)}, u32[]{:S(2)}, u32[]{:S(2)}) collective-permute-start(bf16[128,1024]{1,0:T(8,128)(2,1)} %get-tuple-element.184), channel_id=1, source_target_pairs={{0,2},{1,3},{2,0},{3,1},{4,6},{5,7},{6,4},{7,5},{8,10},{9,11},{10,... | collective-permute-start | bytes 786440 | tf_op jit(solution)/shard_map/ppermute | solution.py:982
  421.9 13.8 %collective-permute-start.20 = (bf16[128,1024]{1,0:T(8,128)(2,1)}, bf16[128,1024]{1,0:T(8,128)(2,1)}, u32[]{:S(2)}, u32[]{:S(2)}) collective-permute-start(bf16[128,1024]{1,0:T(8,128)(2,1)} %get-tuple-element.185), channel_id=1, source_target_pairs={{0,6},{1,7},{2,4},{3,5},{4,2},{5,3},{6,0},{7,1},{8,14},{9,15},{10,... | collective-permute-start | bytes 786440 | tf_op jit(solution)/shard_map/ppermute | solution.py:982
  423.4 13.7 %collective-permute-start.19 = (bf16[128,1024]{1,0:T(8,128)(2,1)}, bf16[128,1024]{1,0:T(8,128)(2,1)}, u32[]{:S(2)}, u32[]{:S(2)}) collective-permute-start(bf16[128,1024]{1,0:T(8,128)(2,1)} %get-tuple-element.186), channel_id=1, source_target_pairs={{0,4},{1,5},{2,6},{3,7},{4,0},{5,1},{6,2},{7,3},{8,12},{9,13},{10,... | collective-permute-start | bytes 786440 | tf_op jit(solution)/shard_map/ppermute | solution.py:982
  (24 other events, 173.9 us)

commit v2 on v1

--- a/solution.py
+++ b/solution.py
@@ -554,8 +554,8 @@
 
 
 def expert_weight_grads(ids, sums, x_near, x_twin, g_near, g_twin, mask_all, slot_all, router_t, weights, copies):
-    chips, unused, group_len, width = x_near.shape
-    held, unused, inner = weights[0].shape
+    chips, count, group_len, width = x_near.shape
+    held, _, inner = weights[0].shape
     groups = 2 * chips
     slots = groups * MOST
     wide, narrow = width // copies, inner // copies
@@ -563,46 +563,56 @@
     def kernel(ids_ref, xn, xt, gn, gt, mr, sr, rt, wg, wu, wd, *refs):
         gate_out, up_out, down_out, x_scr, g_scr, gate_scr = refs[-6:]
         befores = refs[:-6] if sums is not None else (None, None, None)
-        e = pl.program_id(0)
+        step = pl.program_id(0)
         mine, slab = ids_ref[0], ids_ref[1]
 
-        @pl.when(e == 0)
+        @pl.when(step < count)
         def _():
             expert_gather(
                 lambda g: (xn if g < chips else xt)[g % chips, 0],
                 lambda g: (gn if g < chips else gt)[g % chips, 0],
                 lambda g: mr[g],
                 lambda g: sr[g],
-                rt[...], mine * held, x_scr, g_scr, gate_scr, None, groups,
+                rt[...], mine * held, x_scr.at[step], g_scr.at[step], gate_scr.at[step], None, groups,
             )
 
-        x_slots = x_scr[e]
-        hidden, dexpert, dgate_pre, dup_pre = expert_body(
-            x_slots, g_scr[e], gate_scr[e], wg[0], wu[0], wd[0]
-        )
-        x_part, h_part = x_slots[:, :wide], hidden[:, :narrow]
-        for k in range(1, copies):
-            x_part = jnp.where(slab == k, x_slots[:, k * wide : (k + 1) * wide], x_part)
-            h_part = jnp.where(slab == k, hidden[:, k * narrow : (k + 1) * narrow], h_part)
-        for out, before, left, right in zip(
-            (gate_out, up_out, down_out),
-            befores,
-            (x_part, x_part, h_part),
-            (dgate_pre, dup_pre, dexpert),
-        ):
-            part = tn(left, right)
-            out[0] = part if before is None else before[0] + part
-
-    some = lambda *shape: pl.BlockSpec((groups,) + shape, lambda e, m: (m[2], 0, 0))
-    rows = pl.BlockSpec((chips, 1, group_len, width), lambda e, m: (0, m[2], 0, 0))
-    weight = lambda *shape: pl.BlockSpec((1,) + shape, lambda e, m: (e, 0, 0))
-    whole = lambda *shape: pl.BlockSpec(shape, lambda e, m: (0,) * len(shape))
+        @pl.when(step >= count)
+        def _():
+            e, row = (step - count) // count, (step - count) % count
+            x_slots = x_scr[row, e]
+            hidden, dexpert, dgate_pre, dup_pre = expert_body(
+                x_slots, g_scr[row, e], gate_scr[row, e], wg[0], wu[0], wd[0]
+            )
+            x_part, h_part = x_slots[:, :wide], hidden[:, :narrow]
+            for k in range(1, copies):
+                x_part = jnp.where(slab == k, x_slots[:, k * wide : (k + 1) * wide], x_part)
+                h_part = jnp.where(slab == k, hidden[:, k * narrow : (k + 1) * narrow], h_part)
+            for out, before, left, right in zip(
+                (gate_out, up_out, down_out),
+                befores,
+                (x_part, x_part, h_part),
+                (dgate_pre, dup_pre, dexpert),
+            ):
+                part = tn(left, right)
+
+                @pl.when(row == 0)
+                def _():
+                    out[0] = part if before is None else before[0] + part
+
+                @pl.when(row > 0)
+                def _():
+                    out[0] = out[0] + part
+
+    some = lambda *shape: pl.BlockSpec((groups,) + shape, lambda i, m: (jnp.minimum(i, count - 1), 0, 0))
+    rows = pl.BlockSpec((chips, 1, group_len, width), lambda i, m: (0, jnp.minimum(i, count - 1), 0, 0))
+    weight = lambda *shape: pl.BlockSpec((1,) + shape, lambda i, m: (jnp.maximum(i - count, 0) // count, 0, 0))
+    whole = lambda *shape: pl.BlockSpec(shape, lambda i, m: (0,) * len(shape))
     outs = [(held, wide, inner), (held, wide, inner), (held, narrow, width)]
     return pl.pallas_call(
         kernel,
         grid_spec=pltpu.PrefetchScalarGridSpec(
             num_scalar_prefetch=1,
-            grid=(held,),
+            grid=(count + held * count,),
             in_specs=[
                 rows,
                 rows,
@@ -618,9 +628,9 @@
             + ([weight(*shape[1:]) for shape in outs] if sums is not None else []),
             out_specs=[weight(*shape[1:]) for shape in outs],
             scratch_shapes=[
-                pltpu.VMEM((held, slots, width), jnp.bfloat16),
-                pltpu.VMEM((held, slots, width), jnp.bfloat16),
-                pltpu.VMEM((held, slots, 1), jnp.float32),
+                pltpu.VMEM((count, held, slots, width), jnp.bfloat16),
+                pltpu.VMEM((count, held, slots, width), jnp.bfloat16),
+                pltpu.VMEM((count, held, slots, 1), jnp.float32),
             ],
         ),
         out_shape=[jax.ShapeDtypeStruct(shape, jnp.float32) for shape in outs],
@@ -628,7 +638,7 @@
             dimension_semantics=("arbitrary",), vmem_limit_bytes=58 * 2**20
         ),
         cost_estimate=pl.CostEstimate(
-            flops=2 * 4 * held * slots * width * inner, transcendentals=0, bytes_accessed=2**24
+            flops=2 * 4 * count * held * slots * width * inner, transcendentals=0, bytes_accessed=2**24
         ),
         input_output_aliases={11 + i: i for i in range(3)} if sums is not None else {},
         name="expert_weight_grads",
@@ -711,9 +721,9 @@
     return jnp.sum(jnp.where(diagonal, row, 0), axis=1, keepdims=True)
 
 
-def attend_heads(me, near_pay, twin_pay, gain, head_weights, segs, index):
+def attend_heads(me, near_pay, twin_pay, gain, head_weights, index):
     chips = near_pay.shape[0]
-    blocks, group_len = segs.shape
+    blocks, group_len = index.shape
     width, head_cols = head_weights.shape
     length = blocks * group_len
     pair = 2 * HEAD_DIM
@@ -721,14 +731,25 @@
     def device(me, g):
         return 2 * (g % chips) + ((me & 1) ^ (g // chips))
 
-    def kernel(me_ref, near_ref, twin_ref, gain_ref, w_ref, freq_ref, seg_ref, seg_rows, index_ref,
-               index_rows, normed_out, qkv_out, cos_out, sin_out, attn_out, attended_out, lse_out,
-               k_scr, v_scr, pos_scr):
+    def kernel(me_ref, near_ref, twin_ref, gain_ref, w_ref, freq_ref, index_ref, index_rows,
+               normed_out, qkv_out, cos_out, sin_out, attn_out, attended_out, lse_out,
+               seg_rows, seg_ref, k_scr, v_scr, pos_scr):
         step = pl.program_id(0)
 
         @pl.when(step == 0)
         def _():
-            numbers = seg_rows[...]
+            numbers = jnp.concatenate(
+                [
+                    (near_ref if g < chips else twin_ref)[
+                        g % chips, group_len : group_len + 1, :group_len
+                    ].astype(jnp.float32)
+                    for g in range(blocks)
+                ],
+                axis=0,
+            ).astype(jnp.int32)
+            seg_rows[...] = numbers
+            for g in range(blocks):
+                seg_ref[:, g * group_len : (g + 1) * group_len] = numbers[g : g + 1, :]
             start = jnp.zeros(numbers.shape, jnp.float32)
             for s in range(SEGMENTS - 1):
                 found = jnp.where(numbers == s, 1.0, 0.0)
@@ -812,8 +833,6 @@
                 whole(half, 1),
                 whole(1, length),
                 whole(blocks, group_len),
-                whole(1, length),
-                whole(blocks, group_len),
             ],
             out_specs=[
                 whole(blocks, group_len, width),
@@ -823,6 +842,8 @@
                 pl.BlockSpec((1, group_len, pair), lambda i, m: (device(m[0], second(i)), 0, 0)),
                 pl.BlockSpec((group_len, pair), lambda i, m: (second(i), 0)),
                 pl.BlockSpec((group_len, pair), lambda i, m: (second(i), 0)),
+                whole(blocks, group_len),
+                whole(1, length),
             ],
             scratch_shapes=[
                 pltpu.VMEM((length, HEAD_DIM), bf16),
@@ -838,6 +859,8 @@
             jax.ShapeDtypeStruct((blocks, group_len, pair), bf16),
             jax.ShapeDtypeStruct((length, pair), f32),
             jax.ShapeDtypeStruct((length, pair), f32),
+            jax.ShapeDtypeStruct((blocks, group_len), jnp.int32),
+            jax.ShapeDtypeStruct((1, length), jnp.int32),
         ],
         cost_estimate=pl.CostEstimate(
             flops=2 * length * (width * head_cols + 4 * length * HEAD_DIM) * 2,
@@ -847,11 +870,11 @@
         name="attend_heads",
     )(
         me.reshape(1), near_pay, twin_pay, gain[None], head_weights, freqs[:, None],
-        segs.reshape(1, length), segs, index.reshape(1, length), index,
-    )
-
-
-def attend_back(me, near_db, twin_db, out_heads, qkv, cosine, sine, attended, lse, segs, index, copies):
+        index.reshape(1, length), index,
+    )
+
+
+def attend_back(me, near_db, twin_db, out_heads, qkv, cosine, sine, attended, lse, segs, seg_lane, index, copies):
     chips = near_db.shape[0]
     span = out_heads.shape[1] // copies
     blocks, group_len = segs.shape
@@ -965,8 +988,70 @@
         name="attend_back",
     )(
         me.reshape(1), near_db, twin_db, out_heads, qkv, cosine, sine, attended, lse,
-        segs.reshape(1, length), segs, index.reshape(1, length),
-    )
+        seg_lane, segs, index.reshape(1, length),
+    )
+
+
+def token_back(dlin, w_query, w_key, w_value, tokens, dmiddle, gain):
+    devices, group_len, head_cols = dlin.shape
+    width = tokens.shape[1]
+    pair = head_cols - 2 * HEAD_DIM
+
+    def kernel(dlin_ref, wq_ref, wk_ref, wv_ref, tokens_ref, dmid_ref, gain_ref, out_ref, part_ref,
+               sum_scr):
+        j = pl.program_id(0)
+        here = dlin_ref[...]
+        total = nt(jnp.concatenate([here[0][:, :pair], here[1][:, :pair]], axis=1), wq_ref[...])
+        for start, ref in ((pair, wk_ref), (pair + HEAD_DIM, wv_ref)):
+            both = jnp.concatenate(
+                [here[0][:, start : start + HEAD_DIM], here[1][:, start : start + HEAD_DIM]], axis=1
+            )
+            total = total + nt(both, ref[...])
+
+        @pl.when(j == 0)
+        def _():
+            sum_scr[...] = total
+
+        @pl.when(j > 0)
+        def _():
+            sum_scr[...] += total
+
+        @pl.when(j == devices // 2 - 1)
+        def _():
+            rows = tokens_ref[...].astype(jnp.float32)
+            dnormed = sum_scr[...]
+            inverse = lax.rsqrt(jnp.mean(rows * rows, axis=1, keepdims=True) + NORM_EPS)
+            unit = rows * inverse
+            scaled = dnormed * gain_ref[...]
+            mean = jnp.mean(scaled * unit, axis=1, keepdims=True)
+            out_ref[...] = dmid_ref[...] + inverse * (scaled - unit * mean)
+            part_ref[...] = jnp.sum(dnormed * unit, axis=0, keepdims=True)
+
+    whole = lambda *shape: pl.BlockSpec(shape, lambda j: (0,) * len(shape))
+    return pl.pallas_call(
+        kernel,
+        grid=(devices // 2,),
+        in_specs=[
+            pl.BlockSpec((2, group_len, head_cols), lambda j: (j, 0, 0)),
+            pl.BlockSpec((width, 2 * pair), lambda j: (0, j)),
+            pl.BlockSpec((width, 2 * HEAD_DIM), lambda j: (0, j)),
+            pl.BlockSpec((width, 2 * HEAD_DIM), lambda j: (0, j)),
+            whole(group_len, width),
+            whole(group_len, width),
+            whole(1, width),
+        ],
+        out_specs=[whole(group_len, width), whole(1, width)],
+        scratch_shapes=[pltpu.VMEM((group_len, width), jnp.float32)],
+        out_shape=[
+            jax.ShapeDtypeStruct((group_len, width), jnp.float32),
+            jax.ShapeDtypeStruct((1, width), jnp.float32),
+        ],
+        cost_estimate=pl.CostEstimate(
+            flops=2 * group_len * width * head_cols * devices, transcendentals=0,
+            bytes_accessed=2**22,
+        ),
+        name="token_back",
+    )(dlin, w_query, w_key, w_value, tokens, dmiddle, gain[None])
 
 
 def swap_cores(block, devices):
@@ -1073,7 +1158,7 @@
     segment_ids,
     out_grad,
 ):
-    unused, group_len, width = tokens.shape
+    _, group_len, width = tokens.shape
     devices, copies = lax.axis_size("expert"), lax.axis_size("dp")
     me, me_z = lax.axis_index("expert"), lax.axis_index("dp")
     core = me & 1
@@ -1087,9 +1172,6 @@
 
     own = tokens[0]
     near_pay, twin_pay = spread_row(with_tail(own, segment_ids.astype(bf16)), devices)
-    seg_rows = jnp.concatenate(
-        [near_pay[:, group_len, :group_len], twin_pay[:, group_len, :group_len]], axis=0
-    ).astype(jnp.int32)
     row_index = order[:, None] * group_len + jnp.arange(group_len, dtype=jnp.int32)
 
     mask_own = jnp.any(
@@ -1119,8 +1201,8 @@
         ],
         axis=1,
     )
-    normed_row, qkv, cosine, sine, attn_heads, attended, lse = attend_heads(
-        me, near_pay, twin_pay, attn_gain, head_weights, seg_rows, row_index
+    normed_row, qkv, cosine, sine, attn_heads, attended, lse, seg_rows, seg_lane = attend_heads(
+        me, near_pay, twin_pay, attn_gain, head_weights, row_index
     )
     attn_heads, g_near, g_twin = lax.optimization_barrier((attn_heads, g_near, g_twin))
     attn_rows = jnp.swapaxes(exchange(attn_heads, "expert"), 0, 1).reshape(
@@ -1146,8 +1228,8 @@
     d_merged = merge_cores(d_near, d_twin, devices)
     weights = (w_gate, w_up, w_down)
 
-    def expert_row(z, sums, x_rows, g_rows, masks, slots):
-        ids = jnp.stack([me, me_z, jnp.int32(z)])
+    def expert_rows(sums, x_rows, g_rows, masks, slots):
+        ids = jnp.stack([me, me_z])
         return expert_weight_grads(
             ids, sums, *x_rows, *g_rows, masks, slots, router_t, weights, copies
         )
@@ -1156,7 +1238,7 @@
     x_mine, g_mine, d_merged = lax.optimization_barrier(
         ((x_near[:, None], x_twin[:, None]), (g_near[:, None], g_twin[:, None]), d_merged)
     )
-    sums = expert_row(0, None, x_mine, g_mine, mask_row, slot_row)
+    sums = expert_rows(None, x_mine, g_mine, mask_row, slot_row)
     crossed, sums = lax.optimization_barrier((crossed, sums))
     returned = jnp.sum(crossed.astype(jnp.float32), axis=0)
 
@@ -1183,7 +1265,7 @@
     out_heads = lax.dynamic_slice_in_dim(w_output, me * query_cols, query_cols, 0)
     dlin, output_part = attend_back(
         me, branch_near, branch_twin, out_heads, qkv, cosine, sine, attended, lse, seg_rows,
-        row_index, copies,
+        seg_lane, row_index, copies,
     )
     head_cols = query_cols + 2 * HEAD_DIM
     rows_per = width // devices
@@ -1208,21 +1290,11 @@
     )
 
     shared_sum = permute_sum(shared_part, me_z, 1, "dp", copies).astype(bf16)
-    dlin_back = jnp.swapaxes(exchange(dlin, "expert"), 0, 1)
-
-    def token_grad(start, count, weights):
-        rows = dlin_back[:, :, start : start + count].reshape(group_len, devices * count)
-        return jnp.einsum("nh,dh->nd", rows, weights, preferred_element_type=jnp.float32)
-
-    dnormed = (
-        token_grad(0, query_cols, w_query)
-        + token_grad(query_cols, HEAD_DIM, w_key)
-        + token_grad(query_cols + HEAD_DIM, HEAD_DIM, w_value)
-    )
-    unused, unit_attn, inv_attn = rms_forward(residual, attn_gain)
-    dresid_norm, attn_gain_part = rms_backward(dnormed, unit_attn, inv_attn, attn_gain)
-    grad_tokens = (dmiddle + dresid_norm)[None]
-    gain_parts = pack_gains(jnp.stack([attn_gain_part, moe_gain_part]), head_cols)
+    grad_tokens, attn_gain_part = token_back(
+        exchange(dlin, "expert"), w_query, w_key, w_value, own, dmiddle, attn_gain
+    )
+    grad_tokens = grad_tokens[None]
+    gain_parts = pack_gains(jnp.stack([attn_gain_part[0], moe_gain_part]), head_cols)
     column = exchange(broadcast(jnp.concatenate([shared_sum, gain_parts], axis=0), copies), "dp")
 
     g_far, x_far, y_near, y_twin, gain_parts = lax.optimization_barrier(
@@ -1235,11 +1307,6 @@
     y_merged = merge_cores(y_near, y_twin, devices)
     y_sum = permute_sum(y_merged, me >> 1, 2, "expert", devices)
 
-    def far_row(step, sums):
-        return expert_row(step - 1, sums, x_rows, g_rows, masks, slots)
-
-    sums = far_row(1, sums)
-    column, sums = lax.optimization_barrier((column, sums))
     router_start = rows + query_cols
     gain_start = router_start + TAIL
     gain_parts = pack_gains(jnp.sum(unpack_gains(column[:, gain_start:], width), axis=0), head_cols)
@@ -1253,8 +1320,7 @@
         axis=0,
     )
     head_near = across_chips(broadcast(column, chips), devices)
-    for step in range(2, copies):
-        sums = far_row(step, sums)
+    sums = expert_rows(sums, x_rows, g_rows, masks, slots)
     head_near, sums = lax.optimization_barrier((head_near, sums))
     head_twin = swap_cores(head_near, devices)
     mixed = (middle + RESIDUAL_SCALE * y_sum).astype(bf16)[None]

time: 465 us -> 454 us (0.976); the launches traced: 457 us -> 452 us
  local copies, waits for them, and re-layouts: 41.6 us -> 24.2 us
  waiting for transfers between devices: 142 us -> 158 us
    all_to_all x2, waiting for transfers between devices: 4.05 us -> 23.4 us  [exchange(): return lax.all_to_all(blocks, axis, 0, 0, tiled=True)]
    slice x5 -> x0, local copies, waits for them, and re-layouts: 8.84 us -> none  [token_grad(): dlin_back[:, :, start:start + count].reshape(group_len, devices * count)]
    ppermute x18, waiting for transfers between devices: 103 us -> 96.5 us  [permute(): return lax.ppermute(block, axis, [(i, i ^ shift) for i in range(count)])]
    pallas_call x0 -> x1, Pallas kernels: none -> 5.78 us  [token_back(): pl.pallas_call(kernel, grid=(devices // 2,), in_specs=[pl.BlockSpec((2, g...]
    dot_general x3 -> x0, matrix products: 4.98 us -> none  [token_grad(): jnp.einsum('nh,dh->nd', rows, weights, preferred_element_type=jnp.float32)]
    pallas_call x4 -> x2, Pallas kernels: 64.6 us -> 60.5 us  [expert_weight_grads(): pl.pallas_call(kernel, grid_spec=pltpu.PrefetchScalarGridSpec(num_scalar_...]
  transfers between devices with their start and end apart: 33 -> 33, of which waited for: 20 -> 18; matrix products, arithmetic and copies ran while one was open for 10% -> 9% of each run, Pallas kernels for 21% -> 20%
where the time goes in v2:
time: 454 us; the launch traced here: 452 us
  waiting for transfers between devices  158 us (35%)
  Pallas kernels  133 us (29%)
  starting transfers between devices  47.6 us (10%)
  blocking collectives  46.6 us (10%)
  other arithmetic  31.9 us (7%)
  local copies, waits for them, and re-layouts  24.2 us (5%)
  matrix products  8.87 us (2%)
    ppermute x18, waiting for transfers between devices, permute(): return lax.ppermute(block, axis, [(i, i ^ shift) for i in range(count)])  96.5 us
    pallas_call x2, Pallas kernels, expert_weight_grads(): pl.pallas_call(kernel, grid_spec=pltpu.PrefetchScalarGridSpec(num_scalar_...  60.5 us
    all_to_all x2, blocking collectives, across_chips(): lax.all_to_all(blocks, 'expert', 0, 0, axis_index_groups=groups, tiled=True)  36.4 us
    all_to_all x4, waiting for transfers between devices, across_chips(): lax.all_to_all(blocks, 'expert', 0, 0, axis_index_groups=groups, tiled=True)  28.8 us
    all_to_all x2, waiting for transfers between devices, exchange(): return lax.all_to_all(blocks, axis, 0, 0, tiled=True)  23.4 us
    ppermute x18, starting transfers between devices, permute(): return lax.ppermute(block, axis, [(i, i ^ shift) for i in range(count)])  21.6 us
    pallas_call x1, Pallas kernels, near_experts(): pl.pallas_call(kernel, grid_spec=pltpu.PrefetchScalarGridSpec(num_scalar_...  20.4 us
    all_to_all x4, starting transfers between devices, across_chips(): lax.all_to_all(blocks, 'expert', 0, 0, axis_index_groups=groups, tiled=True)  17.7 us
  transfers between devices with their start and end apart: 33, of which 18 were waited for; matrix products, arithmetic and copies ran while one was open for 9% of the time, Pallas kernels for 20%

profile of v2, /device:TPU:0, one launch (start us, length us, event | category | flops | bytes accessed | tf_op | source)
XLA Modules:
  0.0 451.6 jit_solution(8975153009127224169)
XLA Ops:
  3.7 5.2 %all-to-all-start = ((bf16[4,144,1024]{2,1,0:T(8,128)(2,1)}), bf16[4,144,1024]{2,1,0:T(8,128)(2,1)S(1)}, u32[]{:S(2)}, u32[]{:S(2)}) async-start(bf16[4,144,1024]{2,1,0:T(8,128)(2,1)} %broadcast_in_dim.41), calls=%async_computation | async-start | bytes 2359296 | tf_op jit(solution)/shard_map/all_to_all | solution.py:1063
  9.6 14.2 %all-to-all-done.near_ref = bf16[4,144,1024]{2,1,0:T(8,128)(2,1)S(1)} async-done(((bf16[4,144,1024]{2,1,0:T(8,128)(2,1)}), bf16[4,144,1024]{2,1,0:T(8,128)(2,1)S(1)}, u32[]{:S(2)}, u32[]{:S(2)}) %all-to-all-start) | async-done | bytes 1179680 | tf_op jit(solution)/shard_map/all_to_all | solution.py:1063
  23.9 2.3 broadcast_in_dim.43
  26.2 4.3 all-to-all-start.1
  30.5 14.5 %all-to-all-done.1.gn = bf16[4,144,1024]{2,1,0:T(8,128)(2,1)} async-done(((bf16[4,144,1024]{2,1,0:T(8,128)(2,1)}), bf16[4,144,1024]{2,1,0:T(8,128)(2,1)}, u32[]{:S(2)}, u32[]{:S(2)}) %all-to-all-start.1) | async-done | bytes 1179680 | tf_op jit(solution)/shard_map/all_to_all | solution.py:1063
  49.7 16.7 %attend_heads.1 = (bf16[8,128,1024]{2,1,0:T(8,128)(2,1)}, bf16[1024,256]{1,0:T(8,128)(2,1)}, f32[1024,128]{1,0:T(8,128)}, f32[1024,128]{1,0:T(8,128)}, bf16[8,12...) custom-call(s32[1]{0:T(128)} %bitcast.1.me_ref, ...), custom_call_target="tpu_custom_call" | custom-call | flops 2147483648 | bytes 8388608 | tf_op jit(solution)/shard_map/attend_heads/pallas_call | solution.py:823
  66.4 10.2 %all_to_all.45 = bf16[8,128,128]{2,1,0:T(8,128)(2,1)S(1)} all-to-all(bf16[8,128,128]{2,1,0:T(8,128)(2,1)} %get-tuple-element.66), channel_id=1, replica_groups=mesh['dp'=4,'expert'=8] {'expert'}, dimensions={0} | all-to-all | bytes 524288 | tf_op jit(solution)/shard_map/all_to_all | solution.py:1123
  77.7 17.1 %all_to_all.46.xn = bf16[4,128,1024]{2,1,0:T(8,128)(2,1)} all-to-all(bf16[4,128,1024]{2,1,0:T(8,128)(2,1)S(1)} %broadcast_in_dim.44), channel_id=1, replica_groups={{0,2,4,6},{1,3,5,7},{8,10,12,14},{9,11,13,15},{16,18,20,22},{17,19,21,2..., dimensions={0} | all-to-all | bytes 2097152 | tf_op jit(solution)/shard_map/all_to_all | solution.py:1063
  94.8 3.7 collective-permute-start.4
  99.3 7.4 %collective-permute-done.4 = bf16[144,1024]{1,0:T(8,128)(2,1)S(1)} collective-permute-done((bf16[144,1024]{1,0:T(8,128)(2,1)S(1)}, bf16[144,1024]{1,0:T(8,128)(2,1)S(1)}, u32[]{:S(2)}, u32[]{:S(2)}) %collective-permute-start.4) | collective-permute-done | bytes 294944 | tf_op jit(solution)/shard_map/ppermute | solution.py:1067
  106.7 17.6 %collective-permute-done.3 = bf16[144,1024]{1,0:T(8,128)(2,1)S(1)} collective-permute-done((bf16[144,1024]{1,0:T(8,128)(2,1)S(1)}, bf16[144,1024]{1,0:T(8,128)(2,1)S(1)}, u32[]{:S(2)}, u32[]{:S(2)}) %collective-permute-start.3) | collective-permute-done | bytes 294944 | tf_op jit(solution)/shard_map/ppermute | solution.py:1067
  131.7 20.4 %near_experts.1 = (bf16[4,144,1024]{2,1,0:T(8,128)(2,1)}, bf16[4,144,1024]{2,1,0:T(8,128)(2,1)}, bf16[4,128,1024]{2,1,0:T(8,128)(2,1)}, bf16[4,128,1024]{2,1,0:T(8,128)(2,1)}) custom-call(s32[1]{0:T(128)} %bitcast.1.me_ref, bf16[4,128,1024]{2,1,0:T(8,128)(2,1)} %all_to_all.46.xn, bf16[4,128,1024]{2,1,0:T(8,128)(2,1)} %collective-permute-done.8.xt, ...), custom_call_target="tpu_custom_call" | custom-call | flops 11274289152 | bytes 16777216 | tf_op jit(solution)/shard_map/near_experts/pallas_call | solution.py:512
  152.7 2.6 collective-permute-done.9
  155.2 3.1 add_convert_fusion
  158.3 4.5 all-to-all-start.4
  164.0 16.0 %expert_weight_grads.2 = (f32[4,256,512]{2,1,0:T(8,128)}, f32[4,256,512]{2,1,0:T(8,128)}, f32[4,128,1024]{2,1,0:T(8,128)}) custom-call(s32[2]{0:T(128)} %pad_add_fusion.ids_ref, bf16[4,1,128,1024]{3,2,1,0:T(8,128)(2,1)} %bitcast.31.xn, bf16[4,1,128,1024]{3,2,1,0:T(8,128)(2,1)} %bitcast.28.xt, bf16[4,1,144,1024]{3,2,1,0:T(8,128)(2,1)} %bitcast.32.gn, ...), custom_call_target="tpu_custom_call" | custom-call | flops 6442450944 | bytes 16777216 | tf_op jit(solution)/shard_map/expert_weight_grads/pallas_call | solution.py:611
  184.4 2.1 multiply_convert_fusion
  186.7 19.3 %all_to_all.47.near_ref = bf16[4,144,1024]{2,1,0:T(8,128)(2,1)S(1)} all-to-all(bf16[4,144,1024]{2,1,0:T(8,128)(2,1)S(1)} %broadcast_in_dim.100), channel_id=1, replica_groups={{0,2,4,6},{1,3,5,7},{8,10,12,14},{9,11,13,15},{16,18,20,22},{17,19,21,2..., dimensions={0} | all-to-all | bytes 2359296 | tf_op jit(solution)/shard_map/all_to_all | solution.py:1063
  206.9 2.5 collective-permute-start.12
  210.8 7.1 %collective-permute-done.12 = bf16[128,1024]{1,0:T(8,128)(2,1)S(1)} collective-permute-done((bf16[128,1024]{1,0:T(8,128)(2,1)S(1)}, bf16[128,1024]{1,0:T(8,128)(2,1)S(1)}, u32[]{:S(2)}, u32[]{:S(2)}) %collective-permute-start.12) | collective-permute-done | bytes 262176 | tf_op jit(solution)/shard_map/ppermute | solution.py:1067
  219.4 11.8 %collective-permute-done.11 = bf16[128,1024]{1,0:T(8,128)(2,1)S(1)} collective-permute-done((bf16[128,1024]{1,0:T(8,128)(2,1)S(1)}, bf16[128,1024]{1,0:T(8,128)(2,1)S(1)}, u32[]{:S(2)}, u32[]{:S(2)}) %collective-permute-start.11) | collective-permute-done | bytes 262176 | tf_op jit(solution)/shard_map/ppermute | solution.py:1067
  231.3 7.6 %collective-permute-done.10 = bf16[128,1024]{1,0:T(8,128)(2,1)S(1)} collective-permute-done((bf16[128,1024]{1,0:T(8,128)(2,1)S(1)}, bf16[128,1024]{1,0:T(8,128)(2,1)S(1)}, u32[]{:S(2)}, u32[]{:S(2)}) %collective-permute-start.10) | collective-permute-done | bytes 262176 | tf_op jit(solution)/shard_map/ppermute | solution.py:1067
  239.8 2.0 collective-permute-start.15
  245.4 15.3 %attend_back.1 = (bf16[8,128,256]{2,1,0:T(8,128)(2,1)}, bf16[4,128,256]{2,1,0:T(8,128)(2,1)}) custom-call(s32[1]{0:T(128)} %bitcast.1.me_ref, bf16[4,144,1024]{2,1,0:T(8,128)(2,1)} %copy-done.8, bf16[4,144,1024]{2,1,0:T(8,128)(2,1)} %copy-done.15, bf16[128,1024]{1,0:T(8,128)(2,1)} %constant_dynamic-slice_fusion.1.w_ref, ...), custom_call_target="tpu_custom_call" | custom-call | flops 1610612736 | bytes 8388608 | tf_op jit(solution)/shard_map/attend_back/pallas_call | solution.py:952
  260.7 3.8 all-to-all-start.6
  264.5 3.2 pad_maximum_fusion.gn
  268.6 13.2 %collective-permute-done.14 = bf16[3,128,1024]{2,1,0:T(8,128)(2,1)} collective-permute-done((bf16[3,128,1024]{2,1,0:T(8,128)(2,1)}, bf16[3,128,1024]{2,1,0:T(8,128)(2,1)}, u32[]{:S(2)}, u32[]{:S(2)}) %collective-permute-start.14) | collective-permute-done | bytes 786464 | tf_op jit(solution)/shard_map/ppermute | solution.py:1067
  281.8 3.2 pad_maximum_fusion.1.xn
  285.1 2.2 all-to-all-done.6.dlin_ref
  288.1 5.8 %token_back.1 = (f32[128,1024]{1,0:T(8,128)}, f32[1,1024]{1,0:T(1,128)}) custom-call(bf16[8,128,256]{2,1,0:T(8,128)(2,1)} %copy-done.7, bf16[1024,1024]{1,0:T(8,128)(2,1)} %wq_ref.1, bf16[1024,512]{1,0:T(8,128)(2,1)} %wk_ref.1, bf16[1024,512]{1,0:T(8,128)(2,1)} %wv_ref.1, bf16[128,1024]{1,0:T(8,128)(2,1)} %bitcast.114, ...), custom_call_target="tpu_custom_call" | custom-call | flops 536870912 | bytes 4194304 | tf_op jit(solution)/shard_map/token_back/pallas_call | solution.py:1031
  296.9 2.4 fusion.1
  299.6 2.4 collective-permute-start.23
  302.9 4.0 collective-permute-done.21
  306.9 5.4 %collective-permute-done.23 = bf16[400,256]{1,0:T(8,128)(2,1)S(1)} collective-permute-done((bf16[400,256]{1,0:T(8,128)(2,1)S(1)}, bf16[400,256]{1,0:T(8,128)(2,1)S(1)}, u32[]{:S(2)}, u32[]{:S(2)}) %collective-permute-start.23) | collective-permute-done | bytes 204832 | tf_op jit(solution)/shard_map/ppermute | solution.py:1067
  312.3 8.9 %collective-permute-done.22 = bf16[400,256]{1,0:T(8,128)(2,1)S(1)} collective-permute-done((bf16[400,256]{1,0:T(8,128)(2,1)S(1)}, bf16[400,256]{1,0:T(8,128)(2,1)S(1)}, u32[]{:S(2)}, u32[]{:S(2)}) %collective-permute-start.22) | collective-permute-done | bytes 204832 | tf_op jit(solution)/shard_map/ppermute | solution.py:1067
  322.4 3.7 all-to-all-start.7
  327.1 21.2 %all-to-all-done.7 = bf16[4,416,256]{2,1,0:T(8,128)(2,1)S(1)} async-done(((bf16[4,416,256]{2,1,0:T(8,128)(2,1)}), bf16[4,416,256]{2,1,0:T(8,128)(2,1)S(1)}, u32[]{:S(2)}, u32[]{:S(2)}) %all-to-all-start.7) | async-done | bytes 852000 | tf_op jit(solution)/shard_map/all_to_all | solution.py:1123
  350.6 3.7 all-to-all-start.8
  358.6 44.5 %expert_weight_grads.3 = (f32[4,256,512]{2,1,0:T(8,128)}, f32[4,256,512]{2,1,0:T(8,128)}, f32[4,128,1024]{2,1,0:T(8,128)}) custom-call(s32[2]{0:T(128)} %pad_add_fusion.ids_ref, bf16[4,3,128,1024]{3,2,1,0:T(8,128)(2,1)} %pad_maximum_fusion.1.xn, ...), custom_call_target="tpu_custom_call", output_to_operand_aliasing={{0}: (11, {}), {1}: (12, {}), {2}: (13, {})} | custom-call | flops 19327352832 | bytes 16777216 | tf_op jit(solution)/shard_map/expert_weight_grads/pallas_call | solution.py:611
  403.7 6.9 %collective-permute-done.17 = bf16[4,128,1024]{2,1,0:T(8,128)(2,1)} collective-permute-done((bf16[4,128,1024]{2,1,0:T(8,128)(2,1)}, bf16[4,128,1024]{2,1,0:T(8,128)(2,1)}, u32[]{:S(2)}, u32[]{:S(2)}) %collective-permute-start.17) | collective-permute-done | bytes 1048608 | tf_op jit(solution)/shard_map/ppermute | solution.py:1058
  410.6 2.9 add_convert_fusion.1
  413.5 1.9 dynamic-slice_bitcast_fusion.2
  415.5 2.0 collective-permute-start.18
  419.0 6.0 %collective-permute-done.18 = bf16[128,1024]{1,0:T(8,128)(2,1)} collective-permute-done((bf16[128,1024]{1,0:T(8,128)(2,1)}, bf16[128,1024]{1,0:T(8,128)(2,1)}, u32[]{:S(2)}, u32[]{:S(2)}) %collective-permute-start.18) | collective-permute-done | bytes 262176 | tf_op jit(solution)/shard_map/ppermute | solution.py:1067
  425.0 6.3 %collective-permute-done.20 = bf16[128,1024]{1,0:T(8,128)(2,1)} collective-permute-done((bf16[128,1024]{1,0:T(8,128)(2,1)}, bf16[128,1024]{1,0:T(8,128)(2,1)}, u32[]{:S(2)}, u32[]{:S(2)}) %collective-permute-start.20) | collective-permute-done | bytes 262176 | tf_op jit(solution)/shard_map/ppermute | solution.py:1067
  432.4 2.2 fusion.19
  437.3 6.6 %assemble_rows.1 = f32[1024,1024]{1,0:T(8,128)} custom-call(s32[1]{0:T(128)} %bitcast.6.core_ref, bf16[4,1568,256]{2,1,0:T(8,128)(2,1)} %copy-done.2, bf16[4,1568,256]{2,1,0:T(8,128)(2,1)} %collective-permute-done.26.twin_ref), custom_call_target="tpu_custom_call" | custom-call | tf_op jit(solution)/shard_map/assemble_rows/pallas_call | solution.py:695
  443.9 7.6 %assemble_heads.1 = (f32[1024,1024]{1,0:T(8,128)}, f32[1024,512]{1,0:T(8,128)}, f32[1024,512]{1,0:T(8,128)}) custom-call(s32[1]{0:T(128)} %bitcast.6.core_ref, bf16[4,1568,256]{2,1,0:T(8,128)(2,1)} %copy-done.2, bf16[4,1568,256]{2,1,0:T(8,128)(2,1)} %collective-permute-done.26.twin_ref), custom_call_target="tpu_custom_call" | custom-call | tf_op jit(solution)/shard_map/assemble_heads/pallas_call | solution.py:669
  (175 shorter events, 52.5 us)
Async XLA Ops:
  0.6 76.1 %copy-start = (bf16[1024,1024]{1,0:T(8,128)(2,1)S(1)}, bf16[1024,1024]{1,0:T(8,128)(2,1)}, u32[]{:S(2)}) copy-start(bf16[1024,1024]{1,0:T(8,128)(2,1)} %param.19) | copy-start | bytes 6291460
  3.7 20.2 %all-to-all-start = ((bf16[4,144,1024]{2,1,0:T(8,128)(2,1)}), bf16[4,144,1024]{2,1,0:T(8,128)(2,1)S(1)}, u32[]{:S(2)}, u32[]{:S(2)}) async-start(bf16[4,144,1024]{2,1,0:T(8,128)(2,1)} %broadcast_in_dim.41), calls=%async_computation | async-start | bytes 2359296 | tf_op jit(solution)/shard_map/all_to_all | solution.py:1063
  23.9 22.9 %copy-start.9 = (bf16[4,144,1024]{2,1,0:T(8,128)(2,1)}, bf16[4,144,1024]{2,1,0:T(8,128)(2,1)S(1)}, u32[]{:S(2)}) copy-start(bf16[4,144,1024]{2,1,0:T(8,128)(2,1)S(1)} %all-to-all-done.near_ref) | copy-start | bytes 3538948
  26.2 18.9 %all-to-all-start.1 = ((bf16[4,144,1024]{2,1,0:T(8,128)(2,1)}), bf16[4,144,1024]{2,1,0:T(8,128)(2,1)}, u32[]{:S(2)}, u32[]{:S(2)}) async-start(bf16[4,144,1024]{2,1,0:T(8,128)(2,1)} %broadcast_in_dim.43), calls=%async_computation.1 | async-start | bytes 2359296 | tf_op jit(solution)/shard_map/all_to_all | solution.py:1063
  30.5 19.2 %collective-permute-start = (bf16[4,144,1024]{2,1,0:T(8,128)(2,1)S(1)}, bf16[4,144,1024]{2,1,0:T(8,128)(2,1)}, u32[]{:S(2)}, u32[]{:S(2)}) collective-permute-start(bf16[4,144,1024]{2,1,0:T(8,128)(2,1)S(1)} %all-to-all-done.near_ref), channel_id=1, source_target_pairs={{0,1},{1,0},{2,3},{3,2},{4,5},{5,4},{6,7},{7,6},{8,9},{9,8},{10,11... | collective-permute-start | bytes 3538952 | tf_op jit(solution)/shard_map/ppermute | solution.py:1058
  45.1 21.3 %collective-permute-start.1 = (bf16[4,144,1024]{2,1,0:T(8,128)(2,1)}, bf16[4,144,1024]{2,1,0:T(8,128)(2,1)}, u32[]{:S(2)}, u32[]{:S(2)}) collective-permute-start(bf16[4,144,1024]{2,1,0:T(8,128)(2,1)} %all-to-all-done.1.gn), channel_id=1, source_target_pairs={{0,1},{1,0},{2,3},{3,2},{4,5},{5,4},{6,7},{7,6},{8,9},{9,8},{10,11... | collective-permute-start | bytes 3538952 | tf_op jit(solution)/shard_map/ppermute | solution.py:1058
  49.7 27.1 %copy-start.6 = (bf16[1,128,1024]{2,1,0:T(8,128)(2,1)S(1)}, bf16[1,128,1024]{2,1,0:T(8,128)(2,1)}, u32[]{:S(2)}) copy-start(bf16[1,128,1024]{2,1,0:T(8,128)(2,1)} %param.14) | copy-start | bytes 786436
  77.4 107.0 %copy-start.3 = (f32[128,1024]{1,0:T(8,128)}, f32[128,1024]{1,0:T(8,128)S(1)}, u32[]{:S(2)}) copy-start(f32[128,1024]{1,0:T(8,128)S(1)} %get-tuple-element.169) | copy-start | bytes 1572868
  77.4 17.4 %copy-start.22 = (f32[128]{0:T(128)}, f32[128]{0:T(128)S(1)}, u32[]{:S(2)}) copy-start(f32[128]{0:T(128)S(1)} %add_rsqrt_fusion) | copy-start | bytes 1540
  77.4 17.4 %copy-start.10 = (bf16[144,1024]{1,0:T(8,128)(2,1)S(1)}, bf16[144,1024]{1,0:T(8,128)(2,1)}, u32[]{:S(2)}) copy-start(bf16[144,1024]{1,0:T(8,128)(2,1)} %pad_maximum_fusion.6) | copy-start | bytes 884740
  77.6 17.3 %copy-start.4 = (bf16[128,1024]{1,0:T(8,128)(2,1)}, bf16[128,1024]{1,0:T(8,128)(2,1)S(1)}, u32[]{:S(2)}) copy-start(bf16[128,1024]{1,0:T(8,128)(2,1)S(1)} %multiply_convert_fusion.1) | copy-start | bytes 786436
  94.8 36.8 %collective-permute-start.8 = (bf16[4,128,1024]{2,1,0:T(8,128)(2,1)}, bf16[4,128,1024]{2,1,0:T(8,128)(2,1)}, u32[]{:S(2)}, u32[]{:S(2)}) collective-permute-start(bf16[4,128,1024]{2,1,0:T(8,128)(2,1)} %all_to_all.46.xn), channel_id=1, source_target_pairs={{0,1},{1,0},{2,3},{3,2},{4,5},{5,4},{6,7},{7,6},{8,9},{9,8},{10,11... | collective-permute-start | bytes 3145736 | tf_op jit(solution)/shard_map/ppermute | solution.py:1058
  94.8 11.9 %collective-permute-start.4 = (bf16[144,1024]{1,0:T(8,128)(2,1)S(1)}, bf16[144,1024]{1,0:T(8,128)(2,1)S(1)}, u32[]{:S(2)}, u32[]{:S(2)}) collective-permute-start(bf16[144,1024]{1,0:T(8,128)(2,1)S(1)} %copy-done.10), channel_id=1, source_target_pairs={{0,24},{8,16},{16,8},{24,0},{1,25},{9,17},{17,9},{25,1},{2,26},{10... | collective-permute-start | bytes 884744 | tf_op jit(solution)/shard_map/ppermute | solution.py:1067
  98.6 25.7 %collective-permute-start.3 = (bf16[144,1024]{1,0:T(8,128)(2,1)S(1)}, bf16[144,1024]{1,0:T(8,128)(2,1)S(1)}, u32[]{:S(2)}, u32[]{:S(2)}) collective-permute-start(bf16[144,1024]{1,0:T(8,128)(2,1)S(1)} %copy-done.10), channel_id=1, source_target_pairs={{0,16},{8,24},{16,0},{24,8},{1,17},{9,25},{17,1},{25,9},{2,18},{10... | collective-permute-start | bytes 884744 | tf_op jit(solution)/shard_map/ppermute | solution.py:1067
  98.6 25.7 %collective-permute-start.2 = (bf16[144,1024]{1,0:T(8,128)(2,1)S(1)}, bf16[144,1024]{1,0:T(8,128)(2,1)}, u32[]{:S(2)}, u32[]{:S(2)}) collective-permute-start(bf16[144,1024]{1,0:T(8,128)(2,1)S(1)} %copy-done.10), channel_id=1, source_target_pairs={{0,8},{8,0},{16,24},{24,16},{1,9},{9,1},{17,25},{25,17},{2,10},{10... | collective-permute-start | bytes 884744 | tf_op jit(solution)/shard_map/ppermute | solution.py:1067
  106.7 17.6 %copy-start.16 = (bf16[144,1024]{1,0:T(8,128)(2,1)}, bf16[144,1024]{1,0:T(8,128)(2,1)S(1)}, u32[]{:S(2)}) copy-start(bf16[144,1024]{1,0:T(8,128)(2,1)S(1)} %collective-permute-done.4) | copy-start | bytes 884740
  152.0 3.2 collective-permute-start.9
  158.3 21.8 %all-to-all-start.4 = ((bf16[4,144,1024]{2,1,0:T(8,128)(2,1)}), bf16[4,144,1024]{2,1,0:T(8,128)(2,1)}, u32[]{:S(2)}, u32[]{:S(2)}) async-start(bf16[4,144,1024]{2,1,0:T(8,128)(2,1)} %add_convert_fusion), calls=%async_computation.4 | async-start | bytes 2359296 | tf_op jit(solution)/shard_map/all_to_all | solution.py:1063
  164.0 17.7 %copy-start.20 = (f32[128]{0:T(128)}, f32[128]{0:T(128)S(1)}, u32[]{:S(2)}) copy-start(f32[128]{0:T(128)S(1)} %get-tuple-element.170) | copy-start | bytes 1540
  164.0 17.6 %copy-start.21 = (f32[128]{0:T(128)}, f32[128]{0:T(128)S(1)}, u32[]{:S(2)}) copy-start(f32[128]{0:T(128)S(1)} %fusion.33) | copy-start | bytes 1540
  186.5 20.4 %copy-start.5 = (bf16[128,1024]{1,0:T(8,128)(2,1)S(1)}, bf16[128,1024]{1,0:T(8,128)(2,1)}, u32[]{:S(2)}) copy-start(bf16[128,1024]{1,0:T(8,128)(2,1)} %copy-done.4) | copy-start | bytes 786436
  206.0 35.9 %copy-start.8 = (bf16[4,144,1024]{2,1,0:T(8,128)(2,1)}, bf16[4,144,1024]{2,1,0:T(8,128)(2,1)S(1)}, u32[]{:S(2)}) copy-start(bf16[4,144,1024]{2,1,0:T(8,128)(2,1)S(1)} %all_to_all.47.near_ref) | copy-start | bytes 3538948
  206.0 36.9 %collective-permute-start.16 = (bf16[4,144,1024]{2,1,0:T(8,128)(2,1)S(1)}, bf16[4,144,1024]{2,1,0:T(8,128)(2,1)S(1)}, u32[]{:S(2)}, u32[]{:S(2)}) collective-permute-start(bf16[4,144,1024]{2,1,0:T(8,128)(2,1)S(1)} %all_to_all.47.near_ref), channel_id=1, source_target_pairs={{0,1},{1,0},{2,3},{3,2},{4,5},{5,4},{6,7},{7,6},{8,9},{9,8},{10,11... | collective-permute-start | bytes 3538952 | tf_op jit(solution)/shard_map/ppermute | solution.py:1058
  206.0 35.9 %collective-permute-start.7 = (bf16[3,144,1024]{2,1,0:T(8,128)(2,1)S(1)}, bf16[3,144,1024]{2,1,0:T(8,128)(2,1)S(1)}, u32[]{:S(2)}, u32[]{:S(2)}) collective-permute-start(bf16[3,144,1024]{2,1,0:T(8,128)(2,1)S(1)} %pad_maximum_fusion.2), channel_id=1, source_target_pairs={{0,6},{1,7},{2,4},{3,5},{4,2},{5,3},{6,0},{7,1},{8,14},{9,15},{10,... | collective-permute-start | bytes 2654216 | tf_op jit(solution)/shard_map/ppermute | solution.py:1067
  206.9 11.1 %collective-permute-start.12 = (bf16[128,1024]{1,0:T(8,128)(2,1)S(1)}, bf16[128,1024]{1,0:T(8,128)(2,1)S(1)}, u32[]{:S(2)}, u32[]{:S(2)}) collective-permute-start(bf16[128,1024]{1,0:T(8,128)(2,1)S(1)} %copy-done.5), channel_id=1, source_target_pairs={{0,24},{8,16},{16,8},{24,0},{1,25},{9,17},{17,9},{25,1},{2,26},{10... | collective-permute-start | bytes 786440 | tf_op jit(solution)/shard_map/ppermute | solution.py:1067
  209.4 21.9 %collective-permute-start.11 = (bf16[128,1024]{1,0:T(8,128)(2,1)S(1)}, bf16[128,1024]{1,0:T(8,128)(2,1)S(1)}, u32[]{:S(2)}, u32[]{:S(2)}) collective-permute-start(bf16[128,1024]{1,0:T(8,128)(2,1)S(1)} %copy-done.5), channel_id=1, source_target_pairs={{0,16},{8,24},{16,0},{24,8},{1,17},{9,25},{17,1},{25,9},{2,18},{10... | collective-permute-start | bytes 786440 | tf_op jit(solution)/shard_map/ppermute | solution.py:1067
  209.4 55.1 %collective-permute-start.6 = (bf16[3,144,1024]{2,1,0:T(8,128)(2,1)S(1)}, bf16[3,144,1024]{2,1,0:T(8,128)(2,1)}, u32[]{:S(2)}, u32[]{:S(2)}) collective-permute-start(bf16[3,144,1024]{2,1,0:T(8,128)(2,1)S(1)} %pad_maximum_fusion.2), channel_id=1, source_target_pairs={{0,4},{1,5},{2,6},{3,7},{4,0},{5,1},{6,2},{7,3},{8,12},{9,13},{10,... | collective-permute-start | bytes 2654216 | tf_op jit(solution)/shard_map/ppermute | solution.py:1067
  218.0 46.5 %collective-permute-start.5 = (bf16[3,144,1024]{2,1,0:T(8,128)(2,1)S(1)}, bf16[3,144,1024]{2,1,0:T(8,128)(2,1)}, u32[]{:S(2)}, u32[]{:S(2)}) collective-permute-start(bf16[3,144,1024]{2,1,0:T(8,128)(2,1)S(1)} %pad_maximum_fusion.2), channel_id=1, source_target_pairs={{0,2},{1,3},{2,0},{3,1},{4,6},{5,7},{6,4},{7,5},{8,10},{9,11},{10,... | collective-permute-start | bytes 2654216 | tf_op jit(solution)/shard_map/ppermute | solution.py:1067
  231.3 7.6 %collective-permute-start.10 = (bf16[128,1024]{1,0:T(8,128)(2,1)S(1)}, bf16[128,1024]{1,0:T(8,128)(2,1)S(1)}, u32[]{:S(2)}, u32[]{:S(2)}) collective-permute-start(bf16[128,1024]{1,0:T(8,128)(2,1)S(1)} %copy-done.5), channel_id=1, source_target_pairs={{0,8},{8,0},{16,24},{24,16},{1,9},{9,1},{17,25},{25,17},{2,10},{10... | collective-permute-start | bytes 786440 | tf_op jit(solution)/shard_map/ppermute | solution.py:1067
  239.8 28.8 %collective-permute-start.15 = (bf16[3,128,1024]{2,1,0:T(8,128)(2,1)}, bf16[3,128,1024]{2,1,0:T(8,128)(2,1)}, u32[]{:S(2)}, u32[]{:S(2)}) collective-permute-start(bf16[3,128,1024]{2,1,0:T(8,128)(2,1)} %pad_maximum_fusion.4), channel_id=1, source_target_pairs={{0,6},{1,7},{2,4},{3,5},{4,2},{5,3},{6,0},{7,1},{8,14},{9,15},{10,... | collective-permute-start | bytes 2359304 | tf_op jit(solution)/shard_map/ppermute | solution.py:1067
  241.8 40.0 %collective-permute-start.14 = (bf16[3,128,1024]{2,1,0:T(8,128)(2,1)}, bf16[3,128,1024]{2,1,0:T(8,128)(2,1)}, u32[]{:S(2)}, u32[]{:S(2)}) collective-permute-start(bf16[3,128,1024]{2,1,0:T(8,128)(2,1)} %pad_maximum_fusion.4), channel_id=1, source_target_pairs={{0,4},{1,5},{2,6},{3,7},{4,0},{5,1},{6,2},{7,3},{8,12},{9,13},{10,... | collective-permute-start | bytes 2359304 | tf_op jit(solution)/shard_map/ppermute | solution.py:1067
  243.8 38.0 %collective-permute-start.13 = (bf16[3,128,1024]{2,1,0:T(8,128)(2,1)}, bf16[3,128,1024]{2,1,0:T(8,128)(2,1)}, u32[]{:S(2)}, u32[]{:S(2)}) collective-permute-start(bf16[3,128,1024]{2,1,0:T(8,128)(2,1)} %pad_maximum_fusion.4), channel_id=1, source_target_pairs={{0,2},{1,3},{2,0},{3,1},{4,6},{5,7},{6,4},{7,5},{8,10},{9,11},{10,... | collective-permute-start | bytes 2359304 | tf_op jit(solution)/shard_map/ppermute | solution.py:1067
  245.4 19.1 %copy-start.13 = (bf16[3,144,1024]{2,1,0:T(8,128)(2,1)S(1)}, bf16[3,144,1024]{2,1,0:T(8,128)(2,1)}, u32[]{:S(2)}) copy-start(bf16[3,144,1024]{2,1,0:T(8,128)(2,1)} %copy-done.12) | copy-start | bytes 2654212
  260.7 26.6 %all-to-all-start.6 = ((bf16[8,128,256]{2,1,0:T(8,128)(2,1)}), bf16[8,128,256]{2,1,0:T(8,128)(2,1)S(1)}, u32[]{:S(2)}, u32[]{:S(2)}) async-start(bf16[8,128,256]{2,1,0:T(8,128)(2,1)} %get-tuple-element.92), calls=%async_computation.6 | async-start | bytes 1048576 | tf_op jit(solution)/shard_map/all_to_all | solution.py:1123
  295.4 58.9 %collective-permute-start.25 = (bf16[4,3,144,1024]{3,2,1,0:T(8,128)(2,1)}, bf16[4,3,144,1024]{3,2,1,0:T(8,128)(2,1)}, u32[]{:S(2)}, u32[]{:S(2)}) collective-permute-start(bf16[4,3,144,1024]{3,2,1,0:T(8,128)(2,1)} %pad_maximum_fusion.gn), channel_id=1, source_target_pairs={{0,1},{1,0},{2,3},{3,2},{4,5},{5,4},{6,7},{7,6},{8,9},{9,8},{10,11... | collective-permute-start | bytes 10616840 | tf_op jit(solution)/shard_map/ppermute | solution.py:1058
  299.4 7.5 %collective-permute-start.21 = (bf16[400,256]{1,0:T(8,128)(2,1)S(1)}, bf16[400,256]{1,0:T(8,128)(2,1)S(1)}, u32[]{:S(2)}, u32[]{:S(2)}) collective-permute-start(bf16[400,256]{1,0:T(8,128)(2,1)S(1)} %get-tuple-element.163), channel_id=1, source_target_pairs={{0,8},{8,0},{16,24},{24,16},{1,9},{9,1},{17,25},{25,17},{2,10},{10... | collective-permute-start | bytes 614408 | tf_op jit(solution)/shard_map/ppermute | solution.py:1067
  299.6 12.8 %collective-permute-start.23 = (bf16[400,256]{1,0:T(8,128)(2,1)S(1)}, bf16[400,256]{1,0:T(8,128)(2,1)S(1)}, u32[]{:S(2)}, u32[]{:S(2)}) collective-permute-start(bf16[400,256]{1,0:T(8,128)(2,1)S(1)} %get-tuple-element.164), channel_id=1, source_target_pairs={{0,24},{8,16},{16,8},{24,0},{1,25},{9,17},{17,9},{25,1},{2,26},{10... | collective-permute-start | bytes 614408 | tf_op jit(solution)/shard_map/ppermute | solution.py:1067
  302.0 19.3 %collective-permute-start.22 = (bf16[400,256]{1,0:T(8,128)(2,1)S(1)}, bf16[400,256]{1,0:T(8,128)(2,1)S(1)}, u32[]{:S(2)}, u32[]{:S(2)}) collective-permute-start(bf16[400,256]{1,0:T(8,128)(2,1)S(1)} %get-tuple-element.165), channel_id=1, source_target_pairs={{0,16},{8,24},{16,0},{24,8},{1,17},{9,25},{17,1},{25,9},{2,18},{10... | collective-permute-start | bytes 614408 | tf_op jit(solution)/shard_map/ppermute | solution.py:1067
  321.4 37.3 %collective-permute-start.24 = (bf16[4,3,128,1024]{3,2,1,0:T(8,128)(2,1)}, bf16[4,3,128,1024]{3,2,1,0:T(8,128)(2,1)}, u32[]{:S(2)}, u32[]{:S(2)}) collective-permute-start(bf16[4,3,128,1024]{3,2,1,0:T(8,128)(2,1)} %pad_maximum_fusion.1.xn), channel_id=1, source_target_pairs={{0,1},{1,0},{2,3},{3,2},{4,5},{5,4},{6,7},{7,6},{8,9},{9,8},{10,11... | collective-permute-start | bytes 9437192 | tf_op jit(solution)/shard_map/ppermute | solution.py:1058
  322.4 25.9 %all-to-all-start.7 = ((bf16[4,416,256]{2,1,0:T(8,128)(2,1)}), bf16[4,416,256]{2,1,0:T(8,128)(2,1)S(1)}, u32[]{:S(2)}, u32[]{:S(2)}) async-start(bf16[4,416,256]{2,1,0:T(8,128)(2,1)} %broadcast_in_dim.103), calls=%async_computation.7 | async-start | bytes 1703936 | tf_op jit(solution)/shard_map/all_to_all | solution.py:1123
  350.6 52.6 %all-to-all-start.8 = ((bf16[4,1568,256]{2,1,0:T(8,128)(2,1)}), bf16[4,1568,256]{2,1,0:T(8,128)(2,1)S(1)}, u32[]{:S(2)}, u32[]{:S(2)}) async-start(bf16[4,1568,256]{2,1,0:T(8,128)(2,1)} %broadcast_in_dim.104), calls=%async_computation.8 | async-start | bytes 6422528 | tf_op jit(solution)/shard_map/all_to_all | solution.py:1063
  403.1 31.5 %copy-start.2 = (bf16[4,1568,256]{2,1,0:T(8,128)(2,1)}, bf16[4,1568,256]{2,1,0:T(8,128)(2,1)S(1)}, u32[]{:S(2)}) copy-start(bf16[4,1568,256]{2,1,0:T(8,128)(2,1)S(1)} %all-to-all-done.8.near_ref) | copy-start | bytes 9633796
  403.2 31.5 %collective-permute-start.26 = (bf16[4,1568,256]{2,1,0:T(8,128)(2,1)S(1)}, bf16[4,1568,256]{2,1,0:T(8,128)(2,1)}, u32[]{:S(2)}, u32[]{:S(2)}) collective-permute-start(bf16[4,1568,256]{2,1,0:T(8,128)(2,1)S(1)} %all-to-all-done.8.near_ref), channel_id=1, source_target_pairs={{0,1},{1,0},{2,3},{3,2},{4,5},{5,4},{6,7},{7,6},{8,9},{9,8},{10,11... | collective-permute-start | bytes 9633800 | tf_op jit(solution)/shard_map/ppermute | solution.py:1058
  403.2 7.4 %collective-permute-start.17 = (bf16[4,128,1024]{2,1,0:T(8,128)(2,1)}, bf16[4,128,1024]{2,1,0:T(8,128)(2,1)}, u32[]{:S(2)}, u32[]{:S(2)}) collective-permute-start(bf16[4,128,1024]{2,1,0:T(8,128)(2,1)} %get-tuple-element.95), channel_id=1, source_target_pairs={{0,1},{1,0},{2,3},{3,2},{4,5},{5,4},{6,7},{7,6},{8,9},{9,8},{10,11... | collective-permute-start | bytes 3145736 | tf_op jit(solution)/shard_map/ppermute | solution.py:1058
  415.5 9.5 %collective-permute-start.18 = (bf16[128,1024]{1,0:T(8,128)(2,1)}, bf16[128,1024]{1,0:T(8,128)(2,1)}, u32[]{:S(2)}, u32[]{:S(2)}) collective-permute-start(bf16[128,1024]{1,0:T(8,128)(2,1)} %get-tuple-element.160), channel_id=1, source_target_pairs={{0,2},{1,3},{2,0},{3,1},{4,6},{5,7},{6,4},{7,5},{8,10},{9,11},{10,... | collective-permute-start | bytes 786440 | tf_op jit(solution)/shard_map/ppermute | solution.py:1067
  417.5 13.8 %collective-permute-start.20 = (bf16[128,1024]{1,0:T(8,128)(2,1)}, bf16[128,1024]{1,0:T(8,128)(2,1)}, u32[]{:S(2)}, u32[]{:S(2)}) collective-permute-start(bf16[128,1024]{1,0:T(8,128)(2,1)} %get-tuple-element.161), channel_id=1, source_target_pairs={{0,6},{1,7},{2,4},{3,5},{4,2},{5,3},{6,0},{7,1},{8,14},{9,15},{10,... | collective-permute-start | bytes 786440 | tf_op jit(solution)/shard_map/ppermute | solution.py:1067
  418.9 13.5 %collective-permute-start.19 = (bf16[128,1024]{1,0:T(8,128)(2,1)S(1)}, bf16[128,1024]{1,0:T(8,128)(2,1)}, u32[]{:S(2)}, u32[]{:S(2)}) collective-permute-start(bf16[128,1024]{1,0:T(8,128)(2,1)S(1)} %get-tuple-element.162), channel_id=1, source_target_pairs={{0,4},{1,5},{2,6},{3,7},{4,0},{5,1},{6,2},{7,3},{8,12},{9,13},{10,... | collective-permute-start | bytes 786440 | tf_op jit(solution)/shard_map/ppermute | solution.py:1067
  437.3 14.2 %copy-start.1 = (bf16[1024,1024]{1,0:T(8,128)(2,1)S(1)}, bf16[1024,1024]{1,0:T(8,128)(2,1)}, u32[]{:S(2)}) copy-start(bf16[1024,1024]{1,0:T(8,128)(2,1)} %param.19) | copy-start | bytes 6291460
  (10 other events, 38.0 us)
